TPU v7x, 512 devices: a whole 4x4x16 slice. The times are simulated.
512 devices in a mesh: elem: 64 (over y, z), sub: 8 (over x, core).
Axes of the slice: x: 4, y: 4, z: 16, core: 2. Of those that a mesh axis runs over, the one named last changes fastest.
Arguments:
- node_ref: float32 [3, 27, 65536], P(None, None, ('elem', 'sub')), may hold values from -0.05 to 24.05, as said below
- cp_pos: float32 [3, 16384], P(None, ('elem', 'sub')), may hold values from 0 to 24
- cp_coef: float32 [3, 16384], P(None, ('elem', 'sub')), may hold values from -0.24 to 0.24
- cp_count: int32 [512], P(('elem', 'sub')), may hold values from 1 to 32, 4096 in all
- u_prev: float32 [5, 27, 65536], P(None, None, ('elem', 'sub')), may hold values from -6 to 6
- right_side: float32 [5, 27, 65536], P(None, None, ('elem', 'sub')), may hold values from -6 to 6
- elem_count: int32 [512], P(('elem', 'sub')), may hold values from 64 to 128, as said below
- face_link: int32 [6, 65536], P(None, ('elem', 'sub')), may hold values from 0 to 1024, as said below
- send_list: int32 [512, 4, 64], P(('elem', 'sub')), may hold values from 0 to 767
- vol_block: float32 [135, 135], replicated, may hold values from -0.3 to 2.3, as said below
- block_inv: float32 [135, 135], replicated, may hold values from -0.1 to 0.44
- lift_matrix: float32 [135, 270], replicated, may hold values from -0.375 to 0.375
Outputs:
- displacement: float32 [3, 27, 65536], P(None, None, ('elem', 'sub'))
- solution: float32 [5, 27, 65536], P(None, None, ('elem', 'sub'))
Inputs may be any that keep to these rules, and one draw needn't show every extreme that they name: `node_ref`: coordinates of each element's 3 x 3 x 3 nodes: a lattice of spacing one half shifted by the element's anchor, each node moved by at most 0.05. `elem_count`: one device holds 128 live elements in every draw. `face_link`: a value below 768 names a local trace column, a value from 768 on a received slot, and 1024 a face on the physical boundary. `vol_block`: the element block: twice the identity plus a dense part.
All inputs are finite; a program needn't handle non-finite values. No bound on the sum of `cp_count` on one device may be relied on, other than what follows from the above.
Results may differ from a plain program's by a relative error of at most 0.0003.
Values sent between devices are 32-bit elements; how exact they have to be, the bound alone decides.
No kernel may reach another device: no remote copies, remote signals or barrier semaphores. Data moves between devices by JAX's collectives and lax.ppermute only.
A program may use at most 64 MiB of HBM per device.

v0:
```python
import jax
import jax.numpy as jnp
import numpy as np
from jax import lax
from jax.sharding import Mesh
from jax.sharding import PartitionSpec as P

ITERS = 3
ELEM_SUB = ("elem_0", "elem_1", "sub_0", "sub_1")
ELEM = ("elem_0", "elem_1")
SUB = ("sub_0", "sub_1")


HIGH = lax.Precision.HIGHEST
RADIUS = 1.5


def padded_2(shard, sides, width):
    edges = {}
    for axis, dim in sides:
        size, length = (lax.axis_size(axis), shard.shape[dim])
        up = [(i, (i + 1) % size) for i in range(size - 1)]
        last = lax.slice_in_dim(shard, length - width, length, axis=dim)
        initial = lax.slice_in_dim(shard, 0, width, axis=dim)
        edges[dim] = (
            lax.ppermute(last, axis, up),
            lax.ppermute(initial, axis, [(b, a) for a, b in up]),
        )
    done = []
    for _, dim in sides:
        low, high = edges[dim]
        around = [(width, width) if d in done else (0, 0) for d in range(shard.ndim)]
        shard = jnp.concatenate([jnp.pad(low, around), shard, jnp.pad(high, around)], axis=dim)
        done.append(dim)
    return shard


def from_everyone(shard, axis):
    copies = jnp.broadcast_to(shard, (lax.axis_size(axis), *shard.shape))
    return lax.all_to_all(copies, axis, split_axis=0, concat_axis=0, tiled=True)


def in_order(tiles, dim):
    tiles = jnp.moveaxis(tiles, 0, dim)
    lengths = tiles.shape
    return tiles.reshape(*lengths[:dim], lengths[dim] * lengths[dim + 1], *lengths[dim + 2 :])


def gather_axes(shard, axes, dim):
    far, near = axes
    tiles = from_everyone(from_everyone(shard, far), near)
    return in_order(tiles.swapaxes(0, 1).reshape(-1, *shard.shape), dim)


def sent_together(arrays, axis, dim, along):
    ends, at = ([], 0)
    for a in arrays[:-1]:
        at += a.shape[along]
        ends.append(at)
    both = jnp.concatenate(arrays, axis=along)
    return tuple(jnp.split(gather_axes(both, axis, dim), ends, axis=along))


def lagrange_tables():
    slopes = np.array([[-1.5, 2.0, -0.5], [-0.5, 0.0, 0.5], [0.5, -2.0, 1.5]])
    single = np.eye(3)
    derivs = np.stack(
        [
            np.kron(single, np.kron(single, slopes)),
            np.kron(single, np.kron(slopes, single)),
            np.kron(slopes, np.eye(9)),
        ]
    )
    blending = np.zeros((27, 8))
    for node_id in range(27):
        digits = (node_id % 3, node_id // 3 % 3, node_id // 9)
        for corner in range(8):
            corner_side = (corner % 2, corner // 2 % 2, corner // 4)
            weight = 1.0
            for axis_id in range(3):
                position = digits[axis_id] - 1.0
                if corner_side[axis_id]:
                    weight = weight * (1.0 + position) / 2.0
                else:
                    weight = weight * (1.0 - position) / 2.0
            blending[node_id, corner] = weight
    corner_ids = np.array(
        [2 * (corner % 2) + 6 * (corner // 2 % 2) + 18 * (corner // 4) for corner in range(8)]
    )
    face_ids = []
    for axis_id in range(3):
        for layer_id in (0, 2):
            face_ids.append(
                [node_id for node_id in range(27) if node_id // 3**axis_id % 3 == layer_id]
            )
    return (derivs, blending, corner_ids, np.array(face_ids))


def matmul(left, right):
    return jnp.dot(left, right, precision=HIGH, preferred_element_type=jnp.float32)


def radial_sum(corner_major, centers, weights):

    def one_corner(coords):
        dist_sq = (coords[0][None, :] - centers[0][:, None]) ** 2
        dist_sq = dist_sq + (coords[1][None, :] - centers[1][:, None]) ** 2
        dist_sq = dist_sq + (coords[2][None, :] - centers[2][:, None]) ** 2
        ratio = jnp.sqrt(dist_sq) / RADIUS
        inside = jnp.maximum(1.0 - ratio, 0.0)
        kernel = inside**4 * (4.0 * ratio + 1.0)
        return matmul(weights, kernel)

    return lax.map(one_corner, corner_major)


def jacobian_metric(moved_nodes, derivs):
    jacobian = jnp.einsum("jmk,ike->ijme", derivs, moved_nodes, precision=HIGH)
    minor_a = jacobian[1, 1] * jacobian[2, 2] - jacobian[1, 2] * jacobian[2, 1]
    minor_b = jacobian[1, 0] * jacobian[2, 2] - jacobian[1, 2] * jacobian[2, 0]
    minor_c = jacobian[1, 0] * jacobian[2, 1] - jacobian[1, 1] * jacobian[2, 0]
    return 8.0 * (jacobian[0, 0] * minor_a - jacobian[0, 1] * minor_b + jacobian[0, 2] * minor_c)


def swap_faces(packets):
    padded = padded_2(packets[None, None], ((ELEM, 0), (SUB, 1)), 1)
    received = jnp.stack(
        [padded[1, 0, 0], padded[1, 2, 1], padded[0, 1, 2], padded[2, 1, 3]], axis=0
    )
    return received


def per_device(
    node_ref,
    cp_pos,
    cp_coef,
    cp_count,
    u_prev,
    right_side,
    elem_count,
    face_link,
    send_list,
    vol_block,
    block_inv,
    lift_matrix,
):
    derivs, blending, corner_ids, face_ids = lagrange_tables()
    derivs = jnp.asarray(derivs, jnp.float32)
    blending = jnp.asarray(blending, jnp.float32)
    elem_dev = node_ref.shape[2]
    slot_count = cp_pos.shape[1]
    send_slots = send_list.shape[2]
    live_slot = jnp.arange(slot_count, dtype=jnp.int32) < cp_count[0]
    weights = jnp.where(live_slot[None, :], cp_coef, 0.0)
    corner_major = jnp.transpose(node_ref[:, corner_ids, :], (1, 0, 2))
    start_disp = jnp.zeros((8, 3, elem_dev), jnp.float32)
    piece = sent_together((cp_pos, weights), (("elem_0", "elem_1"), ("sub_0", "sub_1")), 1, 0)
    corner_disp = start_disp + radial_sum(corner_major, piece[0], piece[1])
    displacement = jnp.einsum("nc,cie->ine", blending, corner_disp, precision=HIGH)
    metric = jacobian_metric(node_ref + displacement, derivs)
    scaling = jnp.tile(metric, (5, 1))
    live_elem = jnp.arange(elem_dev, dtype=jnp.int32) < elem_count[0]
    iterate = jnp.where(live_elem[None, :], u_prev.reshape(135, elem_dev), 0.0)
    source = right_side.reshape(135, elem_dev)
    for sweep in range(ITERS):
        traces = iterate.reshape(5, 27, elem_dev)[:, face_ids.T, :].reshape(45, 6 * elem_dev)
        packets = jnp.take(traces, send_list[0], axis=1).transpose(1, 0, 2)
        received = swap_faces(packets)
        full_table = jnp.concatenate(
            [traces, received.transpose(1, 0, 2).reshape(45, 4 * send_slots)], axis=1
        )
        neighbor = jnp.take(full_table, face_link, axis=1, mode="fill", fill_value=0.0).reshape(
            270, elem_dev
        )
        applied = scaling * iterate + matmul(vol_block, iterate) - matmul(lift_matrix, neighbor)
        iterate = jnp.where(live_elem[None, :], iterate + matmul(block_inv, source - applied), 0.0)
    return (displacement, iterate.reshape(5, 27, elem_dev))


def solution(mesh):
    torus = Mesh(mesh.devices.reshape(4, 16, 4, 2), ("elem_0", "elem_1", "sub_0", "sub_1"))
    in_specs = (
        P(None, None, ELEM_SUB),
        P(None, ELEM_SUB),
        P(None, ELEM_SUB),
        P(ELEM_SUB),
        P(None, None, ELEM_SUB),
        P(None, None, ELEM_SUB),
        P(ELEM_SUB),
        P(None, ELEM_SUB),
        P(ELEM_SUB, None, None),
        P(),
        P(),
        P(),
    )
    out_specs = (P(None, None, ELEM_SUB), P(None, None, ELEM_SUB))
    return jax.shard_map(
        per_device, mesh=torus, in_specs=in_specs, out_specs=out_specs, check_vma=False
    )
```

profile of v0, /device:TPU:10, one launch (start us, length us, event | category | flops | bytes accessed | tf_op | source)
XLA Modules:
  0.0 207.2 jit_solution(17811881252084767330)
XLA Ops:
  6.3 11.3 %collective-permute-start.3 = (f32[1,1,4,45,64]{3,4,2,1,0:T(8,128)S(1)}, f32[1,1,4,45,64]{3,4,2,1,0:T(8,128)S(1)}, u32[]{:S(2)}, u32[]{:S(2)}) collective-permute-start(f32[1,1,4,45,64]{3,4,2,1,0:T(8,128)S(1)} %select_bitcast_fusion.5), channel_id=1, source_target_pairs={{8,0},{16,8},{24,16},{32,24},{40,32},{48,40},{56,48},{64,56},{72,6... | collective-permute-start | bytes 138248 | tf_op jit(solution)/shard_map/ppermute | solution.py:27
  17.6 1.9 collective-permute-start.2
  19.5 1.9 collective-permute-start.1
  21.4 2.4 %collective-permute-start = (f32[1,1,4,45,64]{3,4,2,1,0:T(8,128)S(1)}, f32[1,1,4,45,64]{3,4,2,1,0:T(8,128)S(1)}, u32[]{:S(2)}, u32[]{:S(2)}) collective-permute-start(f32[1,1,4,45,64]{3,4,2,1,0:T(8,128)S(1)} %select_bitcast_fusion.5), channel_id=1, source_target_pairs={{0,1},{1,2},{2,3},{3,4},{4,5},{5,6},{6,7},{8,9},{9,10},{10,11},{11... | collective-permute-start | bytes 138248 | tf_op jit(solution)/shard_map/ppermute | solution.py:26
  25.4 11.4 %all-to-all-start = ((f32[64,1,192]{2,1,0:T(1,128)}), f32[64,1,192]{2,1,0:T(1,128)S(1)}, u32[]{:S(2)}, u32[]{:S(2)}) async-start(f32[64,1,192]{2,1,0:T(1,128)} %reshape.310), calls=%async_computation | async-start | bytes 131072 | tf_op jit(solution)/shard_map/all_to_all | solution.py:40
  40.3 10.6 %all-to-all-done = f32[64,1,192]{2,1,0:T(1,128)S(1)} async-done(((f32[64,1,192]{2,1,0:T(1,128)}), f32[64,1,192]{2,1,0:T(1,128)S(1)}, u32[]{:S(2)}, u32[]{:S(2)}) %all-to-all-start) | async-done | bytes 49184 | tf_op jit(solution)/shard_map/all_to_all | solution.py:40
  53.7 5.0 %all-to-all-start.1 = ((f32[8,1,12288]{2,1,0:T(1,128)}), f32[8,1,12288]{2,1,0:T(1,128)S(1)}, u32[]{:S(2)}, u32[]{:S(2)}) async-start(f32[8,1,12288]{2,1,0:T(1,128)} %reshape.312), calls=%async_computation.1 | async-start | bytes 786432 | tf_op jit(solution)/shard_map/all_to_all | solution.py:40
  59.8 6.4 %all-to-all-done.1 = f32[8,1,12288]{2,1,0:T(1,128)S(1)} async-done(((f32[8,1,12288]{2,1,0:T(1,128)}), f32[8,1,12288]{2,1,0:T(1,128)S(1)}, u32[]{:S(2)}, u32[]{:S(2)}) %all-to-all-start.1) | async-done | bytes 393248 | tf_op jit(solution)/shard_map/all_to_all | solution.py:40
  69.6 95.8 %while.12 = (s32[]{:T(128)}, f32[8,3,128]{2,0,1:T(8,128)S(1)}, f32[8,3,128]{2,0,1:T(8,128)}, f32[3,16384]{1,0:T(4,128)S(1)}, f32[3,16384]{1,0:T(4,128)S(1)}, /*index=5*/s32[]{:T(128)}, s32[]{:T(128)}, s32[]{}, s32[]{}) while((s32[]{:T(128)}, f32[8,3,128]{2,0,1:T(8,128)S(1)}, f32[8,3,128]{2,0,1:T(8,128)}, f32[3,16384]{1,0:T(4,128)S(1)}, ...), condition=%wide.region_1.2_spmd, body=%wide.region_0.1_spmd.sunk | while | flops 109051904 | bytes 798861 | solution.py:114
  70.5 11.0 %fusion.96 = f32[1,3,128]{2,1,0:T(4,128)S(1)} fusion(f32[3,16384]{1,0:T(4,128)S(1)} %get-tuple-element.168, f32[16384]{0:T(1024)S(1)} %bitcast.217, f32[128]{0:T(128)S(1)} %get-tuple-element.141, f32[16384]{0:T(1024)S(1)} %bitcast.218, f32[128]{0:T(128)S(1)} %get-tuple-element.143, f32[16384]{0:T(1024)S(1)} %bitcast.216, f32[128]{0:T(128)S(1)} %get-tuple-element.145), kind=kOutput, calls=%fused_computation.38.clone.1 | convolution fusion | flops 109051904 | bytes 396288 | tf_op jit(solution)/shard_map/while/body/eval_jaxpr/dot_general | solution.py:100
  82.5 11.0 %fusion.96 = f32[1,3,128]{2,1,0:T(4,128)S(1)} fusion(f32[3,16384]{1,0:T(4,128)S(1)} %get-tuple-element.168, f32[16384]{0:T(1024)S(1)} %bitcast.217, f32[128]{0:T(128)S(1)} %get-tuple-element.141, f32[16384]{0:T(1024)S(1)} %bitcast.218, f32[128]{0:T(128)S(1)} %get-tuple-element.143, f32[16384]{0:T(1024)S(1)} %bitcast.216, f32[128]{0:T(128)S(1)} %get-tuple-element.145), kind=kOutput, calls=%fused_computation.38.clone.1 | convolution fusion | flops 109051904 | bytes 396288 | tf_op jit(solution)/shard_map/while/body/eval_jaxpr/dot_general | solution.py:100
  94.5 11.0 %fusion.96 = f32[1,3,128]{2,1,0:T(4,128)S(1)} fusion(f32[3,16384]{1,0:T(4,128)S(1)} %get-tuple-element.168, f32[16384]{0:T(1024)S(1)} %bitcast.217, f32[128]{0:T(128)S(1)} %get-tuple-element.141, f32[16384]{0:T(1024)S(1)} %bitcast.218, f32[128]{0:T(128)S(1)} %get-tuple-element.143, f32[16384]{0:T(1024)S(1)} %bitcast.216, f32[128]{0:T(128)S(1)} %get-tuple-element.145), kind=kOutput, calls=%fused_computation.38.clone.1 | convolution fusion | flops 109051904 | bytes 396288 | tf_op jit(solution)/shard_map/while/body/eval_jaxpr/dot_general | solution.py:100
  106.4 11.0 %fusion.96 = f32[1,3,128]{2,1,0:T(4,128)S(1)} fusion(f32[3,16384]{1,0:T(4,128)S(1)} %get-tuple-element.168, f32[16384]{0:T(1024)S(1)} %bitcast.217, f32[128]{0:T(128)S(1)} %get-tuple-element.141, f32[16384]{0:T(1024)S(1)} %bitcast.218, f32[128]{0:T(128)S(1)} %get-tuple-element.143, f32[16384]{0:T(1024)S(1)} %bitcast.216, f32[128]{0:T(128)S(1)} %get-tuple-element.145), kind=kOutput, calls=%fused_computation.38.clone.1 | convolution fusion | flops 109051904 | bytes 396288 | tf_op jit(solution)/shard_map/while/body/eval_jaxpr/dot_general | solution.py:100
  118.4 11.0 %fusion.96 = f32[1,3,128]{2,1,0:T(4,128)S(1)} fusion(f32[3,16384]{1,0:T(4,128)S(1)} %get-tuple-element.168, f32[16384]{0:T(1024)S(1)} %bitcast.217, f32[128]{0:T(128)S(1)} %get-tuple-element.141, f32[16384]{0:T(1024)S(1)} %bitcast.218, f32[128]{0:T(128)S(1)} %get-tuple-element.143, f32[16384]{0:T(1024)S(1)} %bitcast.216, f32[128]{0:T(128)S(1)} %get-tuple-element.145), kind=kOutput, calls=%fused_computation.38.clone.1 | convolution fusion | flops 109051904 | bytes 396288 | tf_op jit(solution)/shard_map/while/body/eval_jaxpr/dot_general | solution.py:100
  130.4 11.0 %fusion.96 = f32[1,3,128]{2,1,0:T(4,128)S(1)} fusion(f32[3,16384]{1,0:T(4,128)S(1)} %get-tuple-element.168, f32[16384]{0:T(1024)S(1)} %bitcast.217, f32[128]{0:T(128)S(1)} %get-tuple-element.141, f32[16384]{0:T(1024)S(1)} %bitcast.218, f32[128]{0:T(128)S(1)} %get-tuple-element.143, f32[16384]{0:T(1024)S(1)} %bitcast.216, f32[128]{0:T(128)S(1)} %get-tuple-element.145), kind=kOutput, calls=%fused_computation.38.clone.1 | convolution fusion | flops 109051904 | bytes 396288 | tf_op jit(solution)/shard_map/while/body/eval_jaxpr/dot_general | solution.py:100
  142.4 11.0 %fusion.96 = f32[1,3,128]{2,1,0:T(4,128)S(1)} fusion(f32[3,16384]{1,0:T(4,128)S(1)} %get-tuple-element.168, f32[16384]{0:T(1024)S(1)} %bitcast.217, f32[128]{0:T(128)S(1)} %get-tuple-element.141, f32[16384]{0:T(1024)S(1)} %bitcast.218, f32[128]{0:T(128)S(1)} %get-tuple-element.143, f32[16384]{0:T(1024)S(1)} %bitcast.216, f32[128]{0:T(128)S(1)} %get-tuple-element.145), kind=kOutput, calls=%fused_computation.38.clone.1 | convolution fusion | flops 109051904 | bytes 396288 | tf_op jit(solution)/shard_map/while/body/eval_jaxpr/dot_general | solution.py:100
  154.4 11.0 %fusion.96 = f32[1,3,128]{2,1,0:T(4,128)S(1)} fusion(f32[3,16384]{1,0:T(4,128)S(1)} %get-tuple-element.168, f32[16384]{0:T(1024)S(1)} %bitcast.217, f32[128]{0:T(128)S(1)} %get-tuple-element.141, f32[16384]{0:T(1024)S(1)} %bitcast.218, f32[128]{0:T(128)S(1)} %get-tuple-element.143, f32[16384]{0:T(1024)S(1)} %bitcast.216, f32[128]{0:T(128)S(1)} %get-tuple-element.145), kind=kOutput, calls=%fused_computation.38.clone.1 | convolution fusion | flops 109051904 | bytes 396288 | tf_op jit(solution)/shard_map/while/body/eval_jaxpr/dot_general | solution.py:100
  168.5 3.6 %collective-permute-start.7 = (f32[1,1,4,45,64]{3,4,2,1,0:T(8,128)S(1)}, f32[1,1,4,45,64]{3,4,2,1,0:T(8,128)S(1)}, u32[]{:S(2)}, u32[]{:S(2)}) collective-permute-start(f32[1,1,4,45,64]{3,4,2,1,0:T(8,128)S(1)} %select_bitcast_fusion.4), channel_id=1, source_target_pairs={{8,0},{16,8},{24,16},{32,24},{40,32},{48,40},{56,48},{64,56},{72,6... | collective-permute-start | bytes 138248 | tf_op jit(solution)/shard_map/ppermute | solution.py:27
  172.1 2.2 %collective-permute-start.6 = (f32[1,1,4,45,64]{3,4,2,1,0:T(8,128)S(1)}, f32[1,1,4,45,64]{3,4,2,1,0:T(8,128)S(1)}, u32[]{:S(2)}, u32[]{:S(2)}) collective-permute-start(f32[1,1,4,45,64]{3,4,2,1,0:T(8,128)S(1)} %select_bitcast_fusion.4), channel_id=1, source_target_pairs={{0,8},{8,16},{16,24},{24,32},{32,40},{40,48},{48,56},{56,64},{64,7... | collective-permute-start | bytes 138248 | tf_op jit(solution)/shard_map/ppermute | solution.py:26
  176.3 2.6 %collective-permute-start.4 = (f32[1,1,4,45,64]{3,4,2,1,0:T(8,128)S(1)}, f32[1,1,4,45,64]{3,4,2,1,0:T(8,128)S(1)}, u32[]{:S(2)}, u32[]{:S(2)}) collective-permute-start(f32[1,1,4,45,64]{3,4,2,1,0:T(8,128)S(1)} %select_bitcast_fusion.4), channel_id=1, source_target_pairs={{0,1},{1,2},{2,3},{3,4},{4,5},{5,6},{6,7},{8,9},{9,10},{10,11},{11... | collective-permute-start | bytes 138248 | tf_op jit(solution)/shard_map/ppermute | solution.py:26
  179.0 2.1 %collective-permute-done.6 = f32[1,1,4,45,64]{3,4,2,1,0:T(8,128)S(1)} collective-permute-done((f32[1,1,4,45,64]{3,4,2,1,0:T(8,128)S(1)}, f32[1,1,4,45,64]{3,4,2,1,0:T(8,128)S(1)}, u32[]{:S(2)}, u32[]{:S(2)}) %collective-permute-start.6) | collective-permute-done | bytes 46112 | tf_op jit(solution)/shard_map/ppermute | solution.py:26
  187.6 5.7 %collective-permute-start.11 = (f32[1,1,4,45,64]{3,4,2,1,0:T(8,128)S(1)}, f32[1,1,4,45,64]{3,4,2,1,0:T(8,128)S(1)}, u32[]{:S(2)}, u32[]{:S(2)}) collective-permute-start(f32[1,1,4,45,64]{3,4,2,1,0:T(8,128)S(1)} %select_bitcast_fusion.3), channel_id=1, source_target_pairs={{8,0},{16,8},{24,16},{32,24},{40,32},{48,40},{56,48},{64,56},{72,6... | collective-permute-start | bytes 138248 | tf_op jit(solution)/shard_map/ppermute | solution.py:27
  197.2 2.4 %collective-permute-start.8 = (f32[1,1,4,45,64]{3,4,2,1,0:T(8,128)S(1)}, f32[1,1,4,45,64]{3,4,2,1,0:T(8,128)S(1)}, u32[]{:S(2)}, u32[]{:S(2)}) collective-permute-start(f32[1,1,4,45,64]{3,4,2,1,0:T(8,128)S(1)} %select_bitcast_fusion.3), channel_id=1, source_target_pairs={{0,1},{1,2},{2,3},{3,4},{4,5},{5,6},{6,7},{8,9},{9,10},{10,11},{11... | collective-permute-start | bytes 138248 | tf_op jit(solution)/shard_map/ppermute | solution.py:26
  199.6 2.7 %collective-permute-done.10 = f32[1,1,4,45,64]{3,4,2,1,0:T(8,128)S(1)} collective-permute-done((f32[1,1,4,45,64]{3,4,2,1,0:T(8,128)S(1)}, f32[1,1,4,45,64]{3,4,2,1,0:T(8,128)S(1)}, u32[]{:S(2)}, u32[]{:S(2)}) %collective-permute-start.10) | collective-permute-done | bytes 46112 | tf_op jit(solution)/shard_map/ppermute | solution.py:26
  (196 shorter events, 43.3 us)
Async XLA Ops:
  0.6 58.1 %copy-start = (f32[135,270]{1,0:T(8,128)S(1)}, f32[135,270]{1,0:T(8,128)}, u32[]{:S(2)}) copy-start(f32[135,270]{1,0:T(8,128)} %param.39) | copy-start | bytes 437404
  5.1 31.8 %copy-start.4 = (f32[5,27,128]{2,1,0:T(8,128)S(1)}, f32[5,27,128]{2,1,0:T(8,128)}, u32[]{:S(2)}) copy-start(f32[5,27,128]{2,1,0:T(8,128)} %param.32) | copy-start | bytes 207364
  5.1 31.8 %copy-start.7 = (f32[5,27,128]{2,1,0:T(8,128)S(1)}, f32[5,27,128]{2,1,0:T(8,128)}, u32[]{:S(2)}) copy-start(f32[5,27,128]{2,1,0:T(8,128)} %param.33) | copy-start | bytes 207364
  5.1 31.8 %copy-start.3 = (f32[3,27,128]{2,1,0:T(8,128)S(1)}, f32[3,27,128]{2,1,0:T(8,128)}, u32[]{:S(2)}) copy-start(f32[3,27,128]{2,1,0:T(8,128)} %param.28) | copy-start | bytes 124420
  6.3 31.8 %collective-permute-start.3 = (f32[1,1,4,45,64]{3,4,2,1,0:T(8,128)S(1)}, f32[1,1,4,45,64]{3,4,2,1,0:T(8,128)S(1)}, u32[]{:S(2)}, u32[]{:S(2)}) collective-permute-start(f32[1,1,4,45,64]{3,4,2,1,0:T(8,128)S(1)} %select_bitcast_fusion.5), channel_id=1, source_target_pairs={{8,0},{16,8},{24,16},{32,24},{40,32},{48,40},{56,48},{64,56},{72,6... | collective-permute-start | bytes 138248 | tf_op jit(solution)/shard_map/ppermute | solution.py:27
  17.6 20.5 %collective-permute-start.2 = (f32[1,1,4,45,64]{3,4,2,1,0:T(8,128)S(1)}, f32[1,1,4,45,64]{3,4,2,1,0:T(8,128)S(1)}, u32[]{:S(2)}, u32[]{:S(2)}) collective-permute-start(f32[1,1,4,45,64]{3,4,2,1,0:T(8,128)S(1)} %select_bitcast_fusion.5), channel_id=1, source_target_pairs={{0,8},{8,16},{16,24},{24,32},{32,40},{40,48},{48,56},{56,64},{64,7... | collective-permute-start | bytes 138248 | tf_op jit(solution)/shard_map/ppermute | solution.py:26
  19.5 18.6 %collective-permute-start.1 = (f32[1,1,4,45,64]{3,4,2,1,0:T(8,128)S(1)}, f32[1,1,4,45,64]{3,4,2,1,0:T(8,128)S(1)}, u32[]{:S(2)}, u32[]{:S(2)}) collective-permute-start(f32[1,1,4,45,64]{3,4,2,1,0:T(8,128)S(1)} %select_bitcast_fusion.5), channel_id=1, source_target_pairs={{1,0},{2,1},{3,2},{4,3},{5,4},{6,5},{7,6},{9,8},{10,9},{11,10},{12... | collective-permute-start | bytes 138248 | tf_op jit(solution)/shard_map/ppermute | solution.py:27
  21.4 16.7 %collective-permute-start = (f32[1,1,4,45,64]{3,4,2,1,0:T(8,128)S(1)}, f32[1,1,4,45,64]{3,4,2,1,0:T(8,128)S(1)}, u32[]{:S(2)}, u32[]{:S(2)}) collective-permute-start(f32[1,1,4,45,64]{3,4,2,1,0:T(8,128)S(1)} %select_bitcast_fusion.5), channel_id=1, source_target_pairs={{0,1},{1,2},{2,3},{3,4},{4,5},{5,6},{6,7},{8,9},{9,10},{10,11},{11... | collective-permute-start | bytes 138248 | tf_op jit(solution)/shard_map/ppermute | solution.py:26
  25.4 25.5 %all-to-all-start = ((f32[64,1,192]{2,1,0:T(1,128)}), f32[64,1,192]{2,1,0:T(1,128)S(1)}, u32[]{:S(2)}, u32[]{:S(2)}) async-start(f32[64,1,192]{2,1,0:T(1,128)} %reshape.310), calls=%async_computation | async-start | bytes 131072 | tf_op jit(solution)/shard_map/all_to_all | solution.py:40
  53.7 12.5 %all-to-all-start.1 = ((f32[8,1,12288]{2,1,0:T(1,128)}), f32[8,1,12288]{2,1,0:T(1,128)S(1)}, u32[]{:S(2)}, u32[]{:S(2)}) async-start(f32[8,1,12288]{2,1,0:T(1,128)} %reshape.312), calls=%async_computation.1 | async-start | bytes 786432 | tf_op jit(solution)/shard_map/all_to_all | solution.py:40
  69.6 95.9 %copy-start.17 = (f32[27,8,1]{0,1,2:T(8,128)S(1)}, f32[27,8,1]{0,1,2:T(8,128)}, u32[]{:S(2)}) copy-start(f32[27,8,1]{0,1,2:T(8,128)} %constant.102) | copy-start | bytes 2596
  69.6 96.1 %copy-start.8 = (f32[3,27,27,1]{2,1,0,3:T(8,128)S(1)}, f32[3,27,27,1]{2,1,0,3:T(8,128)}, u32[]{:S(2)}) copy-start(f32[3,27,27,1]{2,1,0,3:T(8,128)} %constant.103) | copy-start | bytes 26248
  69.6 96.5 %copy-start.1 = (f32[135,135]{1,0:T(8,128)S(1)}, f32[135,135]{1,0:T(8,128)}, u32[]{:S(2)}) copy-start(f32[135,135]{1,0:T(8,128)} %param.37) | copy-start | bytes 218704
  69.6 96.5 %copy-start.5 = (f32[135,128]{1,0:T(8,128)S(1)}, f32[135,128]{1,0:T(8,128)}, u32[]{:S(2)}) copy-start(f32[135,128]{1,0:T(8,128)} %convolution_bitcast_fusion.8) | copy-start | bytes 207364
  69.6 96.5 %copy-start.13 = (pred[128]{0:T(512)(128)(4,1)S(1)}, pred[128]{0:T(512)(128)(4,1)}, u32[]{:S(2)}) copy-start(pred[128]{0:T(512)(128)(4,1)} %copy-done.12) | copy-start | bytes 388
  69.6 96.8 %copy-start.2 = (f32[135,135]{1,0:T(8,128)S(1)}, f32[135,135]{1,0:T(8,128)}, u32[]{:S(2)}) copy-start(f32[135,135]{1,0:T(8,128)} %param.38) | copy-start | bytes 218704
  168.5 10.4 %collective-permute-start.7 = (f32[1,1,4,45,64]{3,4,2,1,0:T(8,128)S(1)}, f32[1,1,4,45,64]{3,4,2,1,0:T(8,128)S(1)}, u32[]{:S(2)}, u32[]{:S(2)}) collective-permute-start(f32[1,1,4,45,64]{3,4,2,1,0:T(8,128)S(1)} %select_bitcast_fusion.4), channel_id=1, source_target_pairs={{8,0},{16,8},{24,16},{32,24},{40,32},{48,40},{56,48},{64,56},{72,6... | collective-permute-start | bytes 138248 | tf_op jit(solution)/shard_map/ppermute | solution.py:27
  172.1 9.0 %collective-permute-start.6 = (f32[1,1,4,45,64]{3,4,2,1,0:T(8,128)S(1)}, f32[1,1,4,45,64]{3,4,2,1,0:T(8,128)S(1)}, u32[]{:S(2)}, u32[]{:S(2)}) collective-permute-start(f32[1,1,4,45,64]{3,4,2,1,0:T(8,128)S(1)} %select_bitcast_fusion.4), channel_id=1, source_target_pairs={{0,8},{8,16},{16,24},{24,32},{32,40},{40,48},{48,56},{56,64},{64,7... | collective-permute-start | bytes 138248 | tf_op jit(solution)/shard_map/ppermute | solution.py:26
  174.4 6.7 %collective-permute-start.5 = (f32[1,1,4,45,64]{3,4,2,1,0:T(8,128)S(1)}, f32[1,1,4,45,64]{3,4,2,1,0:T(8,128)S(1)}, u32[]{:S(2)}, u32[]{:S(2)}) collective-permute-start(f32[1,1,4,45,64]{3,4,2,1,0:T(8,128)S(1)} %select_bitcast_fusion.4), channel_id=1, source_target_pairs={{1,0},{2,1},{3,2},{4,3},{5,4},{6,5},{7,6},{9,8},{10,9},{11,10},{12... | collective-permute-start | bytes 138248 | tf_op jit(solution)/shard_map/ppermute | solution.py:27
  176.3 6.3 %collective-permute-start.4 = (f32[1,1,4,45,64]{3,4,2,1,0:T(8,128)S(1)}, f32[1,1,4,45,64]{3,4,2,1,0:T(8,128)S(1)}, u32[]{:S(2)}, u32[]{:S(2)}) collective-permute-start(f32[1,1,4,45,64]{3,4,2,1,0:T(8,128)S(1)} %select_bitcast_fusion.4), channel_id=1, source_target_pairs={{0,1},{1,2},{2,3},{3,4},{4,5},{5,6},{6,7},{8,9},{9,10},{10,11},{11... | collective-permute-start | bytes 138248 | tf_op jit(solution)/shard_map/ppermute | solution.py:26
  187.6 12.0 %collective-permute-start.11 = (f32[1,1,4,45,64]{3,4,2,1,0:T(8,128)S(1)}, f32[1,1,4,45,64]{3,4,2,1,0:T(8,128)S(1)}, u32[]{:S(2)}, u32[]{:S(2)}) collective-permute-start(f32[1,1,4,45,64]{3,4,2,1,0:T(8,128)S(1)} %select_bitcast_fusion.3), channel_id=1, source_target_pairs={{8,0},{16,8},{24,16},{32,24},{40,32},{48,40},{56,48},{64,56},{72,6... | collective-permute-start | bytes 138248 | tf_op jit(solution)/shard_map/ppermute | solution.py:27
  193.3 9.0 %collective-permute-start.10 = (f32[1,1,4,45,64]{3,4,2,1,0:T(8,128)S(1)}, f32[1,1,4,45,64]{3,4,2,1,0:T(8,128)S(1)}, u32[]{:S(2)}, u32[]{:S(2)}) collective-permute-start(f32[1,1,4,45,64]{3,4,2,1,0:T(8,128)S(1)} %select_bitcast_fusion.3), channel_id=1, source_target_pairs={{0,8},{8,16},{16,24},{24,32},{32,40},{40,48},{48,56},{56,64},{64,7... | collective-permute-start | bytes 138248 | tf_op jit(solution)/shard_map/ppermute | solution.py:26
  195.2 7.0 %collective-permute-start.9 = (f32[1,1,4,45,64]{3,4,2,1,0:T(8,128)S(1)}, f32[1,1,4,45,64]{3,4,2,1,0:T(8,128)S(1)}, u32[]{:S(2)}, u32[]{:S(2)}) collective-permute-start(f32[1,1,4,45,64]{3,4,2,1,0:T(8,128)S(1)} %select_bitcast_fusion.3), channel_id=1, source_target_pairs={{1,0},{2,1},{3,2},{4,3},{5,4},{6,5},{7,6},{9,8},{10,9},{11,10},{12... | collective-permute-start | bytes 138248 | tf_op jit(solution)/shard_map/ppermute | solution.py:27
  197.2 6.3 %collective-permute-start.8 = (f32[1,1,4,45,64]{3,4,2,1,0:T(8,128)S(1)}, f32[1,1,4,45,64]{3,4,2,1,0:T(8,128)S(1)}, u32[]{:S(2)}, u32[]{:S(2)}) collective-permute-start(f32[1,1,4,45,64]{3,4,2,1,0:T(8,128)S(1)} %select_bitcast_fusion.3), channel_id=1, source_target_pairs={{0,1},{1,2},{2,3},{3,4},{4,5},{5,6},{6,7},{8,9},{9,10},{10,11},{11... | collective-permute-start | bytes 138248 | tf_op jit(solution)/shard_map/ppermute | solution.py:26
  (11 other events, 137.0 us)
where the time goes:
time: 208 us; the launch traced here: 207 us
  matrix products  92.2 us (44%)
  starting transfers between devices  56.3 us (27%)
  local copies, waits for them, and re-layouts  25.2 us (12%)
  waiting for transfers between devices  24.5 us (12%)
  other arithmetic  5.79 us (3%)
  between operations  2.98 us (1%)
    dot_general x17, matrix products, matmul(): jnp.dot(left, right, precision=HIGH, preferred_element_type=jnp.float32)  91.6 us
    ppermute x6, starting transfers between devices, padded_2(): lax.ppermute(initial, axis, [(b, a) for a, b in up])  26.4 us
    all_to_all x2, waiting for transfers between devices, from_everyone(): return lax.all_to_all(copies, axis, split_axis=0, concat_axis=0, tiled=True)  17 us
    all_to_all x2, starting transfers between devices, from_everyone(): return lax.all_to_all(copies, axis, split_axis=0, concat_axis=0, tiled=True)  16.4 us
    ppermute x6, starting transfers between devices, padded_2(): lax.ppermute(last, axis, up)  13.5 us
    ppermute x6, waiting for transfers between devices, padded_2(): lax.ppermute(last, axis, up)  7.46 us
    sub x8, local copies, waits for them, and re-layouts, one_corner(): dist_sq = (coords[0][None, :] - centers[0][:, None]) ** 2  5.68 us
    gather x6, local copies, waits for them, and re-layouts, per_device(): jnp.take(full_table, face_link, axis=1, mode='fill', fill_value=0.0)  5.35 us
  transfers between devices with their start and end apart: 14, of which 6 were waited for; matrix products, arithmetic and copies ran while one was open for 3% of the time, Pallas kernels for 0%

commit v1 on v0

v1 whole, which is shorter than its diff:
```python
import functools

import jax
import jax.numpy as jnp
import numpy as np
from jax import lax
from jax.experimental import pallas as pl
from jax.experimental.pallas import tpu as pltpu
from jax.sharding import PartitionSpec as P

ITERS = 3
BOTH = ("elem", "sub")
RADIUS = 1.5
FAR = 1000.0
LANES = 128
STRIP = 512
RUN = 768
TILES = 16
SLOTS = 8
INTERPRET = False
F32, BF16, I32 = jnp.float32, jnp.bfloat16, jnp.int32
VMEM = pltpu.MemorySpace.VMEM
SMEM = pltpu.MemorySpace.SMEM


def node_tables():
    slopes = np.array([[-1.5, 2.0, -0.5], [-0.5, 0.0, 0.5], [0.5, -2.0, 1.5]])
    one = np.eye(3)
    derivs = np.zeros((96, 32), np.float32)
    for axis, full in enumerate(
        (
            np.kron(one, np.kron(one, slopes)),
            np.kron(one, np.kron(slopes, one)),
            np.kron(slopes, np.eye(9)),
        )
    ):
        derivs[32 * axis : 32 * axis + 27, :27] = full
    blending = np.zeros((32, 8), np.float32)
    for node in range(27):
        place = (node % 3 - 1.0, node // 3 % 3 - 1.0, node // 9 - 1.0)
        for corner in range(8):
            weight = 1.0
            for axis in range(3):
                side = 1.0 if corner >> axis & 1 else -1.0
                weight *= (1.0 + side * place[axis]) / 2.0
            blending[node, corner] = weight
    select = np.zeros((288, 136), np.float32)
    for face in range(6):
        axis, layer = face // 2, 2 * (face % 2)
        nodes = [n for n in range(27) if n // 3**axis % 3 == layer]
        for var in range(5):
            for at, node in enumerate(nodes):
                select[48 * face + 9 * var + at, 27 * var + node] = 1.0
    place = np.zeros((270, 288), np.float32)
    for face in range(6):
        for entry in range(45):
            place[6 * entry + face, 48 * face + entry] = 1.0
    return derivs, blending, select, place


CORNERS = [2 * (c & 1) + 6 * (c >> 1 & 1) + 18 * (c >> 2) for c in range(8)]


def hdot(a, b):
    return jnp.dot(a, b, precision=lax.Precision.HIGHEST, preferred_element_type=F32)


def pieces(x, count):
    out = []
    for _ in range(count):
        piece = x.astype(BF16)
        out.append(piece)
        x = x - piece.astype(F32)
    return out


def split_dot(a, b):
    a1, a2 = pieces(a, 2)
    b1, b2 = pieces(b, 2)
    high = jnp.dot(a1, b1, preferred_element_type=F32)
    return high + (jnp.dot(a1, b2, preferred_element_type=F32) + jnp.dot(a2, b1, preferred_element_type=F32))


def pick_dot(a, b, count=2):
    out = None
    for piece in pieces(b, count):
        part = jnp.dot(a, piece, preferred_element_type=F32)
        out = part if out is None else out + part
    return out


def nt_dot(a, b):
    return lax.dot_general(a, b, (((1,), (1,)), ((), ())), preferred_element_type=F32)


def iota(shape, dim):
    return lax.broadcasted_iota(I32, shape, dim)


def flag(mask, dtype=F32):
    return jnp.where(mask, 1.0, 0.0).astype(dtype)


def call(body, out_shape, in_spaces, scratch=(), held=True, **kw):
    def place(s):
        return pltpu.VMEM(s.shape, s.dtype) if held and not INTERPRET else s

    run = pl.pallas_call(
        body,
        out_shape=jax.tree.map(place, out_shape),
        in_specs=[pl.BlockSpec(memory_space=s) for s in in_spaces],
        out_specs=jax.tree.map(lambda _: pl.BlockSpec(memory_space=VMEM), out_shape),
        scratch_shapes=list(scratch),
        interpret=INTERPRET,
        **kw,
    )

    def placed(*args):
        if INTERPRET:
            return run(*args)
        return run(*[pltpu.with_memory_space_constraint(a, s) for a, s in zip(args, in_spaces, strict=True)])

    return placed


def shape_of(*dims, dtype=F32):
    return jax.ShapeDtypeStruct(dims, dtype)


def payload_body(count_ref, pos_ref, coef_ref, out_ref, row_ref):
    count = count_ref[0]
    live = iota((1, 32), 1) < count
    for axis in range(3):
        lanes = slice(32 * axis, 32 * axis + 32)
        row_ref[0:1, lanes] = jnp.where(live, pos_ref[axis : axis + 1, :], FAR)
        row_ref[1:2, lanes] = jnp.where(live, coef_ref[axis : axis + 1, :], 0.0)
    row_ref[0:1, 96:128] = jnp.zeros((1, 32), F32)
    row_ref[1:2, 96:128] = jnp.full((1, 32), count, I32).astype(F32)
    out_ref[...] = jnp.broadcast_to(row_ref[0:2, :][None], out_ref.shape)


def compact_body(in_ref, out_ref, part_ref):
    owners = in_ref.shape[0]
    copies, _, room = out_ref.shape
    first, second = in_ref[:, 0, :], in_ref[:, 1, :]
    wide = jnp.broadcast_to(second[:, 96:97], (owners, LANES))
    below = flag(iota((owners, owners), 1) < iota((owners, owners), 0), BF16)
    above = flag(iota((owners, owners), 0) < iota((owners, owners), 1), BF16)
    start_col = jnp.dot(below, wide.astype(BF16), preferred_element_type=F32)
    pick = flag(iota((8, LANES), 1) == 96, BF16)
    count_row = nt_dot(pick, second.astype(BF16))
    start_row = jnp.dot(count_row.astype(BF16), above, preferred_element_type=F32)
    total = jnp.max(start_row + count_row).astype(I32)
    low, end = start_row[0:1, :], (start_row + count_row)[0:1, :]
    for at, piece in enumerate(pieces(first, 3)):
        part_ref[:, LANES * at : LANES * at + LANES] = piece
    for at, piece in enumerate(pieces(second, 3)):
        part_ref[:, LANES * (3 + at) : LANES * (4 + at)] = piece
    for at, piece in enumerate(pieces(start_col, 2)):
        part_ref[:, LANES * (6 + at) : LANES * (7 + at)] = piece
    feature, group = iota((8, LANES), 0), iota((8, LANES), 1) // 32
    fold_first = flag((feature < 3) & (feature == group), BF16)
    fold_second = flag((feature > 3) & (feature < 7) & (feature == group + 4), BF16)
    strip = min(STRIP, room)
    slot = (iota((strip, LANES), 1) % 32).astype(F32)

    def one_strip(at, carry):
        place = (iota((strip, owners), 0) + at * strip).astype(F32)
        owner = flag((place >= low) & (place < end), BF16)
        found = jnp.dot(owner, part_ref[...], preferred_element_type=F32)
        start = found[:, 6 * LANES : 7 * LANES] + found[:, 7 * LANES :]
        here = (iota((strip, LANES), 0) + at * strip).astype(F32)
        mine = slot == here - start
        out = None
        for k in range(3):
            a = jnp.where(mine, found[:, LANES * k : LANES * k + LANES], 0.0).astype(BF16)
            b = jnp.where(mine, found[:, LANES * (3 + k) : LANES * (4 + k)], 0.0).astype(BF16)
            both = nt_dot(fold_first, a) + nt_dot(fold_second, b)
            out = both if out is None else out + both
        dead = iota((8, strip), 1) + at * strip >= total
        row = iota((8, strip), 0)
        out = jnp.where(dead, jnp.where(row < 3, FAR, 0.0), out)
        square = jnp.sum(jnp.where(row < 3, out * out, 0.0), axis=0, keepdims=True)
        out = jnp.where(row == 3, square, out)
        out = jnp.where(row == 7, total.astype(F32), out)
        out_ref[:, :, pl.ds(pl.multiple_of(at * strip, LANES), strip)] = jnp.broadcast_to(
            out[None], (copies, 8, strip)
        )
        return carry

    lax.fori_loop(0, (total + (strip - 1)) // strip, one_strip, 0)


def radial_displacement(z_ref, node_ref, corner_ref, hit_ref, rank_ref, list_ref, sum_ref, over_ref, over_smem, sem):
    groups, _, room = z_ref.shape
    run = min(RUN, room)
    blocks = run // LANES
    at = [[node_ref[i, k : k + 1, :] for k in CORNERS] for i in range(3)]
    middle, reach = [], [None] * 8
    for i in range(3):
        low = functools.reduce(jnp.minimum, at[i])
        high = functools.reduce(jnp.maximum, at[i])
        middle.append(0.5 * (low + high))
        for c in range(8):
            gap = (at[i][c] - middle[i]) ** 2
            reach[c] = gap if i == 0 else reach[c] + gap
    limit = RADIUS + jnp.sqrt(functools.reduce(jnp.maximum, reach))
    offset = middle[0] ** 2 + middle[1] ** 2 + middle[2] ** 2 - limit * limit - 0.02
    row = iota((LANES, LANES), 0)
    table = jnp.where(row == 3, 1.0, 0.0)
    for i in range(3):
        table = jnp.where(row == i, -2.0 * middle[i], table)
    probe = jnp.transpose(table)[:, 0:8]
    offset = jnp.transpose(jnp.broadcast_to(offset, (LANES, LANES)))
    offset = jnp.concatenate([offset] * blocks, axis=1)
    pick = iota((8, LANES), 0) * TILES + iota((8, LANES), 1) % TILES
    for i in range(3):
        for c in range(8):
            corner_ref[i, 8 * c : 8 * c + 8, :] = jnp.take_along_axis(
                jnp.broadcast_to(at[i][c], (8, LANES)), pick, axis=1
            )
        sum_ref[i] = jnp.zeros((64, LANES), F32)
    counts = [jnp.max(z_ref[g, 7:8, 0:LANES]).astype(I32) for g in range(groups)]
    most = functools.reduce(jnp.maximum, counts)
    source, target = iota((LANES, 2 * LANES), 0), iota((LANES, 2 * LANES), 1)
    same_half = source // 64 == target // 64
    prefix = flag(
        (target < LANES) & same_half & (source <= target)
        | (target >= LANES) & (source // 64 == target - LANES),
        BF16,
    )
    half = iota((TILES, LANES), 1) // 64

    def extract(g, start, block, shift):
        points = z_ref[g, :, pl.ds(pl.multiple_of(start + block * LANES, LANES), LANES)]
        three = jnp.concatenate([p.astype(F32) for p in pieces(points, 3)], axis=0).astype(BF16)
        rank = rank_ref[pl.ds(pl.multiple_of((g * blocks + block) * TILES, TILES), TILES), :]
        entries = []
        for h in range(2):
            key = jnp.where(half == h, rank - shift, 0.0)
            chosen = jnp.concatenate([flag(key == s + 1.0) for s in range(SLOTS)], axis=0).astype(BF16)
            found = nt_dot(three, chosen)
            entries.append(found[0:8] + found[8:16] + found[16:24])
        return entries

    def one_part(part, carry):
        first = part * run
        start = jnp.minimum(first, room - run)
        for g in range(groups):
            points = z_ref[g, :, pl.ds(pl.multiple_of(start, LANES), run)]
            gap = hdot(probe, points) + offset
            best = gap[0:TILES]
            for e in range(1, 8):
                best = jnp.minimum(best, gap[TILES * e : TILES * e + TILES])
            lane = iota((TILES, run), 1) + start
            hit = flag((best <= 0.0) & (lane >= first) & (lane < counts[g]))
            for b in range(blocks):
                hit_ref[(g * blocks + b) * TILES : (g * blocks + b + 1) * TILES, :] = hit[:, LANES * b : LANES * b + LANES]
        hits = hit_ref[...]
        ranks = jnp.dot(hits.astype(BF16), prefix, preferred_element_type=F32)
        rank_ref[...] = jnp.where(hits > 0.0, ranks[:, 0:LANES], -1000.0)
        filled = ranks[:, LANES:].reshape(groups * blocks, TILES, LANES)
        filled = jnp.max(filled, axis=1).astype(I32)
        over_ref[...] = filled
        copy = pltpu.make_async_copy(over_ref, over_smem, sem)
        copy.start()
        length = jnp.int32(0)
        for g in range(groups):
            inside = jnp.clip(counts[g] - start, 0, run)
            for b in range(blocks):
                one, two = extract(g, start, b, 0.0)
                list_ref[length] = one
                length = length + jnp.where(inside > LANES * b, 1, 0)
                list_ref[length] = two
                length = length + jnp.where(inside > LANES * b + 64, 1, 0)
        copy.wait()
        crowded = jnp.max(filled) > SLOTS

        def more(length):
            def block_more(index, length):
                g, b = index // blocks, index % blocks

                def round_more(r, length):
                    one, two = extract(g, start, b, (r * SLOTS).astype(F32))
                    list_ref[length] = one
                    length = length + jnp.where(over_smem[index, 0] > r * SLOTS, 1, 0)
                    list_ref[length] = two
                    length = length + jnp.where(over_smem[index, 1] > r * SLOTS, 1, 0)
                    return length

                rounds = (jnp.maximum(over_smem[index, 0], over_smem[index, 1]) + SLOTS - 1) // SLOTS
                return lax.fori_loop(1, rounds, round_more, length)

            return lax.fori_loop(0, groups * blocks, block_more, length)

        length = lax.cond(crowded, more, lambda n: n, length)
        for e in range(4):
            list_ref[length + e] = jnp.zeros((8, LANES), F32)

        def four(step, carry):
            for i in range(2):
                for c in range(0, 64, 8):
                    total = [sum_ref[axis, c : c + 8, :] for axis in range(3)]
                    place = [corner_ref[axis, c : c + 8, :] for axis in range(3)]
                    for e in range(2):
                        entry = list_ref.at[4 * step + 2 * i + e]
                        gap = [place[axis] - entry[axis : axis + 1, :] for axis in range(3)]
                        square = gap[0] * gap[0] + gap[1] * gap[1] + gap[2] * gap[2]
                        ratio = square * lax.rsqrt(jnp.maximum(square, 1e-20)) * (1.0 / RADIUS)
                        inside = jnp.maximum(1.0 - ratio, 0.0)
                        inside = inside * inside
                        kernel = inside * inside * (4.0 * ratio + 1.0)
                        for axis in range(3):
                            total[axis] = total[axis] + entry[4 + axis : 5 + axis, :] * kernel
                    for axis in range(3):
                        sum_ref[axis, c : c + 8, :] = total[axis]
            return carry

        lax.fori_loop(0, (length + 3) // 4, four, 0)
        return carry

    lax.fori_loop(0, (most + (run - 1)) // run, one_part, 0)
    spread = flag(iota((LANES, LANES), 0) % TILES == iota((LANES, LANES), 1) % TILES, BF16)
    own = iota((8, LANES), 0) == iota((8, LANES), 1) // TILES
    out = []
    for i in range(3):
        total = None
        for piece in pieces(sum_ref[i], 3):
            part = jnp.dot(piece, spread, preferred_element_type=F32)
            total = part if total is None else total + part
        rows = [
            jnp.sum(jnp.where(own, total[8 * c : 8 * c + 8], 0.0), axis=0, keepdims=True) for c in range(8)
        ]
        out.append(jnp.concatenate(rows, axis=0))
    return out


def radial_body(
    z_ref, node_ref, derivs_ref, blend_ref, base_ref, start_ref, minus_inv_ref, count_ref, select_ref, send_ref,
    m_ref, where_ref, q0, q1, q2, q3,
    disp_ref, metric_ref, state_ref, trace_ref, packet_ref,
    corner_ref, hit_ref, rank_ref, list_ref, sum_ref, over_ref, over_smem, sem, nodes_ref, remote_ref,
):
    base = base_ref[...] + from_neighbours(q0, q1, q2, q3, where_ref, m_ref, remote_ref)
    corner = radial_displacement(
        z_ref, node_ref, corner_ref, hit_ref, rank_ref, list_ref, sum_ref, over_ref, over_smem, sem
    )
    nodes_ref[...] = jnp.zeros_like(nodes_ref)
    for i in range(3):
        shift = hdot(blend_ref[...], corner[i])
        disp_ref[i] = shift[0:27]
        nodes_ref[0:27, LANES * i : LANES * i + LANES] = node_ref[i] + shift[0:27]
    jac = hdot(derivs_ref[...], nodes_ref[...])
    j = [[jac[32 * l : 32 * l + 32, LANES * i : LANES * i + LANES] for l in range(3)] for i in range(3)]
    minor_a = j[1][1] * j[2][2] - j[1][2] * j[2][1]
    minor_b = j[1][0] * j[2][2] - j[1][2] * j[2][0]
    minor_c = j[1][0] * j[2][1] - j[1][1] * j[2][0]
    metric = 8.0 * (j[0][0] * minor_a - j[0][1] * minor_b + j[0][2] * minor_c)
    metric_ref[...] = jnp.zeros_like(metric_ref)
    for v in range(5):
        metric_ref[27 * v : 27 * v + 27, :] = metric[0:27]
    state = base + split_dot(minus_inv_ref[...], metric_ref[...] * start_ref[...])
    finish(state, count_ref, select_ref, send_ref, state_ref, trace_ref, packet_ref)


def finish(state, count_ref, select_ref, send_ref, state_ref, trace_ref, packet_ref):
    state = jnp.where(iota(state.shape, 1) < count_ref[0], state, 0.0)
    state_ref[...] = state
    traces = pick_dot(select_ref[...], state, 3)
    for f in range(6):
        trace_ref[f] = traces[48 * f : 48 * f + 48]
    tiles = [traces[48 * f : 48 * f + 48] for f in range(6)]
    for pair in range(2):
        packet_ref[pair] = gather_columns(tiles, send_ref[pair : pair + 1, :], 0)


def gather_columns(tiles, index, first):
    rows = tiles[0].shape[0]
    tile = jnp.broadcast_to(index // LANES - first, (rows, LANES))
    lane = jnp.broadcast_to(index % LANES, (rows, LANES))
    out = jnp.zeros((rows, LANES), F32)
    for t, values in enumerate(tiles):
        out = jnp.where(tile == t, jnp.take_along_axis(values, lane, axis=1), out)
    return out


def from_neighbours(q0, q1, q2, q3, where_ref, m_ref, remote_ref):
    for at, q in enumerate((q0, q1, q2, q3)):
        remote_ref[at // 2, :, 64 * (at % 2) : 64 * (at % 2) + 64] = q[...]
    tiles = [remote_ref[0], remote_ref[1]]
    total = None
    for f in range(6):
        found = gather_columns(tiles, where_ref[f : f + 1, :], 6)
        part = split_dot(m_ref[f], found)
        total = part if total is None else total + part
    return total


def setup_state_body(u_ref, count_ref, select_ref, send_ref, state_ref, trace_ref, packet_ref, flat_ref):
    flat_ref[...] = jnp.zeros_like(flat_ref)
    for v in range(5):
        flat_ref[27 * v : 27 * v + 27, :] = u_ref[v]
    finish(flat_ref[...], count_ref, select_ref, send_ref, state_ref, trace_ref, packet_ref)


def setup_matrix_body(
    vol_ref, inv_ref, lift_ref, place_ref, right_ref, state_ref, trace_ref, where_ref,
    minus_ref, both_ref, m_ref, const_ref, base_ref, flat_ref, wide_ref,
):
    wide_ref[...] = jnp.zeros_like(wide_ref)
    wide_ref[0:135, 0:135] = inv_ref[...]
    inverse = wide_ref[:, 0:136]
    minus_ref[...] = -inverse
    both_ref[...] = jnp.zeros_like(both_ref)
    both_ref[0:135, 0:135] = -hdot(inv_ref[...], vol_ref[...])
    m_ref[...] = jnp.zeros_like(m_ref)
    coupling = hdot(inv_ref[...], lift_ref[...])
    moved = None
    for piece in pieces(coupling, 3):
        part = jnp.dot(piece, place_ref[...], preferred_element_type=F32)
        moved = part if moved is None else moved + part
    for f in range(6):
        m_ref[f, 0:135, :] = moved[:, 48 * f : 48 * f + 48]
    flat_ref[...] = jnp.zeros_like(flat_ref)
    for v in range(5):
        flat_ref[27 * v : 27 * v + 27, :] = right_ref[v]
    const = split_dot(inverse, flat_ref[...])
    const_ref[...] = const
    state = state_ref[...]
    base_ref[...] = state + const + split_dot(both_ref[...], state) + local_part(trace_ref, where_ref, m_ref)


def local_part(trace_ref, where_ref, m_ref):
    tiles = [trace_ref[f] for f in range(6)]
    total = None
    for f in range(6):
        found = gather_columns(tiles, where_ref[f : f + 1, :], 0)
        part = split_dot(m_ref[f], found)
        total = part if total is None else total + part
    return total


def local_body(state_ref, trace_ref, metric_ref, const_ref, minus_ref, both_ref, m_ref, where_ref, out_ref):
    state = state_ref[...]
    out = state + const_ref[...] + split_dot(both_ref[...], state)
    out = out + split_dot(minus_ref[...], metric_ref[...] * state)
    out_ref[...] = out + local_part(trace_ref, where_ref, m_ref)


def sweep_body(
    base_ref, count_ref, select_ref, send_ref, m_ref, where_ref, q0, q1, q2, q3,
    state_ref, trace_ref, packet_ref, remote_ref,
):
    state = base_ref[...] + from_neighbours(q0, q1, q2, q3, where_ref, m_ref, remote_ref)
    finish(state, count_ref, select_ref, send_ref, state_ref, trace_ref, packet_ref)


def last_body(base_ref, count_ref, m_ref, where_ref, q0, q1, q2, q3, out_ref, remote_ref, state_ref):
    state = base_ref[...] + from_neighbours(q0, q1, q2, q3, where_ref, m_ref, remote_ref)
    state_ref[...] = jnp.where(iota(state.shape, 1) < count_ref[0], state, 0.0)
    for v in range(5):
        out_ref[v] = state_ref[27 * v : 27 * v + 27, :]


def exchange(packets):
    out = []
    for q, (axis, step) in enumerate((("sub", 1), ("sub", -1), ("elem", 1), ("elem", -1))):
        size = lax.axis_size(axis)
        pairs = [(i, i + step) for i in range(size) if 0 <= i + step < size]
        packet = packets[q // 2, :, 64 * (q % 2) : 64 * (q % 2) + 64]
        out.append(lax.ppermute(packet, axis, pairs))
    return out


def spread(copies, axis):
    return lax.all_to_all(copies, axis, split_axis=0, concat_axis=0, tiled=True)


def per_device(
    node_ref, cp_pos, cp_coef, cp_count, u_prev, right_side, elem_count, face_link, send_list,
    vol_block, block_inv, lift_matrix,
):
    derivs, blending, select, place = node_tables()
    derivs, blending = jnp.asarray(derivs), jnp.asarray(blending)
    select, place = jnp.asarray(select, BF16), jnp.asarray(place, BF16)
    n_elem, n_sub = lax.axis_size("elem"), lax.axis_size("sub")
    room = n_elem * cp_pos.shape[1]
    send = send_list.reshape(2, LANES)
    state_shape = [shape_of(136, LANES), shape_of(6, 48, LANES), shape_of(2, 48, LANES)]

    copies = call(
        payload_body, shape_of(n_elem, 2, LANES), [SMEM, VMEM, VMEM], [pltpu.VMEM((8, LANES), F32)], name="payload"
    )(cp_count, cp_pos, cp_coef)
    mine = spread(copies, "elem")
    state, traces, packets = call(
        setup_state_body, state_shape, [VMEM, SMEM, VMEM, VMEM], [pltpu.VMEM((136, LANES), F32)], name="setup_state"
    )(u_prev, elem_count, select, send)
    received = exchange(packets)
    minus, both, coupling, const, base = call(
        setup_matrix_body,
        [
            shape_of(136, 136), shape_of(136, 136), shape_of(6, 136, 48),
            shape_of(136, LANES), shape_of(136, LANES),
        ],
        [VMEM] * 8,
        [pltpu.VMEM((136, LANES), F32), pltpu.VMEM((136, 256), F32)],
        name="setup_matrix",
    )(vol_block, block_inv, lift_matrix, place, right_side, state, traces, face_link)
    gathered = call(
        compact_body, shape_of(n_sub, 8, room), [VMEM], [pltpu.VMEM((n_elem, 8 * LANES), BF16)], name="compact"
    )(mine)
    points = spread(gathered, "sub")
    blocks = min(RUN, room) // LANES * n_sub
    displacement, metric, state, traces, packets = call(
        radial_body,
        [shape_of(3, 27, LANES), shape_of(136, LANES), *state_shape],
        [VMEM] * 7 + [SMEM] + [VMEM] * 8,
        [
            pltpu.VMEM((3, 64, LANES), F32),
            pltpu.VMEM((blocks * TILES, LANES), F32),
            pltpu.VMEM((blocks * TILES, LANES), F32),
            pltpu.VMEM((blocks * 16 + 8, 8, LANES), F32),
            pltpu.VMEM((3, 64, LANES), F32),
            pltpu.VMEM((blocks, LANES), I32),
            pltpu.SMEM((blocks, LANES), I32),
            pltpu.SemaphoreType.DMA,
            pltpu.VMEM((32, 3 * LANES), F32),
            pltpu.VMEM((2, 48, LANES), F32),
        ],
        name="radial",
    )(
        points, node_ref, derivs, blending, base, state, minus, elem_count, select, send,
        coupling, face_link, *received,
    )
    for sweep in range(1, ITERS):
        received = exchange(packets)
        base = call(local_body, shape_of(136, LANES), [VMEM] * 8, name="local")(
            state, traces, metric, const, minus, both, coupling, face_link
        )
        scratch = [pltpu.VMEM((2, 48, LANES), F32)]
        if sweep < ITERS - 1:
            state, traces, packets = call(
                sweep_body, state_shape, [VMEM, SMEM] + [VMEM] * 8, scratch, name="sweep"
            )(base, elem_count, select, send, coupling, face_link, *received)
        else:
            solution_out = call(
                last_body,
                shape_of(5, 27, LANES),
                [VMEM, SMEM] + [VMEM] * 6,
                scratch + [pltpu.VMEM((136, LANES), F32)],
                held=False,
                name="last",
            )(base, elem_count, coupling, face_link, *received)
    return displacement, solution_out


def solution(mesh):
    in_specs = (
        P(None, None, BOTH), P(None, BOTH), P(None, BOTH), P(BOTH), P(None, None, BOTH), P(None, None, BOTH),
        P(BOTH), P(None, BOTH), P(BOTH, None, None), P(), P(), P(),
    )
    out_specs = (P(None, None, BOTH), P(None, None, BOTH))
    return jax.shard_map(per_device, mesh=mesh, in_specs=in_specs, out_specs=out_specs, check_vma=False)
```

time: 208 us -> 99.9 us (0.48)
  the two profiles are of different devices: /device:TPU:10 before, /device:TPU:14 now
where the time goes in v1:
time: 99.9 us; the launch traced here: 99.2 us
  starting transfers between devices  39.9 us (40%)
  blocking collectives  32.3 us (32%)
  Pallas kernels  17.8 us (18%)
  waiting for transfers between devices  4.54 us (5%)
  local copies, waits for them, and re-layouts  2.35 us (2%)
  between operations  2.26 us (2%)
    ppermute x12, starting transfers between devices, exchange(): out.append(lax.ppermute(packet, axis, pairs))  35 us
    all_to_all x1, blocking collectives, spread(): return lax.all_to_all(copies, axis, split_axis=0, concat_axis=0, tiled=True)  32.3 us
    pallas_call x9, Pallas kernels, placed(): run(*[pltpu.with_memory_space_constraint(a, s) for a, s in zip(args, in_s...  17.8 us
    all_to_all x1, starting transfers between devices, spread(): return lax.all_to_all(copies, axis, split_axis=0, concat_axis=0, tiled=True)  4.92 us
    ppermute x12, waiting for transfers between devices, exchange(): out.append(lax.ppermute(packet, axis, pairs))  4.54 us
    unnamed x29, local copies, waits for them, and re-layouts  2.04 us
  transfers between devices with their start and end apart: 13, of which 4 were waited for; matrix products, arithmetic and copies ran while one was open for 1% of the time, Pallas kernels for 4%

profile of v1, /device:TPU:14, one launch (start us, length us, event | category | flops | bytes accessed | tf_op | source)
XLA Modules:
  0.0 99.2 jit_solution(10978700922744464036)
XLA Ops:
  2.7 32.3 %all_to_all.10.in_ref = f32[64,2,128]{2,1,0:T(2,128)S(1)} all-to-all(f32[64,2,128]{2,1,0:T(2,128)S(1)} %payload.1), channel_id=1, replica_groups=mesh['elem'=64,'sub'=8] {'elem'}, dimensions={0} | all-to-all | bytes 131072 | tf_op jit(solution)/shard_map/all_to_all | solution.py:476
  35.1 2.1 %compact.1 = f32[8,8,2048]{2,1,0:T(8,128)} custom-call(f32[64,2,128]{2,1,0:T(2,128)S(1)} %all_to_all.10.in_ref), custom_call_target="tpu_custom_call" | custom-call | tf_op jit(solution)/shard_map/compact/pallas_call | solution.py:121
  37.2 4.9 %all-to-all-start.1 = ((f32[8,8,2048]{2,1,0:T(8,128)}), f32[8,8,2048]{2,1,0:T(8,128)S(1)}, u32[]{:S(2)}, u32[]{:S(2)}) async-start(f32[8,8,2048]{2,1,0:T(8,128)} %compact.1), calls=%async_computation.1 | async-start | bytes 1048576 | tf_op jit(solution)/shard_map/all_to_all | solution.py:476
  43.3 3.5 %collective-permute-start.3 = (f32[48,64]{1,0:T(8,128)S(1)}, f32[48,64]{1,0:T(8,128)S(1)}, u32[]{:S(2)}, u32[]{:S(2)}) collective-permute-start(f32[48,64]{1,0:T(8,128)S(1)} %get-tuple-element.42), channel_id=1, source_target_pairs={{8,0},{16,8},{24,16},{32,24},{40,32},{48,40},{56,48},{64,56},{72,6... | collective-permute-start | bytes 36872 | tf_op jit(solution)/shard_map/ppermute | solution.py:471
  46.8 2.4 %collective-permute-start.2 = (f32[48,64]{1,0:T(8,128)S(1)}, f32[48,64]{1,0:T(8,128)S(1)}, u32[]{:S(2)}, u32[]{:S(2)}) collective-permute-start(f32[48,64]{1,0:T(8,128)S(1)} %get-tuple-element.43), channel_id=1, source_target_pairs={{0,8},{8,16},{16,24},{24,32},{32,40},{40,48},{48,56},{56,64},{64,7... | collective-permute-start | bytes 36872 | tf_op jit(solution)/shard_map/ppermute | solution.py:471
  49.2 1.9 %collective-permute-start.1 = (f32[48,64]{1,0:T(8,128)S(1)}, f32[48,64]{1,0:T(8,128)S(1)}, u32[]{:S(2)}, u32[]{:S(2)}) collective-permute-start(f32[48,64]{1,0:T(8,128)S(1)} %get-tuple-element.44), channel_id=1, source_target_pairs={{1,0},{2,1},{3,2},{4,3},{5,4},{6,5},{7,6},{9,8},{10,9},{11,10},{12... | collective-permute-start | bytes 36872 | tf_op jit(solution)/shard_map/ppermute | solution.py:471
  51.1 2.4 %collective-permute-start = (f32[48,64]{1,0:T(8,128)S(1)}, f32[48,64]{1,0:T(8,128)S(1)}, u32[]{:S(2)}, u32[]{:S(2)}) collective-permute-start(f32[48,64]{1,0:T(8,128)S(1)} %get-tuple-element.45), channel_id=1, source_target_pairs={{0,1},{1,2},{2,3},{3,4},{4,5},{5,6},{6,7},{8,9},{9,10},{10,11},{11... | collective-permute-start | bytes 36872 | tf_op jit(solution)/shard_map/ppermute | solution.py:471
  53.6 1.9 %setup_matrix.1 = (f32[136,136]{1,0:T(8,128)S(1)}, f32[136,136]{1,0:T(8,128)S(1)}, f32[6,136,48]{2,1,0:T(8,128)S(1)}, f32[136,128]{1,0:T(8,128)S(1)}, f32[136,128]{1,0:T(8,128)S(1)}) custom-call(f32[135,135]{1,0:T(8,128)S(1)} %copy-done.4, f32[135,135]{1,0:T(8,128)S(1)} %copy-done.5, f32[135,270]{1,0:T(8,128)S(1)} %copy-done.1, ...), custom_call_target="tpu_custom_call" | custom-call | tf_op jit(solution)/shard_map/setup_matrix/pallas_call | solution.py:121
  55.6 0.7 collective-permute-done.q0
  56.3 9.4 %radial.1 = (f32[3,27,128]{2,1,0:T(8,128)S(1)}, f32[136,128]{1,0:T(8,128)S(1)}, f32[136,128]{1,0:T(8,128)S(1)}, f32[6,48,128]{2,1,0:T(8,128)S(1)}, f32[2,48,128]{2,1,0:T(8,128)S(1)}) custom-call(f32[8,8,2048]{2,1,0:T(8,128)S(1)} %all-to-all-done.1.z_ref, f32[3,27,128]{2,1,0:T(8,128)S(1)} %copy-done.8, f32[96,32]{1,0:T(8,128)S(1)} %copy-done.9, ...), custom_call_target="tpu_custom_call" | custom-call | tf_op jit(solution)/shard_map/radial/pallas_call | solution.py:121
  65.8 5.6 %collective-permute-start.7 = (f32[48,64]{1,0:T(8,128)S(1)}, f32[48,64]{1,0:T(8,128)S(1)}, u32[]{:S(2)}, u32[]{:S(2)}) collective-permute-start(f32[48,64]{1,0:T(8,128)S(1)} %get-tuple-element.38), channel_id=1, source_target_pairs={{8,0},{16,8},{24,16},{32,24},{40,32},{48,40},{56,48},{64,56},{72,6... | collective-permute-start | bytes 36872 | tf_op jit(solution)/shard_map/ppermute | solution.py:471
  71.4 1.9 %collective-permute-start.6 = (f32[48,64]{1,0:T(8,128)S(1)}, f32[48,64]{1,0:T(8,128)S(1)}, u32[]{:S(2)}, u32[]{:S(2)}) collective-permute-start(f32[48,64]{1,0:T(8,128)S(1)} %get-tuple-element.39), channel_id=1, source_target_pairs={{0,8},{8,16},{16,24},{24,32},{32,40},{40,48},{48,56},{56,64},{64,7... | collective-permute-start | bytes 36872 | tf_op jit(solution)/shard_map/ppermute | solution.py:471
  73.3 3.5 %collective-permute-start.5 = (f32[48,64]{1,0:T(8,128)S(1)}, f32[48,64]{1,0:T(8,128)S(1)}, u32[]{:S(2)}, u32[]{:S(2)}) collective-permute-start(f32[48,64]{1,0:T(8,128)S(1)} %get-tuple-element.40), channel_id=1, source_target_pairs={{1,0},{2,1},{3,2},{4,3},{5,4},{6,5},{7,6},{9,8},{10,9},{11,10},{12... | collective-permute-start | bytes 36872 | tf_op jit(solution)/shard_map/ppermute | solution.py:471
  76.8 1.9 %collective-permute-start.4 = (f32[48,64]{1,0:T(8,128)S(1)}, f32[48,64]{1,0:T(8,128)S(1)}, u32[]{:S(2)}, u32[]{:S(2)}) collective-permute-start(f32[48,64]{1,0:T(8,128)S(1)} %get-tuple-element.41), channel_id=1, source_target_pairs={{0,1},{1,2},{2,3},{3,4},{4,5},{5,6},{6,7},{8,9},{9,10},{10,11},{11... | collective-permute-start | bytes 36872 | tf_op jit(solution)/shard_map/ppermute | solution.py:471
  78.7 0.7 local.2.base_ref
  79.5 2.4 %collective-permute-done.4.q0 = f32[48,64]{1,0:T(8,128)S(1)} collective-permute-done((f32[48,64]{1,0:T(8,128)S(1)}, f32[48,64]{1,0:T(8,128)S(1)}, u32[]{:S(2)}, u32[]{:S(2)}) %collective-permute-start.4) | collective-permute-done | bytes 12320 | tf_op jit(solution)/shard_map/ppermute | solution.py:471
  81.9 1.1 %sweep.1 = (f32[136,128]{1,0:T(8,128)S(1)}, f32[6,48,128]{2,1,0:T(8,128)S(1)}, f32[2,48,128]{2,1,0:T(8,128)S(1)}) custom-call(f32[136,128]{1,0:T(8,128)S(1)} %local.2.base_ref, s32[1]{0:T(128)S(6)} %copy.20.count_ref, bf16[288,136]{1,0:T(8,128)(2,1)S(1)} %copy-done, s32[2,128]{1,0:T(2,128)S(1)} %reshape.7.send_ref, ...), custom_call_target="tpu_custom_call" | custom-call | tf_op jit(solution)/shard_map/sweep/pallas_call | solution.py:121
  83.1 5.8 %collective-permute-start.11 = (f32[48,64]{1,0:T(8,128)S(1)}, f32[48,64]{1,0:T(8,128)S(1)}, u32[]{:S(2)}, u32[]{:S(2)}) collective-permute-start(f32[48,64]{1,0:T(8,128)S(1)} %get-tuple-element.34), channel_id=1, source_target_pairs={{8,0},{16,8},{24,16},{32,24},{40,32},{48,40},{56,48},{64,56},{72,6... | collective-permute-start | bytes 36872 | tf_op jit(solution)/shard_map/ppermute | solution.py:471
  88.9 1.9 %collective-permute-start.10 = (f32[48,64]{1,0:T(8,128)S(1)}, f32[48,64]{1,0:T(8,128)S(1)}, u32[]{:S(2)}, u32[]{:S(2)}) collective-permute-start(f32[48,64]{1,0:T(8,128)S(1)} %get-tuple-element.35), channel_id=1, source_target_pairs={{0,8},{8,16},{16,24},{24,32},{32,40},{40,48},{48,56},{56,64},{64,7... | collective-permute-start | bytes 36872 | tf_op jit(solution)/shard_map/ppermute | solution.py:471
  90.8 1.9 %collective-permute-start.9 = (f32[48,64]{1,0:T(8,128)S(1)}, f32[48,64]{1,0:T(8,128)S(1)}, u32[]{:S(2)}, u32[]{:S(2)}) collective-permute-start(f32[48,64]{1,0:T(8,128)S(1)} %get-tuple-element.36), channel_id=1, source_target_pairs={{1,0},{2,1},{3,2},{4,3},{5,4},{6,5},{7,6},{9,8},{10,9},{11,10},{12... | collective-permute-start | bytes 36872 | tf_op jit(solution)/shard_map/ppermute | solution.py:471
  92.7 2.4 %collective-permute-start.8 = (f32[48,64]{1,0:T(8,128)S(1)}, f32[48,64]{1,0:T(8,128)S(1)}, u32[]{:S(2)}, u32[]{:S(2)}) collective-permute-start(f32[48,64]{1,0:T(8,128)S(1)} %get-tuple-element.37), channel_id=1, source_target_pairs={{0,1},{1,2},{2,3},{3,4},{4,5},{5,6},{6,7},{8,9},{9,10},{10,11},{11... | collective-permute-start | bytes 36872 | tf_op jit(solution)/shard_map/ppermute | solution.py:471
  95.8 0.7 local.3.base_ref
  96.7 1.2 %collective-permute-done.8.q0 = f32[48,64]{1,0:T(8,128)S(1)} collective-permute-done((f32[48,64]{1,0:T(8,128)S(1)}, f32[48,64]{1,0:T(8,128)S(1)}, u32[]{:S(2)}, u32[]{:S(2)}) %collective-permute-start.8) | collective-permute-done | bytes 12320 | tf_op jit(solution)/shard_map/ppermute | solution.py:471
  97.9 1.3 %last.1 = f32[5,27,128]{2,1,0:T(8,128)} custom-call(f32[136,128]{1,0:T(8,128)S(1)} %local.3.base_ref, s32[1]{0:T(128)S(6)} %copy.20.count_ref, f32[6,136,48]{2,1,0:T(8,128)S(1)} %get-tuple-element.22.m_ref, s32[6,128]{1,0:T(8,128)S(1)} %copy-done.3, f32[48,64]{1,0:T(8,128)S(1)} %collective-permute-done.8.q0, f32[48,64]{1,0:T(8,128)S(1)} %collective-permute-done.9.q1, ...), custom_call_target="tpu_custom_call" | custom-call | tf_op jit(solution)/shard_map/last/pallas_call | solution.py:121
  (45 shorter events, 3.1 us)
Async XLA Ops:
  37.1 5.6 %copy-start.13 = (s32[1,4,64]{2,1,0:T(4,128)S(1)}, s32[1,4,64]{2,1,0:T(4,128)}, u32[]{:S(2)}) copy-start(s32[1,4,64]{2,1,0:T(4,128)} %param.24) | copy-start | bytes 3076
  37.1 5.7 %copy-start = (bf16[288,136]{1,0:T(8,128)(2,1)S(1)}, bf16[288,136]{1,0:T(8,128)(2,1)}, u32[]{:S(2)}) copy-start(bf16[288,136]{1,0:T(8,128)(2,1)} %constant.10.clone.select_ref) | copy-start | bytes 235012
  37.1 5.7 %copy-start.6 = (f32[5,27,128]{2,1,0:T(8,128)S(1)}, f32[5,27,128]{2,1,0:T(8,128)}, u32[]{:S(2)}) copy-start(f32[5,27,128]{2,1,0:T(8,128)} %u_ref.1) | copy-start | bytes 207364
  37.1 16.4 %copy-start.4 = (f32[135,135]{1,0:T(8,128)S(1)}, f32[135,135]{1,0:T(8,128)}, u32[]{:S(2)}) copy-start(f32[135,135]{1,0:T(8,128)} %vol_ref.1) | copy-start | bytes 218704
  37.1 16.4 %copy-start.5 = (f32[135,135]{1,0:T(8,128)S(1)}, f32[135,135]{1,0:T(8,128)}, u32[]{:S(2)}) copy-start(f32[135,135]{1,0:T(8,128)} %inv_ref.1) | copy-start | bytes 218704
  37.1 16.4 %copy-start.7 = (f32[5,27,128]{2,1,0:T(8,128)S(1)}, f32[5,27,128]{2,1,0:T(8,128)}, u32[]{:S(2)}) copy-start(f32[5,27,128]{2,1,0:T(8,128)} %right_ref.1) | copy-start | bytes 207364
  37.2 19.1 %all-to-all-start.1 = ((f32[8,8,2048]{2,1,0:T(8,128)}), f32[8,8,2048]{2,1,0:T(8,128)S(1)}, u32[]{:S(2)}, u32[]{:S(2)}) async-start(f32[8,8,2048]{2,1,0:T(8,128)} %compact.1), calls=%async_computation.1 | async-start | bytes 1048576 | tf_op jit(solution)/shard_map/all_to_all | solution.py:476
  42.8 10.7 %copy-start.1 = (f32[135,270]{1,0:T(8,128)S(1)}, f32[135,270]{1,0:T(8,128)}, u32[]{:S(2)}) copy-start(f32[135,270]{1,0:T(8,128)} %lift_ref.1) | copy-start | bytes 437404
  42.8 10.8 %copy-start.2 = (bf16[270,288]{1,0:T(8,128)(2,1)S(1)}, bf16[270,288]{1,0:T(8,128)(2,1)}, u32[]{:S(2)}) copy-start(bf16[270,288]{1,0:T(8,128)(2,1)} %constant.11.clone.place_ref) | copy-start | bytes 466564
  43.3 12.2 %collective-permute-start.3 = (f32[48,64]{1,0:T(8,128)S(1)}, f32[48,64]{1,0:T(8,128)S(1)}, u32[]{:S(2)}, u32[]{:S(2)}) collective-permute-start(f32[48,64]{1,0:T(8,128)S(1)} %get-tuple-element.42), channel_id=1, source_target_pairs={{8,0},{16,8},{24,16},{32,24},{40,32},{48,40},{56,48},{64,56},{72,6... | collective-permute-start | bytes 36872 | tf_op jit(solution)/shard_map/ppermute | solution.py:471
  46.8 6.8 %copy-start.3 = (s32[6,128]{1,0:T(8,128)S(1)}, s32[6,128]{1,0:T(8,128)}, u32[]{:S(2)}) copy-start(s32[6,128]{1,0:T(8,128)} %where_ref.11) | copy-start | bytes 9220
  46.8 8.7 %collective-permute-start.2 = (f32[48,64]{1,0:T(8,128)S(1)}, f32[48,64]{1,0:T(8,128)S(1)}, u32[]{:S(2)}, u32[]{:S(2)}) collective-permute-start(f32[48,64]{1,0:T(8,128)S(1)} %get-tuple-element.43), channel_id=1, source_target_pairs={{0,8},{8,16},{16,24},{24,32},{32,40},{40,48},{48,56},{56,64},{64,7... | collective-permute-start | bytes 36872 | tf_op jit(solution)/shard_map/ppermute | solution.py:471
  49.2 6.3 %collective-permute-start.1 = (f32[48,64]{1,0:T(8,128)S(1)}, f32[48,64]{1,0:T(8,128)S(1)}, u32[]{:S(2)}, u32[]{:S(2)}) collective-permute-start(f32[48,64]{1,0:T(8,128)S(1)} %get-tuple-element.44), channel_id=1, source_target_pairs={{1,0},{2,1},{3,2},{4,3},{5,4},{6,5},{7,6},{9,8},{10,9},{11,10},{12... | collective-permute-start | bytes 36872 | tf_op jit(solution)/shard_map/ppermute | solution.py:471
  51.1 5.1 %collective-permute-start = (f32[48,64]{1,0:T(8,128)S(1)}, f32[48,64]{1,0:T(8,128)S(1)}, u32[]{:S(2)}, u32[]{:S(2)}) collective-permute-start(f32[48,64]{1,0:T(8,128)S(1)} %get-tuple-element.45), channel_id=1, source_target_pairs={{0,1},{1,2},{2,3},{3,4},{4,5},{5,6},{6,7},{8,9},{9,10},{10,11},{11... | collective-permute-start | bytes 36872 | tf_op jit(solution)/shard_map/ppermute | solution.py:471
  53.6 2.7 %copy-start.8 = (f32[3,27,128]{2,1,0:T(8,128)S(1)}, f32[3,27,128]{2,1,0:T(8,128)}, u32[]{:S(2)}) copy-start(f32[3,27,128]{2,1,0:T(8,128)} %node_ref.1) | copy-start | bytes 124420
  53.6 2.7 %copy-start.9 = (f32[96,32]{1,0:T(8,128)S(1)}, f32[96,32]{1,0:T(8,128)}, u32[]{:S(2)}) copy-start(f32[96,32]{1,0:T(8,128)} %constant.8.clone.derivs_ref) | copy-start | bytes 36868
  65.8 13.6 %collective-permute-start.7 = (f32[48,64]{1,0:T(8,128)S(1)}, f32[48,64]{1,0:T(8,128)S(1)}, u32[]{:S(2)}, u32[]{:S(2)}) collective-permute-start(f32[48,64]{1,0:T(8,128)S(1)} %get-tuple-element.38), channel_id=1, source_target_pairs={{8,0},{16,8},{24,16},{32,24},{40,32},{48,40},{56,48},{64,56},{72,6... | collective-permute-start | bytes 36872 | tf_op jit(solution)/shard_map/ppermute | solution.py:471
  71.4 8.1 %collective-permute-start.6 = (f32[48,64]{1,0:T(8,128)S(1)}, f32[48,64]{1,0:T(8,128)S(1)}, u32[]{:S(2)}, u32[]{:S(2)}) collective-permute-start(f32[48,64]{1,0:T(8,128)S(1)} %get-tuple-element.39), channel_id=1, source_target_pairs={{0,8},{8,16},{16,24},{24,32},{32,40},{40,48},{48,56},{56,64},{64,7... | collective-permute-start | bytes 36872 | tf_op jit(solution)/shard_map/ppermute | solution.py:471
  73.3 6.2 %collective-permute-start.5 = (f32[48,64]{1,0:T(8,128)S(1)}, f32[48,64]{1,0:T(8,128)S(1)}, u32[]{:S(2)}, u32[]{:S(2)}) collective-permute-start(f32[48,64]{1,0:T(8,128)S(1)} %get-tuple-element.40), channel_id=1, source_target_pairs={{1,0},{2,1},{3,2},{4,3},{5,4},{6,5},{7,6},{9,8},{10,9},{11,10},{12... | collective-permute-start | bytes 36872 | tf_op jit(solution)/shard_map/ppermute | solution.py:471
  76.8 5.1 %collective-permute-start.4 = (f32[48,64]{1,0:T(8,128)S(1)}, f32[48,64]{1,0:T(8,128)S(1)}, u32[]{:S(2)}, u32[]{:S(2)}) collective-permute-start(f32[48,64]{1,0:T(8,128)S(1)} %get-tuple-element.41), channel_id=1, source_target_pairs={{0,1},{1,2},{2,3},{3,4},{4,5},{5,6},{6,7},{8,9},{9,10},{10,11},{11... | collective-permute-start | bytes 36872 | tf_op jit(solution)/shard_map/ppermute | solution.py:471
  83.1 13.4 %collective-permute-start.11 = (f32[48,64]{1,0:T(8,128)S(1)}, f32[48,64]{1,0:T(8,128)S(1)}, u32[]{:S(2)}, u32[]{:S(2)}) collective-permute-start(f32[48,64]{1,0:T(8,128)S(1)} %get-tuple-element.34), channel_id=1, source_target_pairs={{8,0},{16,8},{24,16},{32,24},{40,32},{48,40},{56,48},{64,56},{72,6... | collective-permute-start | bytes 36872 | tf_op jit(solution)/shard_map/ppermute | solution.py:471
  88.9 7.8 %collective-permute-start.10 = (f32[48,64]{1,0:T(8,128)S(1)}, f32[48,64]{1,0:T(8,128)S(1)}, u32[]{:S(2)}, u32[]{:S(2)}) collective-permute-start(f32[48,64]{1,0:T(8,128)S(1)} %get-tuple-element.35), channel_id=1, source_target_pairs={{0,8},{8,16},{16,24},{24,32},{32,40},{40,48},{48,56},{56,64},{64,7... | collective-permute-start | bytes 36872 | tf_op jit(solution)/shard_map/ppermute | solution.py:471
  90.8 5.9 %collective-permute-start.9 = (f32[48,64]{1,0:T(8,128)S(1)}, f32[48,64]{1,0:T(8,128)S(1)}, u32[]{:S(2)}, u32[]{:S(2)}) collective-permute-start(f32[48,64]{1,0:T(8,128)S(1)} %get-tuple-element.36), channel_id=1, source_target_pairs={{1,0},{2,1},{3,2},{4,3},{5,4},{6,5},{7,6},{9,8},{10,9},{11,10},{12... | collective-permute-start | bytes 36872 | tf_op jit(solution)/shard_map/ppermute | solution.py:471
  92.7 5.1 %collective-permute-start.8 = (f32[48,64]{1,0:T(8,128)S(1)}, f32[48,64]{1,0:T(8,128)S(1)}, u32[]{:S(2)}, u32[]{:S(2)}) collective-permute-start(f32[48,64]{1,0:T(8,128)S(1)} %get-tuple-element.37), channel_id=1, source_target_pairs={{0,1},{1,2},{2,3},{3,4},{4,5},{5,6},{6,7},{8,9},{9,10},{10,11},{11... | collective-permute-start | bytes 36872 | tf_op jit(solution)/shard_map/ppermute | solution.py:471
  (3 other events, 4.0 us)

commit v2 on v1

--- a/solution.py
+++ b/solution.py
@@ -13,14 +13,14 @@
 RADIUS = 1.5
 FAR = 1000.0
 LANES = 128
-STRIP = 512
+STRIP = 768
 RUN = 768
+PACKET = 384
 TILES = 16
 SLOTS = 8
 INTERPRET = False
 F32, BF16, I32 = jnp.float32, jnp.bfloat16, jnp.int32
 VMEM = pltpu.MemorySpace.VMEM
-SMEM = pltpu.MemorySpace.SMEM
 
 
 def node_tables():
@@ -61,10 +61,6 @@
 CORNERS = [2 * (c & 1) + 6 * (c >> 1 & 1) + 18 * (c >> 2) for c in range(8)]
 
 
-def hdot(a, b):
-    return jnp.dot(a, b, precision=lax.Precision.HIGHEST, preferred_element_type=F32)
-
-
 def pieces(x, count):
     out = []
     for _ in range(count):
@@ -101,15 +97,17 @@
     return jnp.where(mask, 1.0, 0.0).astype(dtype)
 
 
-def call(body, out_shape, in_spaces, scratch=(), held=True, **kw):
-    def place(s):
-        return pltpu.VMEM(s.shape, s.dtype) if held and not INTERPRET else s
+def call(body, out_shape, in_spaces, scratch=(), held=True, out_specs=None, **kw):
+    held = held if isinstance(held, list) else jax.tree.map(lambda _: held, out_shape)
+
+    def place(s, stays):
+        return pltpu.VMEM(s.shape, s.dtype) if stays and not INTERPRET else s
 
     run = pl.pallas_call(
         body,
-        out_shape=jax.tree.map(place, out_shape),
-        in_specs=[pl.BlockSpec(memory_space=s) for s in in_spaces],
-        out_specs=jax.tree.map(lambda _: pl.BlockSpec(memory_space=VMEM), out_shape),
+        out_shape=jax.tree.map(place, out_shape, held),
+        in_specs=[pl.BlockSpec(memory_space=VMEM) for _ in in_spaces],
+        out_specs=out_specs or jax.tree.map(lambda _: pl.BlockSpec(memory_space=VMEM), out_shape),
         scratch_shapes=list(scratch),
         interpret=INTERPRET,
         **kw,
@@ -118,7 +116,7 @@
     def placed(*args):
         if INTERPRET:
             return run(*args)
-        return run(*[pltpu.with_memory_space_constraint(a, s) for a, s in zip(args, in_spaces, strict=True)])
+        return run(*[a if s is None else pltpu.with_memory_space_constraint(a, s) for a, s in zip(args, in_spaces, strict=True)])
 
     return placed
 
@@ -127,21 +125,33 @@
     return jax.ShapeDtypeStruct(dims, dtype)
 
 
+STATE = [shape_of(136, LANES), shape_of(6, 48, LANES), *[shape_of(24, LANES)] * 4]
+
+
 def payload_body(count_ref, pos_ref, coef_ref, out_ref, row_ref):
-    count = count_ref[0]
+    count = jnp.broadcast_to(count_ref[...], (1, LANES))[:, 0:32]
     live = iota((1, 32), 1) < count
     for axis in range(3):
         lanes = slice(32 * axis, 32 * axis + 32)
         row_ref[0:1, lanes] = jnp.where(live, pos_ref[axis : axis + 1, :], FAR)
         row_ref[1:2, lanes] = jnp.where(live, coef_ref[axis : axis + 1, :], 0.0)
     row_ref[0:1, 96:128] = jnp.zeros((1, 32), F32)
-    row_ref[1:2, 96:128] = jnp.full((1, 32), count, I32).astype(F32)
+    row_ref[1:2, 96:128] = count.astype(F32)
     out_ref[...] = jnp.broadcast_to(row_ref[0:2, :][None], out_ref.shape)
 
 
-def compact_body(in_ref, out_ref, part_ref):
+def compact_body(in_ref, p0, p1, out_ref, part_ref):
     owners = in_ref.shape[0]
     copies, _, room = out_ref.shape
+    room = room - PACKET
+    me = lax.axis_index("sub")
+    odd = me % 2 == 1
+    ahead, back = jnp.where(odd, p1[...], p0[...]), jnp.where(odd, p0[...], p1[...])
+    for peer in range(copies):
+        for at in range(3):
+            lanes = slice(room + LANES * at, room + LANES * at + LANES)
+            rows = slice(8 * at, 8 * at + 8)
+            out_ref[peer, :, lanes] = jnp.where(peer > me, ahead[rows], back[rows])
     first, second = in_ref[:, 0, :], in_ref[:, 1, :]
     wide = jnp.broadcast_to(second[:, 96:97], (owners, LANES))
     below = flag(iota((owners, owners), 1) < iota((owners, owners), 0), BF16)
@@ -154,10 +164,8 @@
     low, end = start_row[0:1, :], (start_row + count_row)[0:1, :]
     for at, piece in enumerate(pieces(first, 3)):
         part_ref[:, LANES * at : LANES * at + LANES] = piece
-    for at, piece in enumerate(pieces(second, 3)):
+    for at, piece in enumerate(pieces(second, 2) + pieces(start_col, 2)):
         part_ref[:, LANES * (3 + at) : LANES * (4 + at)] = piece
-    for at, piece in enumerate(pieces(start_col, 2)):
-        part_ref[:, LANES * (6 + at) : LANES * (7 + at)] = piece
     feature, group = iota((8, LANES), 0), iota((8, LANES), 1) // 32
     fold_first = flag((feature < 3) & (feature == group), BF16)
     fold_second = flag((feature > 3) & (feature < 7) & (feature == group + 4), BF16)
@@ -165,25 +173,28 @@
     slot = (iota((strip, LANES), 1) % 32).astype(F32)
 
     def one_strip(at, carry):
-        place = (iota((strip, owners), 0) + at * strip).astype(F32)
+        base = jnp.minimum(at * strip, room - strip)
+        place = (iota((strip, owners), 0) + base).astype(F32)
         owner = flag((place >= low) & (place < end), BF16)
         found = jnp.dot(owner, part_ref[...], preferred_element_type=F32)
-        start = found[:, 6 * LANES : 7 * LANES] + found[:, 7 * LANES :]
-        here = (iota((strip, LANES), 0) + at * strip).astype(F32)
+        start = found[:, 5 * LANES : 6 * LANES] + found[:, 6 * LANES :]
+        here = (iota((strip, LANES), 0) + base).astype(F32)
         mine = slot == here - start
         out = None
         for k in range(3):
             a = jnp.where(mine, found[:, LANES * k : LANES * k + LANES], 0.0).astype(BF16)
-            b = jnp.where(mine, found[:, LANES * (3 + k) : LANES * (4 + k)], 0.0).astype(BF16)
-            both = nt_dot(fold_first, a) + nt_dot(fold_second, b)
+            both = nt_dot(fold_first, a)
+            if k < 2:
+                b = jnp.where(mine, found[:, LANES * (3 + k) : LANES * (4 + k)], 0.0).astype(BF16)
+                both = both + nt_dot(fold_second, b)
             out = both if out is None else out + both
-        dead = iota((8, strip), 1) + at * strip >= total
+        dead = iota((8, strip), 1) + base >= total
         row = iota((8, strip), 0)
         out = jnp.where(dead, jnp.where(row < 3, FAR, 0.0), out)
         square = jnp.sum(jnp.where(row < 3, out * out, 0.0), axis=0, keepdims=True)
         out = jnp.where(row == 3, square, out)
         out = jnp.where(row == 7, total.astype(F32), out)
-        out_ref[:, :, pl.ds(pl.multiple_of(at * strip, LANES), strip)] = jnp.broadcast_to(
+        out_ref[:, :, pl.ds(pl.multiple_of(base, LANES), strip)] = jnp.broadcast_to(
             out[None], (copies, 8, strip)
         )
         return carry
@@ -193,6 +204,7 @@
 
 def radial_displacement(z_ref, node_ref, corner_ref, hit_ref, rank_ref, list_ref, sum_ref, over_ref, over_smem, sem):
     groups, _, room = z_ref.shape
+    room = room - PACKET
     run = min(RUN, room)
     blocks = run // LANES
     at = [[node_ref[i, k : k + 1, :] for k in CORNERS] for i in range(3)]
@@ -205,12 +217,13 @@
             gap = (at[i][c] - middle[i]) ** 2
             reach[c] = gap if i == 0 else reach[c] + gap
     limit = RADIUS + jnp.sqrt(functools.reduce(jnp.maximum, reach))
-    offset = middle[0] ** 2 + middle[1] ** 2 + middle[2] ** 2 - limit * limit - 0.02
+    offset = middle[0] ** 2 + middle[1] ** 2 + middle[2] ** 2 - limit * limit * 1.001 - 0.2
     row = iota((LANES, LANES), 0)
-    table = jnp.where(row == 3, 1.0, 0.0)
+    table = jnp.where((row == 3) | (row == 11), 1.0, 0.0)
     for i in range(3):
-        table = jnp.where(row == i, -2.0 * middle[i], table)
-    probe = jnp.transpose(table)[:, 0:8]
+        high, low = (p.astype(F32) for p in pieces(-2.0 * middle[i], 2))
+        table = jnp.where((row == i) | (row == 8 + i), high, jnp.where(row == 16 + i, low, table))
+    probe = jnp.transpose(table)[:, 0:24].astype(BF16)
     offset = jnp.transpose(jnp.broadcast_to(offset, (LANES, LANES)))
     offset = jnp.concatenate([offset] * blocks, axis=1)
     pick = iota((8, LANES), 0) * TILES + iota((8, LANES), 1) % TILES
@@ -248,7 +261,9 @@
         start = jnp.minimum(first, room - run)
         for g in range(groups):
             points = z_ref[g, :, pl.ds(pl.multiple_of(start, LANES), run)]
-            gap = hdot(probe, points) + offset
+            high, low = pieces(points, 2)
+            both = jnp.concatenate([high.astype(F32), low.astype(F32), high.astype(F32)], axis=0)
+            gap = jnp.dot(probe, both.astype(BF16), preferred_element_type=F32) + offset
             best = gap[0:TILES]
             for e in range(1, 8):
                 best = jnp.minimum(best, gap[TILES * e : TILES * e + TILES])
@@ -273,9 +288,6 @@
                 length = length + jnp.where(inside > LANES * b, 1, 0)
                 list_ref[length] = two
                 length = length + jnp.where(inside > LANES * b + 64, 1, 0)
-        copy.wait()
-        crowded = jnp.max(filled) > SLOTS
-
         def more(length):
             def block_more(index, length):
                 g, b = index // blocks, index % blocks
@@ -292,10 +304,6 @@
                 return lax.fori_loop(1, rounds, round_more, length)
 
             return lax.fori_loop(0, groups * blocks, block_more, length)
-
-        length = lax.cond(crowded, more, lambda n: n, length)
-        for e in range(4):
-            list_ref[length + e] = jnp.zeros((8, LANES), F32)
 
         def four(step, carry):
             for i in range(2):
@@ -316,7 +324,18 @@
                         sum_ref[axis, c : c + 8, :] = total[axis]
             return carry
 
-        lax.fori_loop(0, (length + 3) // 4, four, 0)
+        def evaluate(length):
+            for e in range(4):
+                list_ref[length + e] = jnp.zeros((8, LANES), F32)
+            lax.fori_loop(0, (length + 3) // 4, four, 0)
+
+        evaluate(length)
+        copy.wait()
+
+        @pl.when(jnp.max(filled) > SLOTS)
+        def crowded():
+            evaluate(more(jnp.int32(0)))
+
         return carry
 
     lax.fori_loop(0, (most + (run - 1)) // run, one_part, 0)
@@ -325,7 +344,7 @@
     out = []
     for i in range(3):
         total = None
-        for piece in pieces(sum_ref[i], 3):
+        for piece in pieces(sum_ref[i], 2):
             part = jnp.dot(piece, spread, preferred_element_type=F32)
             total = part if total is None else total + part
         rows = [
@@ -337,20 +356,29 @@
 
 def radial_body(
     z_ref, node_ref, derivs_ref, blend_ref, base_ref, start_ref, minus_inv_ref, count_ref, select_ref, send_ref,
-    m_ref, where_ref, q0, q1, q2, q3,
-    disp_ref, metric_ref, state_ref, trace_ref, packet_ref,
-    corner_ref, hit_ref, rank_ref, list_ref, sum_ref, over_ref, over_smem, sem, nodes_ref, remote_ref,
+    m_ref, where_ref, elem_0, elem_1,
+    disp_ref, metric_ref, state_ref, trace_ref, p0, p1, p2, p3,
+    corner_ref, hit_ref, rank_ref, list_ref, sum_ref, over_ref, over_smem, sem, nodes_ref, shift_ref, out_sem,
 ):
-    base = base_ref[...] + from_neighbours(q0, q1, q2, q3, where_ref, m_ref, remote_ref)
+    packet_refs = (p0, p1, p2, p3)
+    me, last = lax.axis_index("sub"), z_ref.shape[0] - 1
+    sides = []
+    for step in (-1, 1):
+        peer, there = jnp.clip(me + step, 0, last), (me + step >= 0) & (me + step <= last)
+        rows = [z_ref[peer, :, z_ref.shape[2] - PACKET + LANES * at :][:, 0:LANES] for at in range(3)]
+        sides.append(jnp.where(there, jnp.concatenate(rows, axis=0), 0.0))
+    base = base_ref[...] + from_neighbours(*sides, *in_line("elem", elem_0[...], elem_1[...]), where_ref, m_ref)
     corner = radial_displacement(
         z_ref, node_ref, corner_ref, hit_ref, rank_ref, list_ref, sum_ref, over_ref, over_smem, sem
     )
     nodes_ref[...] = jnp.zeros_like(nodes_ref)
     for i in range(3):
-        shift = hdot(blend_ref[...], corner[i])
-        disp_ref[i] = shift[0:27]
+        shift = pick_dot(blend_ref[...], corner[i], 2)
+        shift_ref[i] = shift[0:27]
         nodes_ref[0:27, LANES * i : LANES * i + LANES] = node_ref[i] + shift[0:27]
-    jac = hdot(derivs_ref[...], nodes_ref[...])
+    out = pltpu.make_async_copy(shift_ref, disp_ref, out_sem)
+    out.start()
+    jac = pick_dot(derivs_ref[...], nodes_ref[...], 3)
     j = [[jac[32 * l : 32 * l + 32, LANES * i : LANES * i + LANES] for l in range(3)] for i in range(3)]
     minor_a = j[1][1] * j[2][2] - j[1][2] * j[2][1]
     minor_b = j[1][0] * j[2][2] - j[1][2] * j[2][0]
@@ -360,18 +388,26 @@
     for v in range(5):
         metric_ref[27 * v : 27 * v + 27, :] = metric[0:27]
     state = base + split_dot(minus_inv_ref[...], metric_ref[...] * start_ref[...])
-    finish(state, count_ref, select_ref, send_ref, state_ref, trace_ref, packet_ref)
-
-
-def finish(state, count_ref, select_ref, send_ref, state_ref, trace_ref, packet_ref):
-    state = jnp.where(iota(state.shape, 1) < count_ref[0], state, 0.0)
+    finish(state, count_ref, select_ref, send_ref, state_ref, trace_ref, packet_refs)
+    out.wait()
+
+
+def finish(state, count_ref, select_ref, send_ref, state_ref, trace_ref, packet_refs):
+    state = jnp.where(iota(state.shape, 1) < jnp.broadcast_to(count_ref[...], state.shape), state, 0.0)
     state_ref[...] = state
     traces = pick_dot(select_ref[...], state, 3)
     for f in range(6):
         trace_ref[f] = traces[48 * f : 48 * f + 48]
     tiles = [traces[48 * f : 48 * f + 48] for f in range(6)]
+    left = iota((24, LANES), 1) < 64
     for pair in range(2):
-        packet_ref[pair] = gather_columns(tiles, send_ref[pair : pair + 1, :], 0)
+        both = gather_columns(tiles, send_ref[pair : pair + 1, :], 0)
+        top, bottom = both[0:24], both[24:48]
+        ahead = jnp.where(left, top, pltpu.roll(bottom, 64, 1))
+        back = jnp.where(left, pltpu.roll(top, 64, 1), bottom)
+        odd = lax.axis_index(("sub", "elem")[pair]) % 2 == 1
+        packet_refs[2 * pair][...] = jnp.where(odd, back, ahead)
+        packet_refs[2 * pair + 1][...] = jnp.where(odd, ahead, back)
 
 
 def gather_columns(tiles, index, first):
@@ -384,23 +420,40 @@
     return out
 
 
-def from_neighbours(q0, q1, q2, q3, where_ref, m_ref, remote_ref):
-    for at, q in enumerate((q0, q1, q2, q3)):
-        remote_ref[at // 2, :, 64 * (at % 2) : 64 * (at % 2) + 64] = q[...]
-    tiles = [remote_ref[0], remote_ref[1]]
+def in_line(axis, first, second):
+    odd = lax.axis_index(axis) % 2 == 1
+    return jnp.where(odd, first, second), jnp.where(odd, second, first)
+
+
+def from_neighbours(before_sub, behind_sub, before_elem, behind_elem, where_ref, m_ref):
+    packets = (before_sub, behind_sub, before_elem, behind_elem)
     total = None
     for f in range(6):
-        found = gather_columns(tiles, where_ref[f : f + 1, :], 6)
-        part = split_dot(m_ref[f], found)
+        index = where_ref[f : f + 1, :] - 6 * LANES
+        packet = jnp.broadcast_to(jnp.where(index >= 0, index // 64, -1), (24, LANES))
+        lane = jnp.broadcast_to(index % 64, (24, LANES))
+        halves = []
+        for half in range(2):
+            found = jnp.zeros((24, LANES), F32)
+            for q, values in enumerate(packets):
+                found = jnp.where(packet == q, jnp.take_along_axis(values, lane + 64 * half, axis=1), found)
+            halves.append(found)
+        part = split_dot(m_ref[f], jnp.concatenate(halves, axis=0))
         total = part if total is None else total + part
     return total
 
 
-def setup_state_body(u_ref, count_ref, select_ref, send_ref, state_ref, trace_ref, packet_ref, flat_ref):
+def arrived(sub_0, sub_1, elem_0, elem_1, where_ref, m_ref):
+    sub = in_line("sub", sub_0[...], sub_1[...])
+    return from_neighbours(*sub, *in_line("elem", elem_0[...], elem_1[...]), where_ref, m_ref)
+
+
+def setup_state_body(u_ref, count_ref, select_ref, send_ref, state_ref, trace_ref, p0, p1, p2, p3, flat_ref):
+    packet_refs = (p0, p1, p2, p3)
     flat_ref[...] = jnp.zeros_like(flat_ref)
     for v in range(5):
         flat_ref[27 * v : 27 * v + 27, :] = u_ref[v]
-    finish(flat_ref[...], count_ref, select_ref, send_ref, state_ref, trace_ref, packet_ref)
+    finish(flat_ref[...], count_ref, select_ref, send_ref, state_ref, trace_ref, packet_refs)
 
 
 def setup_matrix_body(
@@ -412,9 +465,9 @@
     inverse = wide_ref[:, 0:136]
     minus_ref[...] = -inverse
     both_ref[...] = jnp.zeros_like(both_ref)
-    both_ref[0:135, 0:135] = -hdot(inv_ref[...], vol_ref[...])
+    both_ref[0:135, 0:135] = -split_dot(inv_ref[...], vol_ref[...])
     m_ref[...] = jnp.zeros_like(m_ref)
-    coupling = hdot(inv_ref[...], lift_ref[...])
+    coupling = split_dot(inv_ref[...], lift_ref[...])
     moved = None
     for piece in pieces(coupling, 3):
         part = jnp.dot(piece, place_ref[...], preferred_element_type=F32)
@@ -448,32 +501,64 @@
 
 
 def sweep_body(
-    base_ref, count_ref, select_ref, send_ref, m_ref, where_ref, q0, q1, q2, q3,
-    state_ref, trace_ref, packet_ref, remote_ref,
+    base_ref, count_ref, select_ref, send_ref, m_ref, where_ref, sub_0, sub_1, elem_0, elem_1,
+    state_ref, trace_ref, p0, p1, p2, p3,
 ):
-    state = base_ref[...] + from_neighbours(q0, q1, q2, q3, where_ref, m_ref, remote_ref)
-    finish(state, count_ref, select_ref, send_ref, state_ref, trace_ref, packet_ref)
-
-
-def last_body(base_ref, count_ref, m_ref, where_ref, q0, q1, q2, q3, out_ref, remote_ref, state_ref):
-    state = base_ref[...] + from_neighbours(q0, q1, q2, q3, where_ref, m_ref, remote_ref)
-    state_ref[...] = jnp.where(iota(state.shape, 1) < count_ref[0], state, 0.0)
+    packet_refs = (p0, p1, p2, p3)
+    state = base_ref[...] + arrived(sub_0, sub_1, elem_0, elem_1, where_ref, m_ref)
+    finish(state, count_ref, select_ref, send_ref, state_ref, trace_ref, packet_refs)
+
+
+def last_body(base_ref, count_ref, m_ref, where_ref, sub_0, sub_1, elem_0, elem_1, out_ref, state_ref):
+    state = base_ref[...] + arrived(sub_0, sub_1, elem_0, elem_1, where_ref, m_ref)
+    state_ref[...] = jnp.where(iota(state.shape, 1) < jnp.broadcast_to(count_ref[...], state.shape), state, 0.0)
     for v in range(5):
         out_ref[v] = state_ref[27 * v : 27 * v + 27, :]
 
 
-def exchange(packets):
+def exchange(packets, axes=("sub", "elem")):
     out = []
-    for q, (axis, step) in enumerate((("sub", 1), ("sub", -1), ("elem", 1), ("elem", -1))):
+    for axis in axes:
+        first = 0 if axis == "sub" else 2
         size = lax.axis_size(axis)
-        pairs = [(i, i + step) for i in range(size) if 0 <= i + step < size]
-        packet = packets[q // 2, :, 64 * (q % 2) : 64 * (q % 2) + 64]
-        out.append(lax.ppermute(packet, axis, pairs))
+        for turn in range(2):
+            partner = [(i ^ 1) if turn == 0 else ((i + 1) ^ 1) - 1 for i in range(size)]
+            pairs = [(i, j) for i, j in enumerate(partner) if 0 <= j < size]
+            out.append(lax.ppermute(packets[first + turn], axis, pairs))
     return out
 
 
 def spread(copies, axis):
     return lax.all_to_all(copies, axis, split_axis=0, concat_axis=0, tiled=True)
+
+
+def radial_call(points, node_ref, derivs, blending, base, state, minus, elem_count, select, send, coupling, face_link, received):
+    groups, _, room = points.shape
+    blocks = min(RUN, room - PACKET) // LANES * groups
+    return call(
+        radial_body,
+        [shape_of(3, 27, LANES), shape_of(136, LANES), *STATE],
+        [VMEM] * 7 + [None] + [VMEM] * 6,
+        [
+            pltpu.VMEM((3, 64, LANES), F32),
+            pltpu.VMEM((blocks * TILES, LANES), F32),
+            pltpu.VMEM((blocks * TILES, LANES), F32),
+            pltpu.VMEM((blocks * 16 + 8, 8, LANES), F32),
+            pltpu.VMEM((3, 64, LANES), F32),
+            pltpu.VMEM((blocks, LANES), I32),
+            pltpu.SMEM((blocks, LANES), I32),
+            pltpu.SemaphoreType.DMA,
+            pltpu.VMEM((32, 3 * LANES), F32),
+            pltpu.VMEM((3, 27, LANES), F32),
+            pltpu.SemaphoreType.DMA,
+        ],
+        held=[False] + [True] * 7,
+        out_specs=[pl.BlockSpec(memory_space=pl.ANY)] + [pl.BlockSpec(memory_space=VMEM)] * 7,
+        name="radial",
+    )(
+        points, node_ref, derivs, blending, base, state, minus, elem_count, select, send,
+        coupling, face_link, *received,
+    )
 
 
 def per_device(
@@ -481,21 +566,29 @@
     vol_block, block_inv, lift_matrix,
 ):
     derivs, blending, select, place = node_tables()
-    derivs, blending = jnp.asarray(derivs), jnp.asarray(blending)
+    derivs, blending = jnp.asarray(derivs, BF16), jnp.asarray(blending, BF16)
     select, place = jnp.asarray(select, BF16), jnp.asarray(place, BF16)
     n_elem, n_sub = lax.axis_size("elem"), lax.axis_size("sub")
     room = n_elem * cp_pos.shape[1]
     send = send_list.reshape(2, LANES)
-    state_shape = [shape_of(136, LANES), shape_of(6, 48, LANES), shape_of(2, 48, LANES)]
-
+
+    held_count = elem_count.reshape(1, 1)
     copies = call(
-        payload_body, shape_of(n_elem, 2, LANES), [SMEM, VMEM, VMEM], [pltpu.VMEM((8, LANES), F32)], name="payload"
-    )(cp_count, cp_pos, cp_coef)
+        payload_body, shape_of(n_elem, 2, LANES), [None] * 3, [pltpu.VMEM((8, LANES), F32)], name="payload"
+    )(cp_count.reshape(1, 1), cp_pos, cp_coef)
     mine = spread(copies, "elem")
-    state, traces, packets = call(
-        setup_state_body, state_shape, [VMEM, SMEM, VMEM, VMEM], [pltpu.VMEM((136, LANES), F32)], name="setup_state"
-    )(u_prev, elem_count, select, send)
-    received = exchange(packets)
+    state, traces, *packets = call(
+        setup_state_body, STATE, [VMEM, None, VMEM, VMEM], [pltpu.VMEM((136, LANES), F32)], name="setup_state"
+    )(u_prev, held_count, select, send)
+    gathered = call(
+        compact_body,
+        shape_of(n_sub, 8, room + PACKET),
+        [VMEM] * 3,
+        [pltpu.VMEM((n_elem, 7 * LANES), BF16)],
+        name="compact",
+    )(mine, packets[0], packets[1])
+    points = spread(gathered, "sub")
+    received = exchange(packets, ("elem",))
     minus, both, coupling, const, base = call(
         setup_matrix_body,
         [
@@ -506,51 +599,28 @@
         [pltpu.VMEM((136, LANES), F32), pltpu.VMEM((136, 256), F32)],
         name="setup_matrix",
     )(vol_block, block_inv, lift_matrix, place, right_side, state, traces, face_link)
-    gathered = call(
-        compact_body, shape_of(n_sub, 8, room), [VMEM], [pltpu.VMEM((n_elem, 8 * LANES), BF16)], name="compact"
-    )(mine)
-    points = spread(gathered, "sub")
-    blocks = min(RUN, room) // LANES * n_sub
-    displacement, metric, state, traces, packets = call(
-        radial_body,
-        [shape_of(3, 27, LANES), shape_of(136, LANES), *state_shape],
-        [VMEM] * 7 + [SMEM] + [VMEM] * 8,
-        [
-            pltpu.VMEM((3, 64, LANES), F32),
-            pltpu.VMEM((blocks * TILES, LANES), F32),
-            pltpu.VMEM((blocks * TILES, LANES), F32),
-            pltpu.VMEM((blocks * 16 + 8, 8, LANES), F32),
-            pltpu.VMEM((3, 64, LANES), F32),
-            pltpu.VMEM((blocks, LANES), I32),
-            pltpu.SMEM((blocks, LANES), I32),
-            pltpu.SemaphoreType.DMA,
-            pltpu.VMEM((32, 3 * LANES), F32),
-            pltpu.VMEM((2, 48, LANES), F32),
-        ],
-        name="radial",
-    )(
-        points, node_ref, derivs, blending, base, state, minus, elem_count, select, send,
-        coupling, face_link, *received,
+    displacement, metric, state, traces, *packets = radial_call(
+        points, node_ref, derivs, blending, base, state, minus, held_count, select, send,
+        coupling, face_link, received,
     )
     for sweep in range(1, ITERS):
         received = exchange(packets)
         base = call(local_body, shape_of(136, LANES), [VMEM] * 8, name="local")(
             state, traces, metric, const, minus, both, coupling, face_link
         )
-        scratch = [pltpu.VMEM((2, 48, LANES), F32)]
         if sweep < ITERS - 1:
-            state, traces, packets = call(
-                sweep_body, state_shape, [VMEM, SMEM] + [VMEM] * 8, scratch, name="sweep"
-            )(base, elem_count, select, send, coupling, face_link, *received)
+            state, traces, *packets = call(sweep_body, STATE, [VMEM, None] + [VMEM] * 8, name="sweep")(
+                base, held_count, select, send, coupling, face_link, *received
+            )
         else:
             solution_out = call(
                 last_body,
                 shape_of(5, 27, LANES),
-                [VMEM, SMEM] + [VMEM] * 6,
-                scratch + [pltpu.VMEM((136, LANES), F32)],
+                [VMEM, None] + [VMEM] * 6,
+                [pltpu.VMEM((136, LANES), F32)],
                 held=False,
                 name="last",
-            )(base, elem_count, coupling, face_link, *received)
+            )(base, held_count, coupling, face_link, *received)
     return displacement, solution_out
 
 

time: 99.9 us -> 94.1 us (0.942)
  the two profiles are of different devices: /device:TPU:14 before, /device:TPU:12 now
where the time goes in v2:
time: 94.1 us; the launch traced here: 93.5 us
  starting transfers between devices  49.7 us (53%)
  waiting for transfers between devices  22.1 us (23%)
  Pallas kernels  18.5 us (20%)
  between operations  2.25 us (2%)
  local copies, waits for them, and re-layouts  1.02 us (1%)
    ppermute x10, starting transfers between devices, exchange(): out.append(lax.ppermute(packets[first + turn], axis, pairs))  25.8 us
    all_to_all x2, starting transfers between devices, spread(): return lax.all_to_all(copies, axis, split_axis=0, concat_axis=0, tiled=True)  23.8 us
    pallas_call x9, Pallas kernels, placed(): run(*[a if s is None else pltpu.with_memory_space_constraint(a, s) for a,...  18.5 us
    all_to_all x2, waiting for transfers between devices, spread(): return lax.all_to_all(copies, axis, split_axis=0, concat_axis=0, tiled=True)  11.6 us
    ppermute x10, waiting for transfers between devices, exchange(): out.append(lax.ppermute(packets[first + turn], axis, pairs))  10.5 us
  transfers between devices with their start and end apart: 12, of which 5 were waited for; matrix products, arithmetic and copies ran while one was open for 0% of the time, Pallas kernels for 4%

profile of v2, /device:TPU:12, one launch (start us, length us, event | category | flops | bytes accessed | tf_op | source)
XLA Modules:
  0.0 93.5 jit_solution(18062848245521028467)
XLA Ops:
  1.3 1.5 %payload.1 = f32[64,2,128]{2,1,0:T(2,128)} custom-call(s32[1,1]{1,0:T(1,128)} %bitcast.2.count_ref, f32[3,32]{1,0:T(4,128)} %pos_ref.1, f32[3,32]{1,0:T(4,128)} %coef_ref.1), custom_call_target="tpu_custom_call" | custom-call | tf_op jit(solution)/shard_map/payload/pallas_call | solution.py:119
  2.8 18.9 %all-to-all-start = ((f32[64,2,128]{2,1,0:T(2,128)}), f32[64,2,128]{2,1,0:T(2,128)S(1)}, u32[]{:S(2)}, u32[]{:S(2)}) async-start(f32[64,2,128]{2,1,0:T(2,128)} %payload.1), calls=%async_computation | async-start | bytes 131072 | tf_op jit(solution)/shard_map/all_to_all | solution.py:532
  22.4 0.9 copy-done.6
  23.9 11.6 %all-to-all-done.in_ref = f32[64,2,128]{2,1,0:T(2,128)S(1)} async-done(((f32[64,2,128]{2,1,0:T(2,128)}), f32[64,2,128]{2,1,0:T(2,128)S(1)}, u32[]{:S(2)}, u32[]{:S(2)}) %all-to-all-start) | async-done | bytes 65568 | tf_op jit(solution)/shard_map/all_to_all | solution.py:532
  35.5 2.7 %compact.1 = f32[8,8,2432]{2,1,0:T(8,128)} custom-call(f32[64,2,128]{2,1,0:T(2,128)S(1)} %all-to-all-done.in_ref, f32[24,128]{1,0:T(8,128)S(1)} %get-tuple-element.27.p0, f32[24,128]{1,0:T(8,128)S(1)} %get-tuple-element.28.p1), custom_call_target="tpu_custom_call" | custom-call | tf_op jit(solution)/shard_map/compact/pallas_call | solution.py:119
  38.2 4.9 %all-to-all-start.1 = ((f32[8,8,2432]{2,1,0:T(8,128)}), f32[8,8,2432]{2,1,0:T(8,128)S(1)}, u32[]{:S(2)}, u32[]{:S(2)}) async-start(f32[8,8,2432]{2,1,0:T(8,128)} %compact.1), calls=%async_computation.1 | async-start | bytes 1245184 | tf_op jit(solution)/shard_map/all_to_all | solution.py:532
  43.2 2.8 %collective-permute-start = (f32[24,128]{1,0:T(8,128)S(1)}, f32[24,128]{1,0:T(8,128)S(1)}, u32[]{:S(2)}, u32[]{:S(2)}) collective-permute-start(f32[24,128]{1,0:T(8,128)S(1)} %get-tuple-element.34), channel_id=1, source_target_pairs={{0,8},{8,0},{16,24},{24,16},{32,40},{40,32},{48,56},{56,48},{64,72... | collective-permute-start | bytes 36872 | tf_op jit(solution)/shard_map/ppermute | solution.py:527
  45.9 3.5 %collective-permute-start.1 = (f32[24,128]{1,0:T(8,128)S(1)}, f32[24,128]{1,0:T(8,128)S(1)}, u32[]{:S(2)}, u32[]{:S(2)}) collective-permute-start(f32[24,128]{1,0:T(8,128)S(1)} %get-tuple-element.35), channel_id=1, source_target_pairs={{8,16},{16,8},{24,32},{32,24},{40,48},{48,40},{56,64},{64,56},{72,... | collective-permute-start | bytes 36872 | tf_op jit(solution)/shard_map/ppermute | solution.py:527
  49.5 1.7 %setup_matrix.1 = (f32[136,136]{1,0:T(8,128)S(1)}, f32[136,136]{1,0:T(8,128)S(1)}, f32[6,136,48]{2,1,0:T(8,128)S(1)}, f32[136,128]{1,0:T(8,128)S(1)}, f32[136,128]{1,0:T(8,128)S(1)}) custom-call(f32[135,135]{1,0:T(8,128)S(1)} %copy-done.4, f32[135,135]{1,0:T(8,128)S(1)} %copy-done.5, f32[135,270]{1,0:T(8,128)S(1)} %copy-done.1, ...), custom_call_target="tpu_custom_call" | custom-call | tf_op jit(solution)/shard_map/setup_matrix/pallas_call | solution.py:119
  51.2 2.4 %collective-permute-done.1.elem_1 = f32[24,128]{1,0:T(8,128)S(1)} collective-permute-done((f32[24,128]{1,0:T(8,128)S(1)}, f32[24,128]{1,0:T(8,128)S(1)}, u32[]{:S(2)}, u32[]{:S(2)}) %collective-permute-start.1) | collective-permute-done | bytes 12320 | tf_op jit(solution)/shard_map/ppermute | solution.py:527
  53.7 8.1 %radial.1 = (f32[3,27,128]{2,1,0:T(8,128)}, f32[136,128]{1,0:T(8,128)S(1)}, f32[136,128]{1,0:T(8,128)S(1)}, f32[6,48,128]{2,1,0:T(8,128)S(1)}, f32[24,128]{1,0:T...) custom-call(f32[8,8,2432]{2,1,0:T(8,128)S(1)} %all-to-all-done.1.z_ref, ...), custom_call_target="tpu_custom_call" | custom-call | tf_op jit(solution)/shard_map/radial/pallas_call | solution.py:119
  61.8 1.9 %collective-permute-start.2 = (f32[24,128]{1,0:T(8,128)S(1)}, f32[24,128]{1,0:T(8,128)S(1)}, u32[]{:S(2)}, u32[]{:S(2)}) collective-permute-start(f32[24,128]{1,0:T(8,128)S(1)} %get-tuple-element.42), channel_id=1, source_target_pairs={{0,1},{1,0},{2,3},{3,2},{4,5},{5,4},{6,7},{7,6},{8,9},{9,8},{10,11... | collective-permute-start | bytes 36872 | tf_op jit(solution)/shard_map/ppermute | solution.py:527
  63.7 2.6 %collective-permute-start.3 = (f32[24,128]{1,0:T(8,128)S(1)}, f32[24,128]{1,0:T(8,128)S(1)}, u32[]{:S(2)}, u32[]{:S(2)}) collective-permute-start(f32[24,128]{1,0:T(8,128)S(1)} %get-tuple-element.43), channel_id=1, source_target_pairs={{1,2},{2,1},{3,4},{4,3},{5,6},{6,5},{9,10},{10,9},{11,12},{12,11},... | collective-permute-start | bytes 36872 | tf_op jit(solution)/shard_map/ppermute | solution.py:527
  66.3 1.9 %collective-permute-start.4 = (f32[24,128]{1,0:T(8,128)S(1)}, f32[24,128]{1,0:T(8,128)S(1)}, u32[]{:S(2)}, u32[]{:S(2)}) collective-permute-start(f32[24,128]{1,0:T(8,128)S(1)} %get-tuple-element.44), channel_id=1, source_target_pairs={{0,8},{8,0},{16,24},{24,16},{32,40},{40,32},{48,56},{56,48},{64,72... | collective-permute-start | bytes 36872 | tf_op jit(solution)/shard_map/ppermute | solution.py:527
  68.2 2.2 %collective-permute-start.5 = (f32[24,128]{1,0:T(8,128)S(1)}, f32[24,128]{1,0:T(8,128)S(1)}, u32[]{:S(2)}, u32[]{:S(2)}) collective-permute-start(f32[24,128]{1,0:T(8,128)S(1)} %get-tuple-element.45), channel_id=1, source_target_pairs={{8,16},{16,8},{24,32},{32,24},{40,48},{48,40},{56,64},{64,56},{72,... | collective-permute-start | bytes 36872 | tf_op jit(solution)/shard_map/ppermute | solution.py:527
  70.5 0.7 local.2.base_ref
  71.9 4.0 %collective-permute-done.5.elem_1 = f32[24,128]{1,0:T(8,128)S(1)} collective-permute-done((f32[24,128]{1,0:T(8,128)S(1)}, f32[24,128]{1,0:T(8,128)S(1)}, u32[]{:S(2)}, u32[]{:S(2)}) %collective-permute-start.5) | collective-permute-done | bytes 12320 | tf_op jit(solution)/shard_map/ppermute | solution.py:527
  75.9 1.1 %sweep.1 = (f32[136,128]{1,0:T(8,128)S(1)}, f32[6,48,128]{2,1,0:T(8,128)S(1)}, f32[24,128]{1,0:T(8,128)S(1)}, f32[24,128]{1,0:T(8,128)S(1)}, f32[24,128]{1,0:T(8,128)S(1)}, /*index=5*/f32[24,128]{1,0:T(8,128)S(1)}) custom-call(f32[136,128]{1,0:T(8,128)S(1)} %local.2.base_ref, s32[1,1]{1,0:T(1,128)} %bitcast.5.count_ref, bf16[288,136]{1,0:T(8,128)(2,1)S(1)} %copy-done, ...), custom_call_target="tpu_custom_call" | custom-call | tf_op jit(solution)/shard_map/sweep/pallas_call | solution.py:119
  77.1 1.9 %collective-permute-start.6 = (f32[24,128]{1,0:T(8,128)S(1)}, f32[24,128]{1,0:T(8,128)S(1)}, u32[]{:S(2)}, u32[]{:S(2)}) collective-permute-start(f32[24,128]{1,0:T(8,128)S(1)} %get-tuple-element.48), channel_id=1, source_target_pairs={{0,1},{1,0},{2,3},{3,2},{4,5},{5,4},{6,7},{7,6},{8,9},{9,8},{10,11... | collective-permute-start | bytes 36872 | tf_op jit(solution)/shard_map/ppermute | solution.py:527
  79.0 3.7 %collective-permute-start.7 = (f32[24,128]{1,0:T(8,128)S(1)}, f32[24,128]{1,0:T(8,128)S(1)}, u32[]{:S(2)}, u32[]{:S(2)}) collective-permute-start(f32[24,128]{1,0:T(8,128)S(1)} %get-tuple-element.49), channel_id=1, source_target_pairs={{1,2},{2,1},{3,4},{4,3},{5,6},{6,5},{9,10},{10,9},{11,12},{12,11},... | collective-permute-start | bytes 36872 | tf_op jit(solution)/shard_map/ppermute | solution.py:527
  82.7 1.9 %collective-permute-start.8 = (f32[24,128]{1,0:T(8,128)S(1)}, f32[24,128]{1,0:T(8,128)S(1)}, u32[]{:S(2)}, u32[]{:S(2)}) collective-permute-start(f32[24,128]{1,0:T(8,128)S(1)} %get-tuple-element.50), channel_id=1, source_target_pairs={{0,8},{8,0},{16,24},{24,16},{32,40},{40,32},{48,56},{56,48},{64,72... | collective-permute-start | bytes 36872 | tf_op jit(solution)/shard_map/ppermute | solution.py:527
  84.6 3.4 %collective-permute-start.9 = (f32[24,128]{1,0:T(8,128)S(1)}, f32[24,128]{1,0:T(8,128)S(1)}, u32[]{:S(2)}, u32[]{:S(2)}) collective-permute-start(f32[24,128]{1,0:T(8,128)S(1)} %get-tuple-element.51), channel_id=1, source_target_pairs={{8,16},{16,8},{24,32},{32,24},{40,48},{48,40},{56,64},{64,56},{72,... | collective-permute-start | bytes 36872 | tf_op jit(solution)/shard_map/ppermute | solution.py:527
  88.8 3.5 %collective-permute-done.9.elem_1 = f32[24,128]{1,0:T(8,128)S(1)} collective-permute-done((f32[24,128]{1,0:T(8,128)S(1)}, f32[24,128]{1,0:T(8,128)S(1)}, u32[]{:S(2)}, u32[]{:S(2)}) %collective-permute-start.9) | collective-permute-done | bytes 12320 | tf_op jit(solution)/shard_map/ppermute | solution.py:527
  92.3 1.3 %last.1 = f32[5,27,128]{2,1,0:T(8,128)} custom-call(f32[136,128]{1,0:T(8,128)S(1)} %local.3.base_ref, s32[1,1]{1,0:T(1,128)} %bitcast.6.count_ref, f32[6,136,48]{2,1,0:T(8,128)S(1)} %get-tuple-element.33.m_ref, s32[6,128]{1,0:T(8,128)S(1)} %copy-done.3, f32[24,128]{1,0:T(8,128)S(1)} %collective-permute-done.6.sub_0, ...), custom_call_target="tpu_custom_call" | custom-call | tf_op jit(solution)/shard_map/last/pallas_call | solution.py:119
  (34 shorter events, 2.1 us)
Async XLA Ops:
  0.6 21.8 %copy-start = (bf16[288,136]{1,0:T(8,128)(2,1)S(1)}, bf16[288,136]{1,0:T(8,128)(2,1)}, u32[]{:S(2)}) copy-start(bf16[288,136]{1,0:T(8,128)(2,1)} %constant.10.clone.select_ref) | copy-start | bytes 235012
  2.8 19.5 %copy-start.11 = (s32[1,4,64]{2,1,0:T(4,128)S(1)}, s32[1,4,64]{2,1,0:T(4,128)}, u32[]{:S(2)}) copy-start(s32[1,4,64]{2,1,0:T(4,128)} %param.24) | copy-start | bytes 3076
  2.8 32.7 %all-to-all-start = ((f32[64,2,128]{2,1,0:T(2,128)}), f32[64,2,128]{2,1,0:T(2,128)S(1)}, u32[]{:S(2)}, u32[]{:S(2)}) async-start(f32[64,2,128]{2,1,0:T(2,128)} %payload.1), calls=%async_computation | async-start | bytes 131072 | tf_op jit(solution)/shard_map/all_to_all | solution.py:532
  22.4 0.9 copy-start.6
  38.2 11.2 %copy-start.1 = (f32[135,270]{1,0:T(8,128)S(1)}, f32[135,270]{1,0:T(8,128)}, u32[]{:S(2)}) copy-start(f32[135,270]{1,0:T(8,128)} %lift_ref.1) | copy-start | bytes 437404
  38.2 11.2 %copy-start.2 = (bf16[270,288]{1,0:T(8,128)(2,1)S(1)}, bf16[270,288]{1,0:T(8,128)(2,1)}, u32[]{:S(2)}) copy-start(bf16[270,288]{1,0:T(8,128)(2,1)} %constant.11.clone.place_ref) | copy-start | bytes 466564
  38.2 11.3 %copy-start.4 = (f32[135,135]{1,0:T(8,128)S(1)}, f32[135,135]{1,0:T(8,128)}, u32[]{:S(2)}) copy-start(f32[135,135]{1,0:T(8,128)} %vol_ref.1) | copy-start | bytes 218704
  38.2 11.3 %copy-start.5 = (f32[135,135]{1,0:T(8,128)S(1)}, f32[135,135]{1,0:T(8,128)}, u32[]{:S(2)}) copy-start(f32[135,135]{1,0:T(8,128)} %inv_ref.1) | copy-start | bytes 218704
  38.2 11.3 %copy-start.7 = (f32[5,27,128]{2,1,0:T(8,128)S(1)}, f32[5,27,128]{2,1,0:T(8,128)}, u32[]{:S(2)}) copy-start(f32[5,27,128]{2,1,0:T(8,128)} %right_ref.1) | copy-start | bytes 207364
  38.2 15.4 %all-to-all-start.1 = ((f32[8,8,2432]{2,1,0:T(8,128)}), f32[8,8,2432]{2,1,0:T(8,128)S(1)}, u32[]{:S(2)}, u32[]{:S(2)}) async-start(f32[8,8,2432]{2,1,0:T(8,128)} %compact.1), calls=%async_computation.1 | async-start | bytes 1245184 | tf_op jit(solution)/shard_map/all_to_all | solution.py:532
  43.2 6.3 %copy-start.3 = (s32[6,128]{1,0:T(8,128)S(1)}, s32[6,128]{1,0:T(8,128)}, u32[]{:S(2)}) copy-start(s32[6,128]{1,0:T(8,128)} %where_ref.11) | copy-start | bytes 9220
  43.2 8.1 %collective-permute-start = (f32[24,128]{1,0:T(8,128)S(1)}, f32[24,128]{1,0:T(8,128)S(1)}, u32[]{:S(2)}, u32[]{:S(2)}) collective-permute-start(f32[24,128]{1,0:T(8,128)S(1)} %get-tuple-element.34), channel_id=1, source_target_pairs={{0,8},{8,0},{16,24},{24,16},{32,40},{40,32},{48,56},{56,48},{64,72... | collective-permute-start | bytes 36872 | tf_op jit(solution)/shard_map/ppermute | solution.py:527
  45.9 7.7 %collective-permute-start.1 = (f32[24,128]{1,0:T(8,128)S(1)}, f32[24,128]{1,0:T(8,128)S(1)}, u32[]{:S(2)}, u32[]{:S(2)}) collective-permute-start(f32[24,128]{1,0:T(8,128)S(1)} %get-tuple-element.35), channel_id=1, source_target_pairs={{8,16},{16,8},{24,32},{32,24},{40,48},{48,40},{56,64},{64,56},{72,... | collective-permute-start | bytes 36872 | tf_op jit(solution)/shard_map/ppermute | solution.py:527
  49.5 4.2 %copy-start.8 = (f32[3,27,128]{2,1,0:T(8,128)S(1)}, f32[3,27,128]{2,1,0:T(8,128)}, u32[]{:S(2)}) copy-start(f32[3,27,128]{2,1,0:T(8,128)} %node_ref.1) | copy-start | bytes 124420
  49.5 4.1 %copy-start.9 = (bf16[96,32]{1,0:T(8,128)(2,1)S(1)}, bf16[96,32]{1,0:T(8,128)(2,1)}, u32[]{:S(2)}) copy-start(bf16[96,32]{1,0:T(8,128)(2,1)} %constant.8.clone.derivs_ref) | copy-start | bytes 18436
  49.5 4.1 %copy-start.10 = (bf16[32,8]{1,0:T(8,128)(2,1)S(1)}, bf16[32,8]{1,0:T(8,128)(2,1)}, u32[]{:S(2)}) copy-start(bf16[32,8]{1,0:T(8,128)(2,1)} %constant.9.clone.blend_ref) | copy-start | bytes 1540
  61.8 9.4 %collective-permute-start.2 = (f32[24,128]{1,0:T(8,128)S(1)}, f32[24,128]{1,0:T(8,128)S(1)}, u32[]{:S(2)}, u32[]{:S(2)}) collective-permute-start(f32[24,128]{1,0:T(8,128)S(1)} %get-tuple-element.42), channel_id=1, source_target_pairs={{0,1},{1,0},{2,3},{3,2},{4,5},{5,4},{6,7},{7,6},{8,9},{9,8},{10,11... | collective-permute-start | bytes 36872 | tf_op jit(solution)/shard_map/ppermute | solution.py:527
  63.7 7.5 %collective-permute-start.3 = (f32[24,128]{1,0:T(8,128)S(1)}, f32[24,128]{1,0:T(8,128)S(1)}, u32[]{:S(2)}, u32[]{:S(2)}) collective-permute-start(f32[24,128]{1,0:T(8,128)S(1)} %get-tuple-element.43), channel_id=1, source_target_pairs={{1,2},{2,1},{3,4},{4,3},{5,6},{6,5},{9,10},{10,9},{11,12},{12,11},... | collective-permute-start | bytes 36872 | tf_op jit(solution)/shard_map/ppermute | solution.py:527
  66.3 5.6 %collective-permute-start.4 = (f32[24,128]{1,0:T(8,128)S(1)}, f32[24,128]{1,0:T(8,128)S(1)}, u32[]{:S(2)}, u32[]{:S(2)}) collective-permute-start(f32[24,128]{1,0:T(8,128)S(1)} %get-tuple-element.44), channel_id=1, source_target_pairs={{0,8},{8,0},{16,24},{24,16},{32,40},{40,32},{48,56},{56,48},{64,72... | collective-permute-start | bytes 36872 | tf_op jit(solution)/shard_map/ppermute | solution.py:527
  68.2 7.7 %collective-permute-start.5 = (f32[24,128]{1,0:T(8,128)S(1)}, f32[24,128]{1,0:T(8,128)S(1)}, u32[]{:S(2)}, u32[]{:S(2)}) collective-permute-start(f32[24,128]{1,0:T(8,128)S(1)} %get-tuple-element.45), channel_id=1, source_target_pairs={{8,16},{16,8},{24,32},{32,24},{40,48},{48,40},{56,64},{64,56},{72,... | collective-permute-start | bytes 36872 | tf_op jit(solution)/shard_map/ppermute | solution.py:527
  77.1 11.7 %collective-permute-start.6 = (f32[24,128]{1,0:T(8,128)S(1)}, f32[24,128]{1,0:T(8,128)S(1)}, u32[]{:S(2)}, u32[]{:S(2)}) collective-permute-start(f32[24,128]{1,0:T(8,128)S(1)} %get-tuple-element.48), channel_id=1, source_target_pairs={{0,1},{1,0},{2,3},{3,2},{4,5},{5,4},{6,7},{7,6},{8,9},{9,8},{10,11... | collective-permute-start | bytes 36872 | tf_op jit(solution)/shard_map/ppermute | solution.py:527
  79.0 9.8 %collective-permute-start.7 = (f32[24,128]{1,0:T(8,128)S(1)}, f32[24,128]{1,0:T(8,128)S(1)}, u32[]{:S(2)}, u32[]{:S(2)}) collective-permute-start(f32[24,128]{1,0:T(8,128)S(1)} %get-tuple-element.49), channel_id=1, source_target_pairs={{1,2},{2,1},{3,4},{4,3},{5,6},{6,5},{9,10},{10,9},{11,12},{12,11},... | collective-permute-start | bytes 36872 | tf_op jit(solution)/shard_map/ppermute | solution.py:527
  82.7 6.2 %collective-permute-start.8 = (f32[24,128]{1,0:T(8,128)S(1)}, f32[24,128]{1,0:T(8,128)S(1)}, u32[]{:S(2)}, u32[]{:S(2)}) collective-permute-start(f32[24,128]{1,0:T(8,128)S(1)} %get-tuple-element.50), channel_id=1, source_target_pairs={{0,8},{8,0},{16,24},{24,16},{32,40},{40,32},{48,56},{56,48},{64,72... | collective-permute-start | bytes 36872 | tf_op jit(solution)/shard_map/ppermute | solution.py:527
  84.6 7.7 %collective-permute-start.9 = (f32[24,128]{1,0:T(8,128)S(1)}, f32[24,128]{1,0:T(8,128)S(1)}, u32[]{:S(2)}, u32[]{:S(2)}) collective-permute-start(f32[24,128]{1,0:T(8,128)S(1)} %get-tuple-element.51), channel_id=1, source_target_pairs={{8,16},{16,8},{24,32},{32,24},{40,48},{48,40},{56,64},{64,56},{72,... | collective-permute-start | bytes 36872 | tf_op jit(solution)/shard_map/ppermute | solution.py:527

commit v3 on v2

--- a/solution.py
+++ b/solution.py
@@ -13,7 +13,7 @@
 RADIUS = 1.5
 FAR = 1000.0
 LANES = 128
-STRIP = 768
+STRIP = 640
 RUN = 768
 PACKET = 384
 TILES = 16
@@ -21,6 +21,7 @@
 INTERPRET = False
 F32, BF16, I32 = jnp.float32, jnp.bfloat16, jnp.int32
 VMEM = pltpu.MemorySpace.VMEM
+HBM = pltpu.MemorySpace.HBM
 
 
 def node_tables():
@@ -70,6 +71,12 @@
     return out
 
 
+def stored_dot(a_ref, b):
+    b1, b2 = pieces(b, 2)
+    high = jnp.dot(a_ref[0], b1, preferred_element_type=F32)
+    return high + (jnp.dot(a_ref[0], b2, preferred_element_type=F32) + jnp.dot(a_ref[1], b1, preferred_element_type=F32))
+
+
 def split_dot(a, b):
     a1, a2 = pieces(a, 2)
     b1, b2 = pieces(b, 2)
@@ -97,7 +104,7 @@
     return jnp.where(mask, 1.0, 0.0).astype(dtype)
 
 
-def call(body, out_shape, in_spaces, scratch=(), held=True, out_specs=None, **kw):
+def call(body, out_shape, in_spaces, scratch=(), held=True, in_specs=None, out_specs=None, **kw):
     held = held if isinstance(held, list) else jax.tree.map(lambda _: held, out_shape)
 
     def place(s, stays):
@@ -106,7 +113,7 @@
     run = pl.pallas_call(
         body,
         out_shape=jax.tree.map(place, out_shape, held),
-        in_specs=[pl.BlockSpec(memory_space=VMEM) for _ in in_spaces],
+        in_specs=in_specs or [pl.BlockSpec(memory_space=VMEM) for _ in in_spaces],
         out_specs=out_specs or jax.tree.map(lambda _: pl.BlockSpec(memory_space=VMEM), out_shape),
         scratch_shapes=list(scratch),
         interpret=INTERPRET,
@@ -140,7 +147,7 @@
     out_ref[...] = jnp.broadcast_to(row_ref[0:2, :][None], out_ref.shape)
 
 
-def compact_body(in_ref, p0, p1, out_ref, part_ref):
+def compact_body(in_ref, p0, p1, order_ref, out_ref, part_ref):
     owners = in_ref.shape[0]
     copies, _, room = out_ref.shape
     room = room - PACKET
@@ -160,8 +167,8 @@
     pick = flag(iota((8, LANES), 1) == 96, BF16)
     count_row = nt_dot(pick, second.astype(BF16))
     start_row = jnp.dot(count_row.astype(BF16), above, preferred_element_type=F32)
-    total = jnp.max(start_row + count_row).astype(I32)
     low, end = start_row[0:1, :], (start_row + count_row)[0:1, :]
+    total = jnp.max(end, axis=1, keepdims=True)
     for at, piece in enumerate(pieces(first, 3)):
         part_ref[:, LANES * at : LANES * at + LANES] = piece
     for at, piece in enumerate(pieces(second, 2) + pieces(start_col, 2)):
@@ -173,7 +180,7 @@
     slot = (iota((strip, LANES), 1) % 32).astype(F32)
 
     def one_strip(at, carry):
-        base = jnp.minimum(at * strip, room - strip)
+        base = min(at * strip, room - strip) if isinstance(at, int) else jnp.minimum(at * strip, room - strip)
         place = (iota((strip, owners), 0) + base).astype(F32)
         owner = flag((place >= low) & (place < end), BF16)
         found = jnp.dot(owner, part_ref[...], preferred_element_type=F32)
@@ -188,18 +195,20 @@
                 b = jnp.where(mine, found[:, LANES * (3 + k) : LANES * (4 + k)], 0.0).astype(BF16)
                 both = both + nt_dot(fold_second, b)
             out = both if out is None else out + both
-        dead = iota((8, strip), 1) + base >= total
+        dead = (iota((8, strip), 1) + base).astype(F32) >= total
         row = iota((8, strip), 0)
         out = jnp.where(dead, jnp.where(row < 3, FAR, 0.0), out)
         square = jnp.sum(jnp.where(row < 3, out * out, 0.0), axis=0, keepdims=True)
         out = jnp.where(row == 3, square, out)
-        out = jnp.where(row == 7, total.astype(F32), out)
-        out_ref[:, :, pl.ds(pl.multiple_of(base, LANES), strip)] = jnp.broadcast_to(
+        out = jnp.where(row == 7, total, out)
+        out_ref[:, :, pl.ds(base if isinstance(base, int) else pl.multiple_of(base, LANES), strip)] = jnp.broadcast_to(
             out[None], (copies, 8, strip)
         )
         return carry
 
-    lax.fori_loop(0, (total + (strip - 1)) // strip, one_strip, 0)
+    one_strip(0, 0)
+    strips = (jnp.max(total).astype(I32) + (strip - 1)) // strip
+    lax.fori_loop(1, strips, one_strip, 0)
 
 
 def radial_displacement(z_ref, node_ref, corner_ref, hit_ref, rank_ref, list_ref, sum_ref, over_ref, over_smem, sem):
@@ -231,7 +240,7 @@
         for c in range(8):
             corner_ref[i, 8 * c : 8 * c + 8, :] = jnp.take_along_axis(
                 jnp.broadcast_to(at[i][c], (8, LANES)), pick, axis=1
-            )
+            ) * (1.0 / RADIUS)
         sum_ref[i] = jnp.zeros((64, LANES), F32)
     counts = [jnp.max(z_ref[g, 7:8, 0:LANES]).astype(I32) for g in range(groups)]
     most = functools.reduce(jnp.maximum, counts)
@@ -253,7 +262,8 @@
             key = jnp.where(half == h, rank - shift, 0.0)
             chosen = jnp.concatenate([flag(key == s + 1.0) for s in range(SLOTS)], axis=0).astype(BF16)
             found = nt_dot(three, chosen)
-            entries.append(found[0:8] + found[8:16] + found[16:24])
+            found = found[0:8] + found[8:16] + found[16:24]
+            entries.append(jnp.where(iota((8, LANES), 0) < 4, found * (1.0 / RADIUS), found * 4.0))
         return entries
 
     def one_part(part, carry):
@@ -314,10 +324,10 @@
                         entry = list_ref.at[4 * step + 2 * i + e]
                         gap = [place[axis] - entry[axis : axis + 1, :] for axis in range(3)]
                         square = gap[0] * gap[0] + gap[1] * gap[1] + gap[2] * gap[2]
-                        ratio = square * lax.rsqrt(jnp.maximum(square, 1e-20)) * (1.0 / RADIUS)
+                        ratio = square * lax.rsqrt(jnp.maximum(square, 1e-20))
                         inside = jnp.maximum(1.0 - ratio, 0.0)
                         inside = inside * inside
-                        kernel = inside * inside * (4.0 * ratio + 1.0)
+                        kernel = inside * inside * (ratio + 0.25)
                         for axis in range(3):
                             total[axis] = total[axis] + entry[4 + axis : 5 + axis, :] * kernel
                     for axis in range(3):
@@ -387,7 +397,7 @@
     metric_ref[...] = jnp.zeros_like(metric_ref)
     for v in range(5):
         metric_ref[27 * v : 27 * v + 27, :] = metric[0:27]
-    state = base + split_dot(minus_inv_ref[...], metric_ref[...] * start_ref[...])
+    state = base + stored_dot(minus_inv_ref, metric_ref[...] * start_ref[...])
     finish(state, count_ref, select_ref, send_ref, state_ref, trace_ref, packet_refs)
     out.wait()
 
@@ -395,7 +405,7 @@
 def finish(state, count_ref, select_ref, send_ref, state_ref, trace_ref, packet_refs):
     state = jnp.where(iota(state.shape, 1) < jnp.broadcast_to(count_ref[...], state.shape), state, 0.0)
     state_ref[...] = state
-    traces = pick_dot(select_ref[...], state, 3)
+    traces = pick_dot(select_ref[...], state, 2)
     for f in range(6):
         trace_ref[f] = traces[48 * f : 48 * f + 48]
     tiles = [traces[48 * f : 48 * f + 48] for f in range(6)]
@@ -427,7 +437,7 @@
 
 def from_neighbours(before_sub, behind_sub, before_elem, behind_elem, where_ref, m_ref):
     packets = (before_sub, behind_sub, before_elem, behind_elem)
-    total = None
+    columns = []
     for f in range(6):
         index = where_ref[f : f + 1, :] - 6 * LANES
         packet = jnp.broadcast_to(jnp.where(index >= 0, index // 64, -1), (24, LANES))
@@ -438,9 +448,8 @@
             for q, values in enumerate(packets):
                 found = jnp.where(packet == q, jnp.take_along_axis(values, lane + 64 * half, axis=1), found)
             halves.append(found)
-        part = split_dot(m_ref[f], jnp.concatenate(halves, axis=0))
-        total = part if total is None else total + part
-    return total
+        columns += halves
+    return stored_dot(m_ref, jnp.concatenate(columns, axis=0))
 
 
 def arrived(sub_0, sub_1, elem_0, elem_1, where_ref, m_ref):
@@ -448,55 +457,49 @@
     return from_neighbours(*sub, *in_line("elem", elem_0[...], elem_1[...]), where_ref, m_ref)
 
 
-def setup_state_body(u_ref, count_ref, select_ref, send_ref, state_ref, trace_ref, p0, p1, p2, p3, flat_ref):
-    packet_refs = (p0, p1, p2, p3)
+def setup_body(
+    u_ref, count_ref, select_ref, send_ref, vol_ref, inv_ref, lift_ref, place_ref, right_ref, where_ref,
+    state_ref, trace_ref, p0, p1, p2, p3, held_ref, sent_ref, link_ref, minus_ref, both_ref, m_ref, const_ref, base_ref,
+    flat_ref, wide_ref,
+):
+    held_ref[...] = jnp.broadcast_to(count_ref[...], held_ref.shape)
+    sent_ref[...] = send_ref[...]
+    link_ref[...] = where_ref[...]
     flat_ref[...] = jnp.zeros_like(flat_ref)
     for v in range(5):
         flat_ref[27 * v : 27 * v + 27, :] = u_ref[v]
-    finish(flat_ref[...], count_ref, select_ref, send_ref, state_ref, trace_ref, packet_refs)
-
-
-def setup_matrix_body(
-    vol_ref, inv_ref, lift_ref, place_ref, right_ref, state_ref, trace_ref, where_ref,
-    minus_ref, both_ref, m_ref, const_ref, base_ref, flat_ref, wide_ref,
-):
+    finish(flat_ref[...], held_ref, select_ref, send_ref, state_ref, trace_ref, (p0, p1, p2, p3))
     wide_ref[...] = jnp.zeros_like(wide_ref)
     wide_ref[0:135, 0:135] = inv_ref[...]
     inverse = wide_ref[:, 0:136]
-    minus_ref[...] = -inverse
-    both_ref[...] = jnp.zeros_like(both_ref)
-    both_ref[0:135, 0:135] = -split_dot(inv_ref[...], vol_ref[...])
-    m_ref[...] = jnp.zeros_like(m_ref)
-    coupling = split_dot(inv_ref[...], lift_ref[...])
-    moved = None
-    for piece in pieces(coupling, 3):
-        part = jnp.dot(piece, place_ref[...], preferred_element_type=F32)
-        moved = part if moved is None else moved + part
-    for f in range(6):
-        m_ref[f, 0:135, :] = moved[:, 48 * f : 48 * f + 48]
+    wide_ref[0:135, 0:135] = -split_dot(inv_ref[...], vol_ref[...])
+    for k, piece in enumerate(pieces(-inverse, 2)):
+        minus_ref[k] = piece
+    for k, piece in enumerate(pieces(wide_ref[:, 0:136], 2)):
+        both_ref[k] = piece
+    coupling = split_dot(inverse[:, 0:135], lift_ref[...])
+    moved = [jnp.dot(piece, place_ref[...], preferred_element_type=F32) for piece in pieces(coupling, 2)]
+    for k in range(2):
+        m_ref[k] = moved[k].astype(BF16)
     flat_ref[...] = jnp.zeros_like(flat_ref)
     for v in range(5):
         flat_ref[27 * v : 27 * v + 27, :] = right_ref[v]
     const = split_dot(inverse, flat_ref[...])
     const_ref[...] = const
     state = state_ref[...]
-    base_ref[...] = state + const + split_dot(both_ref[...], state) + local_part(trace_ref, where_ref, m_ref)
+    base_ref[...] = state + const + stored_dot(both_ref, state) + local_part(trace_ref, where_ref, m_ref)
 
 
 def local_part(trace_ref, where_ref, m_ref):
     tiles = [trace_ref[f] for f in range(6)]
-    total = None
-    for f in range(6):
-        found = gather_columns(tiles, where_ref[f : f + 1, :], 0)
-        part = split_dot(m_ref[f], found)
-        total = part if total is None else total + part
-    return total
+    columns = [gather_columns(tiles, where_ref[f : f + 1, :], 0) for f in range(6)]
+    return stored_dot(m_ref, jnp.concatenate(columns, axis=0))
 
 
 def local_body(state_ref, trace_ref, metric_ref, const_ref, minus_ref, both_ref, m_ref, where_ref, out_ref):
     state = state_ref[...]
-    out = state + const_ref[...] + split_dot(both_ref[...], state)
-    out = out + split_dot(minus_ref[...], metric_ref[...] * state)
+    out = state + const_ref[...] + stored_dot(both_ref, state)
+    out = out + stored_dot(minus_ref, metric_ref[...] * state)
     out_ref[...] = out + local_part(trace_ref, where_ref, m_ref)
 
 
@@ -538,7 +541,7 @@
     return call(
         radial_body,
         [shape_of(3, 27, LANES), shape_of(136, LANES), *STATE],
-        [VMEM] * 7 + [None] + [VMEM] * 6,
+        [VMEM] * 14,
         [
             pltpu.VMEM((3, 64, LANES), F32),
             pltpu.VMEM((blocks * TILES, LANES), F32),
@@ -572,55 +575,55 @@
     room = n_elem * cp_pos.shape[1]
     send = send_list.reshape(2, LANES)
 
-    held_count = elem_count.reshape(1, 1)
     copies = call(
         payload_body, shape_of(n_elem, 2, LANES), [None] * 3, [pltpu.VMEM((8, LANES), F32)], name="payload"
     )(cp_count.reshape(1, 1), cp_pos, cp_coef)
     mine = spread(copies, "elem")
-    state, traces, *packets = call(
-        setup_state_body, STATE, [VMEM, None, VMEM, VMEM], [pltpu.VMEM((136, LANES), F32)], name="setup_state"
-    )(u_prev, held_count, select, send)
+    *first, held_count, sent, link, minus, both, coupling, const, base = call(
+        setup_body,
+        [
+            *STATE, shape_of(1, LANES, dtype=I32), shape_of(2, LANES, dtype=I32), shape_of(6, LANES, dtype=I32),
+            shape_of(2, 136, 136, dtype=BF16), shape_of(2, 136, 136, dtype=BF16), shape_of(2, 136, 288, dtype=BF16),
+            shape_of(136, LANES), shape_of(136, LANES),
+        ],
+        [None, None, HBM, None, HBM, HBM, HBM, HBM, HBM, HBM],
+        [pltpu.VMEM((136, LANES), F32), pltpu.VMEM((136, 256), F32)],
+        name="setup",
+    )(
+        u_prev, elem_count.reshape(1, 1), select, send, vol_block, block_inv, lift_matrix, place, right_side, face_link
+    )
+    state, traces, *packets = first
     gathered = call(
         compact_body,
         shape_of(n_sub, 8, room + PACKET),
-        [VMEM] * 3,
+        [VMEM] * 4,
         [pltpu.VMEM((n_elem, 7 * LANES), BF16)],
         name="compact",
-    )(mine, packets[0], packets[1])
+    )(mine, packets[0], packets[1], base)
     points = spread(gathered, "sub")
     received = exchange(packets, ("elem",))
-    minus, both, coupling, const, base = call(
-        setup_matrix_body,
-        [
-            shape_of(136, 136), shape_of(136, 136), shape_of(6, 136, 48),
-            shape_of(136, LANES), shape_of(136, LANES),
-        ],
-        [VMEM] * 8,
-        [pltpu.VMEM((136, LANES), F32), pltpu.VMEM((136, 256), F32)],
-        name="setup_matrix",
-    )(vol_block, block_inv, lift_matrix, place, right_side, state, traces, face_link)
     displacement, metric, state, traces, *packets = radial_call(
-        points, node_ref, derivs, blending, base, state, minus, held_count, select, send,
-        coupling, face_link, received,
+        points, node_ref, derivs, blending, base, state, minus, held_count, select, sent,
+        coupling, link, received,
     )
     for sweep in range(1, ITERS):
         received = exchange(packets)
         base = call(local_body, shape_of(136, LANES), [VMEM] * 8, name="local")(
-            state, traces, metric, const, minus, both, coupling, face_link
+            state, traces, metric, const, minus, both, coupling, link
         )
         if sweep < ITERS - 1:
-            state, traces, *packets = call(sweep_body, STATE, [VMEM, None] + [VMEM] * 8, name="sweep")(
-                base, held_count, select, send, coupling, face_link, *received
+            state, traces, *packets = call(sweep_body, STATE, [VMEM] * 10, name="sweep")(
+                base, held_count, select, sent, coupling, link, *received
             )
         else:
             solution_out = call(
                 last_body,
                 shape_of(5, 27, LANES),
-                [VMEM, None] + [VMEM] * 6,
+                [VMEM] * 8,
                 [pltpu.VMEM((136, LANES), F32)],
                 held=False,
                 name="last",
-            )(base, held_count, coupling, face_link, *received)
+            )(base, held_count, coupling, link, *received)
     return displacement, solution_out
 
 

time: 94.1 us -> 92.7 us (0.985)
  the two profiles are of different devices: /device:TPU:12 before, /device:TPU:14 now
where the time goes in v3:
time: 92.7 us; the launch traced here: 91.5 us
  starting transfers between devices  49.4 us (53%)
  waiting for transfers between devices  22 us (24%)
  Pallas kernels  17.3 us (19%)
  between operations  2.11 us (2%)
    ppermute x10, starting transfers between devices, exchange(): out.append(lax.ppermute(packets[first + turn], axis, pairs))  25.6 us
    all_to_all x2, starting transfers between devices, spread(): return lax.all_to_all(copies, axis, split_axis=0, concat_axis=0, tiled=True)  23.8 us
    pallas_call x8, Pallas kernels, placed(): run(*[a if s is None else pltpu.with_memory_space_constraint(a, s) for a,...  17.3 us
    ppermute x10, waiting for transfers between devices, exchange(): out.append(lax.ppermute(packets[first + turn], axis, pairs))  12.8 us
    all_to_all x2, waiting for transfers between devices, spread(): return lax.all_to_all(copies, axis, split_axis=0, concat_axis=0, tiled=True)  9.27 us
  transfers between devices with their start and end apart: 12, of which 6 were waited for; matrix products, arithmetic and copies ran while one was open for 1% of the time, Pallas kernels for 5%

profile of v3, /device:TPU:14, one launch (start us, length us, event | category | flops | bytes accessed | tf_op | source)
XLA Modules:
  0.0 91.5 jit_solution(9320554371927144312)
XLA Ops:
  1.3 1.5 %payload.1 = f32[64,2,128]{2,1,0:T(2,128)} custom-call(s32[1,1]{1,0:T(1,128)} %bitcast.2.count_ref, f32[3,32]{1,0:T(4,128)} %pos_ref.1, f32[3,32]{1,0:T(4,128)} %coef_ref.1), custom_call_target="tpu_custom_call" | custom-call | tf_op jit(solution)/shard_map/payload/pallas_call | solution.py:126
  2.8 18.9 %all-to-all-start = ((f32[64,2,128]{2,1,0:T(2,128)}), f32[64,2,128]{2,1,0:T(2,128)S(1)}, u32[]{:S(2)}, u32[]{:S(2)}) async-start(f32[64,2,128]{2,1,0:T(2,128)} %payload.1), calls=%async_computation | async-start | bytes 131072 | tf_op jit(solution)/shard_map/all_to_all | solution.py:535
  22.3 0.6 reshape.15.send_ref
  22.9 3.2 %setup.1 = (f32[136,128]{1,0:T(8,128)S(1)}, f32[6,48,128]{2,1,0:T(8,128)}, f32[24,128]{1,0:T(8,128)S(1)}, f32[24,128]{1,0:T(8,128)S(1)}, f32[24,128]{1,0:T(8,128...) custom-call(f32[5,27,128]{2,1,0:T(8,128)} %u_ref.1, ...), custom_call_target="tpu_custom_call" | custom-call | tf_op jit(solution)/shard_map/setup/pallas_call | solution.py:126
  26.2 9.3 %all-to-all-done.in_ref = f32[64,2,128]{2,1,0:T(2,128)S(1)} async-done(((f32[64,2,128]{2,1,0:T(2,128)}), f32[64,2,128]{2,1,0:T(2,128)S(1)}, u32[]{:S(2)}, u32[]{:S(2)}) %all-to-all-start) | async-done | bytes 65568 | tf_op jit(solution)/shard_map/all_to_all | solution.py:535
  35.4 2.4 %compact.1 = f32[8,8,2432]{2,1,0:T(8,128)} custom-call(f32[64,2,128]{2,1,0:T(2,128)S(1)} %all-to-all-done.in_ref, f32[24,128]{1,0:T(8,128)S(1)} %get-tuple-element.29.p0, f32[24,128]{1,0:T(8,128)S(1)} %get-tuple-element.30.p1, f32[136,128]{1,0:T(8,128)S(1)} %get-tuple-element.31.order_ref.base_ref), custom_call_target="tpu_custom_call" | custom-call | tf_op jit(solution)/shard_map/compact/pallas_call | solution.py:126
  37.8 4.9 %all-to-all-start.1 = ((f32[8,8,2432]{2,1,0:T(8,128)}), f32[8,8,2432]{2,1,0:T(8,128)S(1)}, u32[]{:S(2)}, u32[]{:S(2)}) async-start(f32[8,8,2432]{2,1,0:T(8,128)} %compact.1), calls=%async_computation.1 | async-start | bytes 1245184 | tf_op jit(solution)/shard_map/all_to_all | solution.py:535
  42.7 2.8 %collective-permute-start = (f32[24,128]{1,0:T(8,128)S(1)}, f32[24,128]{1,0:T(8,128)S(1)}, u32[]{:S(2)}, u32[]{:S(2)}) collective-permute-start(f32[24,128]{1,0:T(8,128)S(1)} %get-tuple-element.38), channel_id=1, source_target_pairs={{0,8},{8,0},{16,24},{24,16},{32,40},{40,32},{48,56},{56,48},{64,72... | collective-permute-start | bytes 36872 | tf_op jit(solution)/shard_map/ppermute | solution.py:530
  45.5 3.5 %collective-permute-start.1 = (f32[24,128]{1,0:T(8,128)S(1)}, f32[24,128]{1,0:T(8,128)S(1)}, u32[]{:S(2)}, u32[]{:S(2)}) collective-permute-start(f32[24,128]{1,0:T(8,128)S(1)} %get-tuple-element.39), channel_id=1, source_target_pairs={{8,16},{16,8},{24,32},{32,24},{40,48},{48,40},{56,64},{64,56},{72,... | collective-permute-start | bytes 36872 | tf_op jit(solution)/shard_map/ppermute | solution.py:530
  49.0 4.2 %collective-permute-done.1.elem_1 = f32[24,128]{1,0:T(8,128)S(1)} collective-permute-done((f32[24,128]{1,0:T(8,128)S(1)}, f32[24,128]{1,0:T(8,128)S(1)}, u32[]{:S(2)}, u32[]{:S(2)}) %collective-permute-start.1) | collective-permute-done | bytes 12320 | tf_op jit(solution)/shard_map/ppermute | solution.py:530
  53.2 6.5 %radial.1 = (f32[3,27,128]{2,1,0:T(8,128)}, f32[136,128]{1,0:T(8,128)S(1)}, f32[136,128]{1,0:T(8,128)S(1)}, f32[6,48,128]{2,1,0:T(8,128)S(1)}, f32[24,128]{1,0:T...) custom-call(f32[8,8,2432]{2,1,0:T(8,128)S(1)} %all-to-all-done.1.z_ref, ...), custom_call_target="tpu_custom_call" | custom-call | tf_op jit(solution)/shard_map/radial/pallas_call | solution.py:126
  59.8 1.9 %collective-permute-start.2 = (f32[24,128]{1,0:T(8,128)S(1)}, f32[24,128]{1,0:T(8,128)S(1)}, u32[]{:S(2)}, u32[]{:S(2)}) collective-permute-start(f32[24,128]{1,0:T(8,128)S(1)} %get-tuple-element.46), channel_id=1, source_target_pairs={{0,1},{1,0},{2,3},{3,2},{4,5},{5,4},{6,7},{7,6},{8,9},{9,8},{10,11... | collective-permute-start | bytes 36872 | tf_op jit(solution)/shard_map/ppermute | solution.py:530
  61.7 4.3 %collective-permute-start.3 = (f32[24,128]{1,0:T(8,128)S(1)}, f32[24,128]{1,0:T(8,128)S(1)}, u32[]{:S(2)}, u32[]{:S(2)}) collective-permute-start(f32[24,128]{1,0:T(8,128)S(1)} %get-tuple-element.47), channel_id=1, source_target_pairs={{1,2},{2,1},{3,4},{4,3},{5,6},{6,5},{9,10},{10,9},{11,12},{12,11},... | collective-permute-start | bytes 36872 | tf_op jit(solution)/shard_map/ppermute | solution.py:530
  66.0 1.9 %collective-permute-start.4 = (f32[24,128]{1,0:T(8,128)S(1)}, f32[24,128]{1,0:T(8,128)S(1)}, u32[]{:S(2)}, u32[]{:S(2)}) collective-permute-start(f32[24,128]{1,0:T(8,128)S(1)} %get-tuple-element.48), channel_id=1, source_target_pairs={{0,8},{8,0},{16,24},{24,16},{32,40},{40,32},{48,56},{56,48},{64,72... | collective-permute-start | bytes 36872 | tf_op jit(solution)/shard_map/ppermute | solution.py:530
  67.9 2.6 %collective-permute-start.5 = (f32[24,128]{1,0:T(8,128)S(1)}, f32[24,128]{1,0:T(8,128)S(1)}, u32[]{:S(2)}, u32[]{:S(2)}) collective-permute-start(f32[24,128]{1,0:T(8,128)S(1)} %get-tuple-element.49), channel_id=1, source_target_pairs={{8,16},{16,8},{24,32},{32,24},{40,48},{48,40},{56,64},{64,56},{72,... | collective-permute-start | bytes 36872 | tf_op jit(solution)/shard_map/ppermute | solution.py:530
  70.5 0.6 local.2.base_ref
  71.6 4.0 %collective-permute-done.5.elem_1 = f32[24,128]{1,0:T(8,128)S(1)} collective-permute-done((f32[24,128]{1,0:T(8,128)S(1)}, f32[24,128]{1,0:T(8,128)S(1)}, u32[]{:S(2)}, u32[]{:S(2)}) %collective-permute-start.5) | collective-permute-done | bytes 12320 | tf_op jit(solution)/shard_map/ppermute | solution.py:530
  75.6 1.1 %sweep.1 = (f32[136,128]{1,0:T(8,128)S(1)}, f32[6,48,128]{2,1,0:T(8,128)S(1)}, f32[24,128]{1,0:T(8,128)S(1)}, f32[24,128]{1,0:T(8,128)S(1)}, f32[24,128]{1,0:T(8,128)S(1)}, /*index=5*/f32[24,128]{1,0:T(8,128)S(1)}) custom-call(f32[136,128]{1,0:T(8,128)S(1)} %local.2.base_ref, s32[1,128]{1,0:T(1,128)S(1)} %get-tuple-element.34.count_ref, ...), custom_call_target="tpu_custom_call" | custom-call | tf_op jit(solution)/shard_map/sweep/pallas_call | solution.py:126
  76.7 1.9 %collective-permute-start.6 = (f32[24,128]{1,0:T(8,128)S(1)}, f32[24,128]{1,0:T(8,128)S(1)}, u32[]{:S(2)}, u32[]{:S(2)}) collective-permute-start(f32[24,128]{1,0:T(8,128)S(1)} %get-tuple-element.52), channel_id=1, source_target_pairs={{0,1},{1,0},{2,3},{3,2},{4,5},{5,4},{6,7},{7,6},{8,9},{9,8},{10,11... | collective-permute-start | bytes 36872 | tf_op jit(solution)/shard_map/ppermute | solution.py:530
  78.6 1.9 %collective-permute-start.7 = (f32[24,128]{1,0:T(8,128)S(1)}, f32[24,128]{1,0:T(8,128)S(1)}, u32[]{:S(2)}, u32[]{:S(2)}) collective-permute-start(f32[24,128]{1,0:T(8,128)S(1)} %get-tuple-element.53), channel_id=1, source_target_pairs={{1,2},{2,1},{3,4},{4,3},{5,6},{6,5},{9,10},{10,9},{11,12},{12,11},... | collective-permute-start | bytes 36872 | tf_op jit(solution)/shard_map/ppermute | solution.py:530
  80.6 1.9 %collective-permute-start.8 = (f32[24,128]{1,0:T(8,128)S(1)}, f32[24,128]{1,0:T(8,128)S(1)}, u32[]{:S(2)}, u32[]{:S(2)}) collective-permute-start(f32[24,128]{1,0:T(8,128)S(1)} %get-tuple-element.54), channel_id=1, source_target_pairs={{0,8},{8,0},{16,24},{24,16},{32,40},{40,32},{48,56},{56,48},{64,72... | collective-permute-start | bytes 36872 | tf_op jit(solution)/shard_map/ppermute | solution.py:530
  82.5 2.9 %collective-permute-start.9 = (f32[24,128]{1,0:T(8,128)S(1)}, f32[24,128]{1,0:T(8,128)S(1)}, u32[]{:S(2)}, u32[]{:S(2)}) collective-permute-start(f32[24,128]{1,0:T(8,128)S(1)} %get-tuple-element.55), channel_id=1, source_target_pairs={{8,16},{16,8},{24,32},{32,24},{40,48},{48,40},{56,64},{64,56},{72,... | collective-permute-start | bytes 36872 | tf_op jit(solution)/shard_map/ppermute | solution.py:530
  86.1 4.0 %collective-permute-done.9.elem_1 = f32[24,128]{1,0:T(8,128)S(1)} collective-permute-done((f32[24,128]{1,0:T(8,128)S(1)}, f32[24,128]{1,0:T(8,128)S(1)}, u32[]{:S(2)}, u32[]{:S(2)}) %collective-permute-start.9) | collective-permute-done | bytes 12320 | tf_op jit(solution)/shard_map/ppermute | solution.py:530
  90.2 1.3 %last.1 = f32[5,27,128]{2,1,0:T(8,128)} custom-call(f32[136,128]{1,0:T(8,128)S(1)} %local.3.base_ref, s32[1,128]{1,0:T(1,128)S(1)} %get-tuple-element.34.count_ref, bf16[2,136,288]{2,1,0:T(8,128)(2,1)S(1)} %get-tuple-element.36.m_ref, s32[6,128]{1,0:T(8,128)S(1)} %get-tuple-element.37.where_ref, f32[24,128]{1,0:T(8,128)S(1)} %collective-permute-done.6.sub_0, ...), custom_call_target="tpu_custom_call" | custom-call | tf_op jit(solution)/shard_map/last/pallas_call | solution.py:126
  (19 shorter events, 1.1 us)
Async XLA Ops:
  2.8 19.5 %copy-start.4 = (s32[1,4,64]{2,1,0:T(4,128)S(1)}, s32[1,4,64]{2,1,0:T(4,128)}, u32[]{:S(2)}) copy-start(s32[1,4,64]{2,1,0:T(4,128)} %param.24) | copy-start | bytes 3076
  2.8 32.7 %all-to-all-start = ((f32[64,2,128]{2,1,0:T(2,128)}), f32[64,2,128]{2,1,0:T(2,128)S(1)}, u32[]{:S(2)}, u32[]{:S(2)}) async-start(f32[64,2,128]{2,1,0:T(2,128)} %payload.1), calls=%async_computation | async-start | bytes 131072 | tf_op jit(solution)/shard_map/all_to_all | solution.py:535
  37.8 15.4 %copy-start = (bf16[288,136]{1,0:T(8,128)(2,1)S(1)}, bf16[288,136]{1,0:T(8,128)(2,1)}, u32[]{:S(2)}) copy-start(bf16[288,136]{1,0:T(8,128)(2,1)} %constant.10.clone.select_ref) | copy-start | bytes 235012
  37.8 15.4 %copy-start.1 = (f32[3,27,128]{2,1,0:T(8,128)S(1)}, f32[3,27,128]{2,1,0:T(8,128)}, u32[]{:S(2)}) copy-start(f32[3,27,128]{2,1,0:T(8,128)} %node_ref.1) | copy-start | bytes 124420
  37.8 15.4 %copy-start.2 = (bf16[96,32]{1,0:T(8,128)(2,1)S(1)}, bf16[96,32]{1,0:T(8,128)(2,1)}, u32[]{:S(2)}) copy-start(bf16[96,32]{1,0:T(8,128)(2,1)} %constant.8.clone.derivs_ref) | copy-start | bytes 18436
  37.8 15.4 %all-to-all-start.1 = ((f32[8,8,2432]{2,1,0:T(8,128)}), f32[8,8,2432]{2,1,0:T(8,128)S(1)}, u32[]{:S(2)}, u32[]{:S(2)}) async-start(f32[8,8,2432]{2,1,0:T(8,128)} %compact.1), calls=%async_computation.1 | async-start | bytes 1245184 | tf_op jit(solution)/shard_map/all_to_all | solution.py:535
  42.7 10.5 %copy-start.3 = (bf16[32,8]{1,0:T(8,128)(2,1)S(1)}, bf16[32,8]{1,0:T(8,128)(2,1)}, u32[]{:S(2)}) copy-start(bf16[32,8]{1,0:T(8,128)(2,1)} %constant.9.clone.blend_ref) | copy-start | bytes 1540
  42.7 6.3 %collective-permute-start = (f32[24,128]{1,0:T(8,128)S(1)}, f32[24,128]{1,0:T(8,128)S(1)}, u32[]{:S(2)}, u32[]{:S(2)}) collective-permute-start(f32[24,128]{1,0:T(8,128)S(1)} %get-tuple-element.38), channel_id=1, source_target_pairs={{0,8},{8,0},{16,24},{24,16},{32,40},{40,32},{48,56},{56,48},{64,72... | collective-permute-start | bytes 36872 | tf_op jit(solution)/shard_map/ppermute | solution.py:530
  45.5 7.7 %collective-permute-start.1 = (f32[24,128]{1,0:T(8,128)S(1)}, f32[24,128]{1,0:T(8,128)S(1)}, u32[]{:S(2)}, u32[]{:S(2)}) collective-permute-start(f32[24,128]{1,0:T(8,128)S(1)} %get-tuple-element.39), channel_id=1, source_target_pairs={{8,16},{16,8},{24,32},{32,24},{40,48},{48,40},{56,64},{64,56},{72,... | collective-permute-start | bytes 36872 | tf_op jit(solution)/shard_map/ppermute | solution.py:530
  59.8 11.4 %collective-permute-start.2 = (f32[24,128]{1,0:T(8,128)S(1)}, f32[24,128]{1,0:T(8,128)S(1)}, u32[]{:S(2)}, u32[]{:S(2)}) collective-permute-start(f32[24,128]{1,0:T(8,128)S(1)} %get-tuple-element.46), channel_id=1, source_target_pairs={{0,1},{1,0},{2,3},{3,2},{4,5},{5,4},{6,7},{7,6},{8,9},{9,8},{10,11... | collective-permute-start | bytes 36872 | tf_op jit(solution)/shard_map/ppermute | solution.py:530
  61.7 9.5 %collective-permute-start.3 = (f32[24,128]{1,0:T(8,128)S(1)}, f32[24,128]{1,0:T(8,128)S(1)}, u32[]{:S(2)}, u32[]{:S(2)}) collective-permute-start(f32[24,128]{1,0:T(8,128)S(1)} %get-tuple-element.47), channel_id=1, source_target_pairs={{1,2},{2,1},{3,4},{4,3},{5,6},{6,5},{9,10},{10,9},{11,12},{12,11},... | collective-permute-start | bytes 36872 | tf_op jit(solution)/shard_map/ppermute | solution.py:530
  66.0 5.6 %collective-permute-start.4 = (f32[24,128]{1,0:T(8,128)S(1)}, f32[24,128]{1,0:T(8,128)S(1)}, u32[]{:S(2)}, u32[]{:S(2)}) collective-permute-start(f32[24,128]{1,0:T(8,128)S(1)} %get-tuple-element.48), channel_id=1, source_target_pairs={{0,8},{8,0},{16,24},{24,16},{32,40},{40,32},{48,56},{56,48},{64,72... | collective-permute-start | bytes 36872 | tf_op jit(solution)/shard_map/ppermute | solution.py:530
  67.9 7.7 %collective-permute-start.5 = (f32[24,128]{1,0:T(8,128)S(1)}, f32[24,128]{1,0:T(8,128)S(1)}, u32[]{:S(2)}, u32[]{:S(2)}) collective-permute-start(f32[24,128]{1,0:T(8,128)S(1)} %get-tuple-element.49), channel_id=1, source_target_pairs={{8,16},{16,8},{24,32},{32,24},{40,48},{48,40},{56,64},{64,56},{72,... | collective-permute-start | bytes 36872 | tf_op jit(solution)/shard_map/ppermute | solution.py:530
  76.7 9.3 %collective-permute-start.6 = (f32[24,128]{1,0:T(8,128)S(1)}, f32[24,128]{1,0:T(8,128)S(1)}, u32[]{:S(2)}, u32[]{:S(2)}) collective-permute-start(f32[24,128]{1,0:T(8,128)S(1)} %get-tuple-element.52), channel_id=1, source_target_pairs={{0,1},{1,0},{2,3},{3,2},{4,5},{5,4},{6,7},{7,6},{8,9},{9,8},{10,11... | collective-permute-start | bytes 36872 | tf_op jit(solution)/shard_map/ppermute | solution.py:530
  78.6 7.4 %collective-permute-start.7 = (f32[24,128]{1,0:T(8,128)S(1)}, f32[24,128]{1,0:T(8,128)S(1)}, u32[]{:S(2)}, u32[]{:S(2)}) collective-permute-start(f32[24,128]{1,0:T(8,128)S(1)} %get-tuple-element.53), channel_id=1, source_target_pairs={{1,2},{2,1},{3,4},{4,3},{5,6},{6,5},{9,10},{10,9},{11,12},{12,11},... | collective-permute-start | bytes 36872 | tf_op jit(solution)/shard_map/ppermute | solution.py:530
  80.6 5.6 %collective-permute-start.8 = (f32[24,128]{1,0:T(8,128)S(1)}, f32[24,128]{1,0:T(8,128)S(1)}, u32[]{:S(2)}, u32[]{:S(2)}) collective-permute-start(f32[24,128]{1,0:T(8,128)S(1)} %get-tuple-element.54), channel_id=1, source_target_pairs={{0,8},{8,0},{16,24},{24,16},{32,40},{40,32},{48,56},{56,48},{64,72... | collective-permute-start | bytes 36872 | tf_op jit(solution)/shard_map/ppermute | solution.py:530
  82.5 7.7 %collective-permute-start.9 = (f32[24,128]{1,0:T(8,128)S(1)}, f32[24,128]{1,0:T(8,128)S(1)}, u32[]{:S(2)}, u32[]{:S(2)}) collective-permute-start(f32[24,128]{1,0:T(8,128)S(1)} %get-tuple-element.55), channel_id=1, source_target_pairs={{8,16},{16,8},{24,32},{32,24},{40,48},{48,40},{56,64},{64,56},{72,... | collective-permute-start | bytes 36872 | tf_op jit(solution)/shard_map/ppermute | solution.py:530

commit v4 on v3

--- a/solution.py
+++ b/solution.py
@@ -13,7 +13,8 @@
 RADIUS = 1.5
 FAR = 1000.0
 LANES = 128
-STRIP = 640
+STRIP = 256
+HEAD = 640
 RUN = 768
 PACKET = 384
 TILES = 16
@@ -147,16 +148,16 @@
     out_ref[...] = jnp.broadcast_to(row_ref[0:2, :][None], out_ref.shape)
 
 
-def compact_body(in_ref, p0, p1, order_ref, out_ref, part_ref):
+def compact_body(in_ref, p0, p1, order_ref, out_ref, far_ref, part_ref):
     owners = in_ref.shape[0]
-    copies, _, room = out_ref.shape
-    room = room - PACKET
+    copies, _, near = out_ref.shape
+    near = near - PACKET
     me = lax.axis_index("sub")
     odd = me % 2 == 1
     ahead, back = jnp.where(odd, p1[...], p0[...]), jnp.where(odd, p0[...], p1[...])
     for peer in range(copies):
         for at in range(3):
-            lanes = slice(room + LANES * at, room + LANES * at + LANES)
+            lanes = slice(near + LANES * at, near + LANES * at + LANES)
             rows = slice(8 * at, 8 * at + 8)
             out_ref[peer, :, lanes] = jnp.where(peer > me, ahead[rows], back[rows])
     first, second = in_ref[:, 0, :], in_ref[:, 1, :]
@@ -176,11 +177,9 @@
     feature, group = iota((8, LANES), 0), iota((8, LANES), 1) // 32
     fold_first = flag((feature < 3) & (feature == group), BF16)
     fold_second = flag((feature > 3) & (feature < 7) & (feature == group + 4), BF16)
-    strip = min(STRIP, room)
-    slot = (iota((strip, LANES), 1) % 32).astype(F32)
-
-    def one_strip(at, carry):
-        base = min(at * strip, room - strip) if isinstance(at, int) else jnp.minimum(at * strip, room - strip)
+
+    def one_strip(base, strip, target, at):
+        slot = (iota((strip, LANES), 1) % 32).astype(F32)
         place = (iota((strip, owners), 0) + base).astype(F32)
         owner = flag((place >= low) & (place < end), BF16)
         found = jnp.dot(owner, part_ref[...], preferred_element_type=F32)
@@ -201,20 +200,29 @@
         square = jnp.sum(jnp.where(row < 3, out * out, 0.0), axis=0, keepdims=True)
         out = jnp.where(row == 3, square, out)
         out = jnp.where(row == 7, total, out)
-        out_ref[:, :, pl.ds(base if isinstance(base, int) else pl.multiple_of(base, LANES), strip)] = jnp.broadcast_to(
-            out[None], (copies, 8, strip)
-        )
-        return carry
-
-    one_strip(0, 0)
-    strips = (jnp.max(total).astype(I32) + (strip - 1)) // strip
-    lax.fori_loop(1, strips, one_strip, 0)
-
-
-def radial_displacement(z_ref, node_ref, corner_ref, hit_ref, rank_ref, list_ref, sum_ref, over_ref, over_smem, sem):
-    groups, _, room = z_ref.shape
-    room = room - PACKET
-    run = min(RUN, room)
+        target[:, :, at : at + strip] = jnp.broadcast_to(out[None], (copies, 8, strip))
+
+    head = min(HEAD, near)
+    one_strip(0, head, out_ref, 0)
+    if head < near or far_ref is not None:
+        count = jnp.max(total)
+    if head < near:
+
+        @pl.when(count > head)
+        def second():
+            one_strip(head, near - head, out_ref, head)
+
+    if far_ref is not None:
+        for at in range(0, far_ref.shape[2], STRIP):
+
+            @pl.when(count > near + at)
+            def further(at=at):
+                one_strip(near + at, min(STRIP, far_ref.shape[2] - at), far_ref, at)
+
+
+def radial_displacement(z_ref, far_ref, node_ref, corner_ref, hit_ref, rank_ref, list_ref, sum_ref, over_ref, over_smem, sem):
+    groups, _, run = z_ref.shape
+    run = run - PACKET
     blocks = run // LANES
     at = [[node_ref[i, k : k + 1, :] for k in CORNERS] for i in range(3)]
     middle, reach = [], [None] * 8
@@ -253,8 +261,8 @@
     )
     half = iota((TILES, LANES), 1) // 64
 
-    def extract(g, start, block, shift):
-        points = z_ref[g, :, pl.ds(pl.multiple_of(start + block * LANES, LANES), LANES)]
+    def extract(source, g, start, block, shift):
+        points = source[g, :, pl.ds(pl.multiple_of(start + block * LANES, LANES), LANES)]
         three = jnp.concatenate([p.astype(F32) for p in pieces(points, 3)], axis=0).astype(BF16)
         rank = rank_ref[pl.ds(pl.multiple_of((g * blocks + block) * TILES, TILES), TILES), :]
         entries = []
@@ -266,18 +274,16 @@
             entries.append(jnp.where(iota((8, LANES), 0) < 4, found * (1.0 / RADIUS), found * 4.0))
         return entries
 
-    def one_part(part, carry):
-        first = part * run
-        start = jnp.minimum(first, room - run)
+    def one_part(source, first, start, ahead):
         for g in range(groups):
-            points = z_ref[g, :, pl.ds(pl.multiple_of(start, LANES), run)]
+            points = source[g, :, pl.ds(pl.multiple_of(start, LANES), run)]
             high, low = pieces(points, 2)
             both = jnp.concatenate([high.astype(F32), low.astype(F32), high.astype(F32)], axis=0)
             gap = jnp.dot(probe, both.astype(BF16), preferred_element_type=F32) + offset
             best = gap[0:TILES]
             for e in range(1, 8):
                 best = jnp.minimum(best, gap[TILES * e : TILES * e + TILES])
-            lane = iota((TILES, run), 1) + start
+            lane = iota((TILES, run), 1) + (ahead + start)
             hit = flag((best <= 0.0) & (lane >= first) & (lane < counts[g]))
             for b in range(blocks):
                 hit_ref[(g * blocks + b) * TILES : (g * blocks + b + 1) * TILES, :] = hit[:, LANES * b : LANES * b + LANES]
@@ -291,9 +297,9 @@
         copy.start()
         length = jnp.int32(0)
         for g in range(groups):
-            inside = jnp.clip(counts[g] - start, 0, run)
+            inside = jnp.clip(counts[g] - (ahead + start), 0, run)
             for b in range(blocks):
-                one, two = extract(g, start, b, 0.0)
+                one, two = extract(source, g, start, b, 0.0)
                 list_ref[length] = one
                 length = length + jnp.where(inside > LANES * b, 1, 0)
                 list_ref[length] = two
@@ -303,7 +309,7 @@
                 g, b = index // blocks, index % blocks
 
                 def round_more(r, length):
-                    one, two = extract(g, start, b, (r * SLOTS).astype(F32))
+                    one, two = extract(source, g, start, b, (r * SLOTS).astype(F32))
                     list_ref[length] = one
                     length = length + jnp.where(over_smem[index, 0] > r * SLOTS, 1, 0)
                     list_ref[length] = two
@@ -313,7 +319,11 @@
                 rounds = (jnp.maximum(over_smem[index, 0], over_smem[index, 1]) + SLOTS - 1) // SLOTS
                 return lax.fori_loop(1, rounds, round_more, length)
 
-            return lax.fori_loop(0, groups * blocks, block_more, length)
+            for g in range(groups):
+                crowd = [over_smem[g * blocks + b, h] for b in range(blocks) for h in range(2)]
+                last = jnp.where(functools.reduce(jnp.maximum, crowd) > SLOTS, blocks, 0)
+                length = lax.fori_loop(g * blocks, g * blocks + last, block_more, length)
+            return length
 
         def four(step, carry):
             for i in range(2):
@@ -346,9 +356,16 @@
         def crowded():
             evaluate(more(jnp.int32(0)))
 
-        return carry
-
-    lax.fori_loop(0, (most + (run - 1)) // run, one_part, 0)
+    one_part(z_ref, 0, 0, 0)
+    if far_ref is not None:
+        step = min(run, far_ref.shape[2])
+
+        def far_part(part, carry):
+            first = (part - 1) * step
+            one_part(far_ref, run + first, jnp.minimum(first, far_ref.shape[2] - step), run)
+            return carry
+
+        lax.fori_loop(1, 1 + (jnp.maximum(most - run, 0) + (step - 1)) // step, far_part, 0)
     spread = flag(iota((LANES, LANES), 0) % TILES == iota((LANES, LANES), 1) % TILES, BF16)
     own = iota((8, LANES), 0) == iota((8, LANES), 1) // TILES
     out = []
@@ -365,11 +382,15 @@
 
 
 def radial_body(
-    z_ref, node_ref, derivs_ref, blend_ref, base_ref, start_ref, minus_inv_ref, count_ref, select_ref, send_ref,
+    z_ref, far_ref, node_any, derivs_any, blend_any, base_ref, start_ref, minus_inv_ref, count_ref, select_any, send_ref,
     m_ref, where_ref, elem_0, elem_1,
     disp_ref, metric_ref, state_ref, trace_ref, p0, p1, p2, p3,
-    corner_ref, hit_ref, rank_ref, list_ref, sum_ref, over_ref, over_smem, sem, nodes_ref, shift_ref, out_sem,
+    corner_ref, hit_ref, rank_ref, list_ref, sum_ref, over_ref, over_smem, sem, nodes_ref, shift_ref, out_sem, node_ref, derivs_ref, blend_ref, select_ref, in_sems,
 ):
+    moves = ((node_any, node_ref), (blend_any, blend_ref), (derivs_any, derivs_ref), (select_any, select_ref))
+    copies = [pltpu.make_async_copy(a, b, in_sems.at[k]) for k, (a, b) in enumerate(moves)]
+    for copy in copies:
+        copy.start()
     packet_refs = (p0, p1, p2, p3)
     me, last = lax.axis_index("sub"), z_ref.shape[0] - 1
     sides = []
@@ -378,9 +399,12 @@
         rows = [z_ref[peer, :, z_ref.shape[2] - PACKET + LANES * at :][:, 0:LANES] for at in range(3)]
         sides.append(jnp.where(there, jnp.concatenate(rows, axis=0), 0.0))
     base = base_ref[...] + from_neighbours(*sides, *in_line("elem", elem_0[...], elem_1[...]), where_ref, m_ref)
+    copies[0].wait()
     corner = radial_displacement(
-        z_ref, node_ref, corner_ref, hit_ref, rank_ref, list_ref, sum_ref, over_ref, over_smem, sem
+        z_ref, far_ref, node_ref, corner_ref, hit_ref, rank_ref, list_ref, sum_ref, over_ref, over_smem, sem
     )
+    for copy in copies[1:]:
+        copy.wait()
     nodes_ref[...] = jnp.zeros_like(nodes_ref)
     for i in range(3):
         shift = pick_dot(blend_ref[...], corner[i], 2)
@@ -463,12 +487,13 @@
     flat_ref, wide_ref,
 ):
     held_ref[...] = jnp.broadcast_to(count_ref[...], held_ref.shape)
-    sent_ref[...] = send_ref[...]
+    for q in range(4):
+        sent_ref[q // 2 : q // 2 + 1, 64 * (q % 2) : 64 * (q % 2) + 64] = send_ref[0, q : q + 1, :]
     link_ref[...] = where_ref[...]
     flat_ref[...] = jnp.zeros_like(flat_ref)
     for v in range(5):
         flat_ref[27 * v : 27 * v + 27, :] = u_ref[v]
-    finish(flat_ref[...], held_ref, select_ref, send_ref, state_ref, trace_ref, (p0, p1, p2, p3))
+    finish(flat_ref[...], held_ref, select_ref, sent_ref, state_ref, trace_ref, (p0, p1, p2, p3))
     wide_ref[...] = jnp.zeros_like(wide_ref)
     wide_ref[0:135, 0:135] = inv_ref[...]
     inverse = wide_ref[:, 0:136]
@@ -535,13 +560,13 @@
     return lax.all_to_all(copies, axis, split_axis=0, concat_axis=0, tiled=True)
 
 
-def radial_call(points, node_ref, derivs, blending, base, state, minus, elem_count, select, send, coupling, face_link, received):
-    groups, _, room = points.shape
-    blocks = min(RUN, room - PACKET) // LANES * groups
+def radial_call(points, far, node_ref, derivs, blending, base, state, minus, elem_count, select, send, coupling, face_link, received):
+    groups, _, run = points.shape
+    blocks = (run - PACKET) // LANES * groups
     return call(
         radial_body,
         [shape_of(3, 27, LANES), shape_of(136, LANES), *STATE],
-        [VMEM] * 14,
+        [VMEM, VMEM, None, None, None, VMEM, VMEM, VMEM, VMEM, None, VMEM, VMEM, VMEM, VMEM, VMEM],
         [
             pltpu.VMEM((3, 64, LANES), F32),
             pltpu.VMEM((blocks * TILES, LANES), F32),
@@ -554,12 +579,18 @@
             pltpu.VMEM((32, 3 * LANES), F32),
             pltpu.VMEM((3, 27, LANES), F32),
             pltpu.SemaphoreType.DMA,
+            pltpu.VMEM(node_ref.shape, F32),
+            pltpu.VMEM(derivs.shape, BF16),
+            pltpu.VMEM(blending.shape, BF16),
+            pltpu.VMEM(select.shape, BF16),
+            pltpu.SemaphoreType.DMA((4,)),
         ],
+        in_specs=[pl.BlockSpec(memory_space=pl.ANY if k in (2, 3, 4, 9) else VMEM) for k in range(15)],
         held=[False] + [True] * 7,
         out_specs=[pl.BlockSpec(memory_space=pl.ANY)] + [pl.BlockSpec(memory_space=VMEM)] * 7,
         name="radial",
     )(
-        points, node_ref, derivs, blending, base, state, minus, elem_count, select, send,
+        points, far, node_ref, derivs, blending, base, state, minus, elem_count, select, send,
         coupling, face_link, *received,
     )
 
@@ -573,7 +604,6 @@
     select, place = jnp.asarray(select, BF16), jnp.asarray(place, BF16)
     n_elem, n_sub = lax.axis_size("elem"), lax.axis_size("sub")
     room = n_elem * cp_pos.shape[1]
-    send = send_list.reshape(2, LANES)
 
     copies = call(
         payload_body, shape_of(n_elem, 2, LANES), [None] * 3, [pltpu.VMEM((8, LANES), F32)], name="payload"
@@ -590,20 +620,22 @@
         [pltpu.VMEM((136, LANES), F32), pltpu.VMEM((136, 256), F32)],
         name="setup",
     )(
-        u_prev, elem_count.reshape(1, 1), select, send, vol_block, block_inv, lift_matrix, place, right_side, face_link
+        u_prev, elem_count.reshape(1, 1), select, send_list, vol_block, block_inv, lift_matrix, place, right_side, face_link
     )
     state, traces, *packets = first
-    gathered = call(
+    near = min(RUN, room)
+    gathered, rest = call(
         compact_body,
-        shape_of(n_sub, 8, room + PACKET),
+        [shape_of(n_sub, 8, near + PACKET), shape_of(n_sub, 8, max(room - near, near))],
         [VMEM] * 4,
         [pltpu.VMEM((n_elem, 7 * LANES), BF16)],
         name="compact",
     )(mine, packets[0], packets[1], base)
     points = spread(gathered, "sub")
     received = exchange(packets, ("elem",))
+    far = lax.cond(jnp.max(points[:, 7, 0]) > near, lambda x: spread(x, "sub"), lambda x: x, rest)
     displacement, metric, state, traces, *packets = radial_call(
-        points, node_ref, derivs, blending, base, state, minus, held_count, select, sent,
+        points, far, node_ref, derivs, blending, base, state, minus, held_count, select, sent,
         coupling, link, received,
     )
     for sweep in range(1, ITERS):

time: 92.7 us -> 91.8 us (level)
  waiting for transfers between devices: 22 us -> 19.9 us
  Pallas kernels: 17.3 us -> 18.4 us
    ppermute x10, waiting for transfers between devices: 12.8 us -> 9.99 us  [exchange(): out.append(lax.ppermute(packets[first + turn], axis, pairs))]
    pallas_call x8, Pallas kernels: 17.3 us -> 18.4 us  [placed(): run(*[a if s is None else pltpu.with_memory_space_constraint(a, s) for a,...]
  transfers between devices with their start and end apart: 12 -> 12, of which waited for: 6 -> 4; matrix products, arithmetic and copies ran while one was open for 1% -> 1% of each run, Pallas kernels for 5% -> 5%
where the time goes in v4:
time: 91.8 us; the launch traced here: 91.1 us
  starting transfers between devices  49.4 us (54%)
  waiting for transfers between devices  19.9 us (22%)
  Pallas kernels  18.4 us (20%)
  between operations  2.77 us (3%)
    ppermute x10, starting transfers between devices, exchange(): out.append(lax.ppermute(packets[first + turn], axis, pairs))  25.9 us
    all_to_all x2, starting transfers between devices, spread(): return lax.all_to_all(copies, axis, split_axis=0, concat_axis=0, tiled=True)  23.5 us
    pallas_call x8, Pallas kernels, placed(): run(*[a if s is None else pltpu.with_memory_space_constraint(a, s) for a,...  18.4 us
    ppermute x10, waiting for transfers between devices, exchange(): out.append(lax.ppermute(packets[first + turn], axis, pairs))  9.99 us
    all_to_all x2, waiting for transfers between devices, spread(): return lax.all_to_all(copies, axis, split_axis=0, concat_axis=0, tiled=True)  9.91 us
  transfers between devices with their start and end apart: 12, of which 4 were waited for; matrix products, arithmetic and copies ran while one was open for 1% of the time, Pallas kernels for 5%

profile of v4, /device:TPU:14, one launch (start us, length us, event | category | flops | bytes accessed | tf_op | source)
XLA Modules:
  0.0 91.1 jit_solution(12054870321673445934)
XLA Ops:
  1.3 1.5 %payload.1 = f32[64,2,128]{2,1,0:T(2,128)} custom-call(s32[1,1]{1,0:T(1,128)} %bitcast.2.count_ref, f32[3,32]{1,0:T(4,128)} %pos_ref.1, f32[3,32]{1,0:T(4,128)} %coef_ref.1), custom_call_target="tpu_custom_call" | custom-call | tf_op jit(solution)/shard_map/payload/pallas_call | solution.py:127
  2.8 18.7 %all-to-all-start.1 = ((f32[64,2,128]{2,1,0:T(2,128)}), f32[64,2,128]{2,1,0:T(2,128)S(1)}, u32[]{:S(2)}, u32[]{:S(2)}) async-start(f32[64,2,128]{2,1,0:T(2,128)} %payload.1), calls=%async_computation.1 | async-start | bytes 131072 | tf_op jit(solution)/shard_map/all_to_all | solution.py:560
  22.2 3.2 %setup.1 = (f32[136,128]{1,0:T(8,128)S(1)}, f32[6,48,128]{2,1,0:T(8,128)}, f32[24,128]{1,0:T(8,128)S(1)}, f32[24,128]{1,0:T(8,128)S(1)}, f32[24,128]{1,0:T(8,128...) custom-call(f32[5,27,128]{2,1,0:T(8,128)} %u_ref.1, ...), custom_call_target="tpu_custom_call" | custom-call | tf_op jit(solution)/shard_map/setup/pallas_call | solution.py:127
  25.4 9.9 %all-to-all-done.1.in_ref = f32[64,2,128]{2,1,0:T(2,128)S(1)} async-done(((f32[64,2,128]{2,1,0:T(2,128)}), f32[64,2,128]{2,1,0:T(2,128)S(1)}, u32[]{:S(2)}, u32[]{:S(2)}) %all-to-all-start.1) | async-done | bytes 65568 | tf_op jit(solution)/shard_map/all_to_all | solution.py:560
  35.3 2.3 %compact.1 = (f32[8,8,1152]{2,1,0:T(8,128)}, f32[8,8,1280]{2,1,0:T(8,128)S(1)}) custom-call(f32[64,2,128]{2,1,0:T(2,128)S(1)} %all-to-all-done.1.in_ref, f32[24,128]{1,0:T(8,128)S(1)} %get-tuple-element.36.p0, f32[24,128]{1,0:T(8,128)S(1)} %get-tuple-element.37.p1, f32[136,128]{1,0:T(8,128)S(1)} %get-tuple-element.38.order_ref.base_ref), custom_call_target="tpu_custom_call" | custom-call | tf_op jit(solution)/shard_map/compact/pallas_call | solution.py:127
  37.6 4.8 %all-to-all-start.2 = ((f32[8,8,1152]{2,1,0:T(8,128)}), f32[8,8,1152]{2,1,0:T(8,128)S(1)}, u32[]{:S(2)}, u32[]{:S(2)}) async-start(f32[8,8,1152]{2,1,0:T(8,128)} %get-tuple-element.39), calls=%async_computation.2 | async-start | bytes 589824 | tf_op jit(solution)/shard_map/all_to_all | solution.py:560
  42.3 2.6 %collective-permute-start = (f32[24,128]{1,0:T(8,128)S(1)}, f32[24,128]{1,0:T(8,128)S(1)}, u32[]{:S(2)}, u32[]{:S(2)}) collective-permute-start(f32[24,128]{1,0:T(8,128)S(1)} %get-tuple-element.47), channel_id=1, source_target_pairs={{0,8},{8,0},{16,24},{24,16},{32,40},{40,32},{48,56},{56,48},{64,72... | collective-permute-start | bytes 36872 | tf_op jit(solution)/shard_map/ppermute | solution.py:555
  45.0 3.5 %collective-permute-start.1 = (f32[24,128]{1,0:T(8,128)S(1)}, f32[24,128]{1,0:T(8,128)S(1)}, u32[]{:S(2)}, u32[]{:S(2)}) collective-permute-start(f32[24,128]{1,0:T(8,128)S(1)} %get-tuple-element.48), channel_id=1, source_target_pairs={{8,16},{16,8},{24,32},{32,24},{40,48},{48,40},{56,64},{64,56},{72,... | collective-permute-start | bytes 36872 | tf_op jit(solution)/shard_map/ppermute | solution.py:555
  49.8 2.9 %collective-permute-done.1.elem_1 = f32[24,128]{1,0:T(8,128)S(1)} collective-permute-done((f32[24,128]{1,0:T(8,128)S(1)}, f32[24,128]{1,0:T(8,128)S(1)}, u32[]{:S(2)}, u32[]{:S(2)}) %collective-permute-start.1) | collective-permute-done | bytes 12320 | tf_op jit(solution)/shard_map/ppermute | solution.py:555
  52.7 7.8 %radial.1 = (f32[3,27,128]{2,1,0:T(8,128)}, f32[136,128]{1,0:T(8,128)S(1)}, f32[136,128]{1,0:T(8,128)S(1)}, f32[6,48,128]{2,1,0:T(8,128)S(1)}, f32[24,128]{1,0:T...) custom-call(f32[8,8,1152]{2,1,0:T(8,128)S(1)} %all-to-all-done.2.z_ref, ...), custom_call_target="tpu_custom_call" | custom-call | tf_op jit(solution)/shard_map/radial/pallas_call | solution.py:127
  60.4 2.1 %collective-permute-start.2 = (f32[24,128]{1,0:T(8,128)S(1)}, f32[24,128]{1,0:T(8,128)S(1)}, u32[]{:S(2)}, u32[]{:S(2)}) collective-permute-start(f32[24,128]{1,0:T(8,128)S(1)} %get-tuple-element.55), channel_id=1, source_target_pairs={{0,1},{1,0},{2,3},{3,2},{4,5},{5,4},{6,7},{7,6},{8,9},{9,8},{10,11... | collective-permute-start | bytes 36872 | tf_op jit(solution)/shard_map/ppermute | solution.py:555
  62.5 2.3 %collective-permute-start.3 = (f32[24,128]{1,0:T(8,128)S(1)}, f32[24,128]{1,0:T(8,128)S(1)}, u32[]{:S(2)}, u32[]{:S(2)}) collective-permute-start(f32[24,128]{1,0:T(8,128)S(1)} %get-tuple-element.56), channel_id=1, source_target_pairs={{1,2},{2,1},{3,4},{4,3},{5,6},{6,5},{9,10},{10,9},{11,12},{12,11},... | collective-permute-start | bytes 36872 | tf_op jit(solution)/shard_map/ppermute | solution.py:555
  64.9 1.9 %collective-permute-start.4 = (f32[24,128]{1,0:T(8,128)S(1)}, f32[24,128]{1,0:T(8,128)S(1)}, u32[]{:S(2)}, u32[]{:S(2)}) collective-permute-start(f32[24,128]{1,0:T(8,128)S(1)} %get-tuple-element.57), channel_id=1, source_target_pairs={{0,8},{8,0},{16,24},{24,16},{32,40},{40,32},{48,56},{56,48},{64,72... | collective-permute-start | bytes 36872 | tf_op jit(solution)/shard_map/ppermute | solution.py:555
  66.8 3.5 %collective-permute-start.5 = (f32[24,128]{1,0:T(8,128)S(1)}, f32[24,128]{1,0:T(8,128)S(1)}, u32[]{:S(2)}, u32[]{:S(2)}) collective-permute-start(f32[24,128]{1,0:T(8,128)S(1)} %get-tuple-element.58), channel_id=1, source_target_pairs={{8,16},{16,8},{24,32},{32,24},{40,48},{48,40},{56,64},{64,56},{72,... | collective-permute-start | bytes 36872 | tf_op jit(solution)/shard_map/ppermute | solution.py:555
  70.3 0.6 local.2.base_ref
  71.0 3.5 %collective-permute-done.5.elem_1 = f32[24,128]{1,0:T(8,128)S(1)} collective-permute-done((f32[24,128]{1,0:T(8,128)S(1)}, f32[24,128]{1,0:T(8,128)S(1)}, u32[]{:S(2)}, u32[]{:S(2)}) %collective-permute-start.5) | collective-permute-done | bytes 12320 | tf_op jit(solution)/shard_map/ppermute | solution.py:555
  74.5 1.1 %sweep.1 = (f32[136,128]{1,0:T(8,128)S(1)}, f32[6,48,128]{2,1,0:T(8,128)S(1)}, f32[24,128]{1,0:T(8,128)S(1)}, f32[24,128]{1,0:T(8,128)S(1)}, f32[24,128]{1,0:T(8,128)S(1)}, /*index=5*/f32[24,128]{1,0:T(8,128)S(1)}) custom-call(f32[136,128]{1,0:T(8,128)S(1)} %local.2.base_ref, s32[1,128]{1,0:T(1,128)S(1)} %get-tuple-element.43.count_ref, ...), custom_call_target="tpu_custom_call" | custom-call | tf_op jit(solution)/shard_map/sweep/pallas_call | solution.py:127
  75.6 1.9 %collective-permute-start.6 = (f32[24,128]{1,0:T(8,128)S(1)}, f32[24,128]{1,0:T(8,128)S(1)}, u32[]{:S(2)}, u32[]{:S(2)}) collective-permute-start(f32[24,128]{1,0:T(8,128)S(1)} %get-tuple-element.61), channel_id=1, source_target_pairs={{0,1},{1,0},{2,3},{3,2},{4,5},{5,4},{6,7},{7,6},{8,9},{9,8},{10,11... | collective-permute-start | bytes 36872 | tf_op jit(solution)/shard_map/ppermute | solution.py:555
  77.6 2.6 %collective-permute-start.7 = (f32[24,128]{1,0:T(8,128)S(1)}, f32[24,128]{1,0:T(8,128)S(1)}, u32[]{:S(2)}, u32[]{:S(2)}) collective-permute-start(f32[24,128]{1,0:T(8,128)S(1)} %get-tuple-element.62), channel_id=1, source_target_pairs={{1,2},{2,1},{3,4},{4,3},{5,6},{6,5},{9,10},{10,9},{11,12},{12,11},... | collective-permute-start | bytes 36872 | tf_op jit(solution)/shard_map/ppermute | solution.py:555
  80.2 1.9 %collective-permute-start.8 = (f32[24,128]{1,0:T(8,128)S(1)}, f32[24,128]{1,0:T(8,128)S(1)}, u32[]{:S(2)}, u32[]{:S(2)}) collective-permute-start(f32[24,128]{1,0:T(8,128)S(1)} %get-tuple-element.63), channel_id=1, source_target_pairs={{0,8},{8,0},{16,24},{24,16},{32,40},{40,32},{48,56},{56,48},{64,72... | collective-permute-start | bytes 36872 | tf_op jit(solution)/shard_map/ppermute | solution.py:555
  82.1 3.5 %collective-permute-start.9 = (f32[24,128]{1,0:T(8,128)S(1)}, f32[24,128]{1,0:T(8,128)S(1)}, u32[]{:S(2)}, u32[]{:S(2)}) collective-permute-start(f32[24,128]{1,0:T(8,128)S(1)} %get-tuple-element.64), channel_id=1, source_target_pairs={{8,16},{16,8},{24,32},{32,24},{40,48},{48,40},{56,64},{64,56},{72,... | collective-permute-start | bytes 36872 | tf_op jit(solution)/shard_map/ppermute | solution.py:555
  85.6 0.6 local.3.base_ref
  86.2 3.5 %collective-permute-done.9.elem_1 = f32[24,128]{1,0:T(8,128)S(1)} collective-permute-done((f32[24,128]{1,0:T(8,128)S(1)}, f32[24,128]{1,0:T(8,128)S(1)}, u32[]{:S(2)}, u32[]{:S(2)}) %collective-permute-start.9) | collective-permute-done | bytes 12320 | tf_op jit(solution)/shard_map/ppermute | solution.py:555
  89.8 1.3 %last.1 = f32[5,27,128]{2,1,0:T(8,128)} custom-call(f32[136,128]{1,0:T(8,128)S(1)} %local.3.base_ref, s32[1,128]{1,0:T(1,128)S(1)} %get-tuple-element.43.count_ref, bf16[2,136,288]{2,1,0:T(8,128)(2,1)S(1)} %get-tuple-element.45.m_ref, s32[6,128]{1,0:T(8,128)S(1)} %get-tuple-element.46.where_ref, f32[24,128]{1,0:T(8,128)S(1)} %collective-permute-done.6.sub_0, ...), custom_call_target="tpu_custom_call" | custom-call | tf_op jit(solution)/shard_map/last/pallas_call | solution.py:127
  (12 shorter events, 0.6 us)
Async XLA Ops:
  2.8 32.5 %all-to-all-start.1 = ((f32[64,2,128]{2,1,0:T(2,128)}), f32[64,2,128]{2,1,0:T(2,128)S(1)}, u32[]{:S(2)}, u32[]{:S(2)}) async-start(f32[64,2,128]{2,1,0:T(2,128)} %payload.1), calls=%async_computation.1 | async-start | bytes 131072 | tf_op jit(solution)/shard_map/all_to_all | solution.py:560
  37.6 10.9 %all-to-all-start.2 = ((f32[8,8,1152]{2,1,0:T(8,128)}), f32[8,8,1152]{2,1,0:T(8,128)S(1)}, u32[]{:S(2)}, u32[]{:S(2)}) async-start(f32[8,8,1152]{2,1,0:T(8,128)} %get-tuple-element.39), calls=%async_computation.2 | async-start | bytes 589824 | tf_op jit(solution)/shard_map/all_to_all | solution.py:560
  42.3 7.4 %collective-permute-start = (f32[24,128]{1,0:T(8,128)S(1)}, f32[24,128]{1,0:T(8,128)S(1)}, u32[]{:S(2)}, u32[]{:S(2)}) collective-permute-start(f32[24,128]{1,0:T(8,128)S(1)} %get-tuple-element.47), channel_id=1, source_target_pairs={{0,8},{8,0},{16,24},{24,16},{32,40},{40,32},{48,56},{56,48},{64,72... | collective-permute-start | bytes 36872 | tf_op jit(solution)/shard_map/ppermute | solution.py:555
  45.0 7.7 %collective-permute-start.1 = (f32[24,128]{1,0:T(8,128)S(1)}, f32[24,128]{1,0:T(8,128)S(1)}, u32[]{:S(2)}, u32[]{:S(2)}) collective-permute-start(f32[24,128]{1,0:T(8,128)S(1)} %get-tuple-element.48), channel_id=1, source_target_pairs={{8,16},{16,8},{24,32},{32,24},{40,48},{48,40},{56,64},{64,56},{72,... | collective-permute-start | bytes 36872 | tf_op jit(solution)/shard_map/ppermute | solution.py:555
  60.4 10.5 %collective-permute-start.2 = (f32[24,128]{1,0:T(8,128)S(1)}, f32[24,128]{1,0:T(8,128)S(1)}, u32[]{:S(2)}, u32[]{:S(2)}) collective-permute-start(f32[24,128]{1,0:T(8,128)S(1)} %get-tuple-element.55), channel_id=1, source_target_pairs={{0,1},{1,0},{2,3},{3,2},{4,5},{5,4},{6,7},{7,6},{8,9},{9,8},{10,11... | collective-permute-start | bytes 36872 | tf_op jit(solution)/shard_map/ppermute | solution.py:555
  62.5 8.4 %collective-permute-start.3 = (f32[24,128]{1,0:T(8,128)S(1)}, f32[24,128]{1,0:T(8,128)S(1)}, u32[]{:S(2)}, u32[]{:S(2)}) collective-permute-start(f32[24,128]{1,0:T(8,128)S(1)} %get-tuple-element.56), channel_id=1, source_target_pairs={{1,2},{2,1},{3,4},{4,3},{5,6},{6,5},{9,10},{10,9},{11,12},{12,11},... | collective-permute-start | bytes 36872 | tf_op jit(solution)/shard_map/ppermute | solution.py:555
  64.9 6.1 %collective-permute-start.4 = (f32[24,128]{1,0:T(8,128)S(1)}, f32[24,128]{1,0:T(8,128)S(1)}, u32[]{:S(2)}, u32[]{:S(2)}) collective-permute-start(f32[24,128]{1,0:T(8,128)S(1)} %get-tuple-element.57), channel_id=1, source_target_pairs={{0,8},{8,0},{16,24},{24,16},{32,40},{40,32},{48,56},{56,48},{64,72... | collective-permute-start | bytes 36872 | tf_op jit(solution)/shard_map/ppermute | solution.py:555
  66.8 7.7 %collective-permute-start.5 = (f32[24,128]{1,0:T(8,128)S(1)}, f32[24,128]{1,0:T(8,128)S(1)}, u32[]{:S(2)}, u32[]{:S(2)}) collective-permute-start(f32[24,128]{1,0:T(8,128)S(1)} %get-tuple-element.58), channel_id=1, source_target_pairs={{8,16},{16,8},{24,32},{32,24},{40,48},{48,40},{56,64},{64,56},{72,... | collective-permute-start | bytes 36872 | tf_op jit(solution)/shard_map/ppermute | solution.py:555
  70.3 4.2 %copy-start = (bf16[288,136]{1,0:T(8,128)(2,1)S(1)}, bf16[288,136]{1,0:T(8,128)(2,1)}, u32[]{:S(2)}) copy-start(bf16[288,136]{1,0:T(8,128)(2,1)} %constant.14.clone.select_ref.select_any) | copy-start | bytes 235012
  75.6 10.6 %collective-permute-start.6 = (f32[24,128]{1,0:T(8,128)S(1)}, f32[24,128]{1,0:T(8,128)S(1)}, u32[]{:S(2)}, u32[]{:S(2)}) collective-permute-start(f32[24,128]{1,0:T(8,128)S(1)} %get-tuple-element.61), channel_id=1, source_target_pairs={{0,1},{1,0},{2,3},{3,2},{4,5},{5,4},{6,7},{7,6},{8,9},{9,8},{10,11... | collective-permute-start | bytes 36872 | tf_op jit(solution)/shard_map/ppermute | solution.py:555
  77.6 8.7 %collective-permute-start.7 = (f32[24,128]{1,0:T(8,128)S(1)}, f32[24,128]{1,0:T(8,128)S(1)}, u32[]{:S(2)}, u32[]{:S(2)}) collective-permute-start(f32[24,128]{1,0:T(8,128)S(1)} %get-tuple-element.62), channel_id=1, source_target_pairs={{1,2},{2,1},{3,4},{4,3},{5,6},{6,5},{9,10},{10,9},{11,12},{12,11},... | collective-permute-start | bytes 36872 | tf_op jit(solution)/shard_map/ppermute | solution.py:555
  80.2 6.1 %collective-permute-start.8 = (f32[24,128]{1,0:T(8,128)S(1)}, f32[24,128]{1,0:T(8,128)S(1)}, u32[]{:S(2)}, u32[]{:S(2)}) collective-permute-start(f32[24,128]{1,0:T(8,128)S(1)} %get-tuple-element.63), channel_id=1, source_target_pairs={{0,8},{8,0},{16,24},{24,16},{32,40},{40,32},{48,56},{56,48},{64,72... | collective-permute-start | bytes 36872 | tf_op jit(solution)/shard_map/ppermute | solution.py:555
  82.1 7.7 %collective-permute-start.9 = (f32[24,128]{1,0:T(8,128)S(1)}, f32[24,128]{1,0:T(8,128)S(1)}, u32[]{:S(2)}, u32[]{:S(2)}) collective-permute-start(f32[24,128]{1,0:T(8,128)S(1)} %get-tuple-element.64), channel_id=1, source_target_pairs={{8,16},{16,8},{24,32},{32,24},{40,48},{48,40},{56,64},{64,56},{72,... | collective-permute-start | bytes 36872 | tf_op jit(solution)/shard_map/ppermute | solution.py:555

commit v5 on v4

--- a/solution.py
+++ b/solution.py
@@ -382,15 +382,11 @@
 
 
 def radial_body(
-    z_ref, far_ref, node_any, derivs_any, blend_any, base_ref, start_ref, minus_inv_ref, count_ref, select_any, send_ref,
+    z_ref, far_ref, node_ref, derivs_ref, blend_ref, base_ref, start_ref, minus_inv_ref, count_ref, select_ref, send_ref,
     m_ref, where_ref, elem_0, elem_1,
     disp_ref, metric_ref, state_ref, trace_ref, p0, p1, p2, p3,
-    corner_ref, hit_ref, rank_ref, list_ref, sum_ref, over_ref, over_smem, sem, nodes_ref, shift_ref, out_sem, node_ref, derivs_ref, blend_ref, select_ref, in_sems,
+    corner_ref, hit_ref, rank_ref, list_ref, sum_ref, over_ref, over_smem, sem, nodes_ref, shift_ref, out_sem,
 ):
-    moves = ((node_any, node_ref), (blend_any, blend_ref), (derivs_any, derivs_ref), (select_any, select_ref))
-    copies = [pltpu.make_async_copy(a, b, in_sems.at[k]) for k, (a, b) in enumerate(moves)]
-    for copy in copies:
-        copy.start()
     packet_refs = (p0, p1, p2, p3)
     me, last = lax.axis_index("sub"), z_ref.shape[0] - 1
     sides = []
@@ -399,12 +395,9 @@
         rows = [z_ref[peer, :, z_ref.shape[2] - PACKET + LANES * at :][:, 0:LANES] for at in range(3)]
         sides.append(jnp.where(there, jnp.concatenate(rows, axis=0), 0.0))
     base = base_ref[...] + from_neighbours(*sides, *in_line("elem", elem_0[...], elem_1[...]), where_ref, m_ref)
-    copies[0].wait()
     corner = radial_displacement(
         z_ref, far_ref, node_ref, corner_ref, hit_ref, rank_ref, list_ref, sum_ref, over_ref, over_smem, sem
     )
-    for copy in copies[1:]:
-        copy.wait()
     nodes_ref[...] = jnp.zeros_like(nodes_ref)
     for i in range(3):
         shift = pick_dot(blend_ref[...], corner[i], 2)
@@ -482,14 +475,19 @@
 
 
 def setup_body(
-    u_ref, count_ref, select_ref, send_ref, vol_ref, inv_ref, lift_ref, place_ref, right_ref, where_ref,
-    state_ref, trace_ref, p0, p1, p2, p3, held_ref, sent_ref, link_ref, minus_ref, both_ref, m_ref, const_ref, base_ref,
+    u_ref, count_ref, select_in, send_ref, vol_ref, inv_ref, lift_ref, place_ref, right_ref, where_ref,
+    node_in, derivs_in, blend_in,
+    state_ref, trace_ref, p0, p1, p2, p3, held_ref, sent_ref, link_ref, node_ref, derivs_ref, blend_ref, select_ref, minus_ref, both_ref, m_ref, const_ref, base_ref,
     flat_ref, wide_ref,
 ):
     held_ref[...] = jnp.broadcast_to(count_ref[...], held_ref.shape)
     for q in range(4):
         sent_ref[q // 2 : q // 2 + 1, 64 * (q % 2) : 64 * (q % 2) + 64] = send_ref[0, q : q + 1, :]
     link_ref[...] = where_ref[...]
+    node_ref[...] = node_in[...]
+    derivs_ref[...] = derivs_in[...]
+    blend_ref[...] = blend_in[...]
+    select_ref[...] = select_in[...]
     flat_ref[...] = jnp.zeros_like(flat_ref)
     for v in range(5):
         flat_ref[27 * v : 27 * v + 27, :] = u_ref[v]
@@ -566,7 +564,7 @@
     return call(
         radial_body,
         [shape_of(3, 27, LANES), shape_of(136, LANES), *STATE],
-        [VMEM, VMEM, None, None, None, VMEM, VMEM, VMEM, VMEM, None, VMEM, VMEM, VMEM, VMEM, VMEM],
+        [VMEM] * 15,
         [
             pltpu.VMEM((3, 64, LANES), F32),
             pltpu.VMEM((blocks * TILES, LANES), F32),
@@ -579,13 +577,7 @@
             pltpu.VMEM((32, 3 * LANES), F32),
             pltpu.VMEM((3, 27, LANES), F32),
             pltpu.SemaphoreType.DMA,
-            pltpu.VMEM(node_ref.shape, F32),
-            pltpu.VMEM(derivs.shape, BF16),
-            pltpu.VMEM(blending.shape, BF16),
-            pltpu.VMEM(select.shape, BF16),
-            pltpu.SemaphoreType.DMA((4,)),
         ],
-        in_specs=[pl.BlockSpec(memory_space=pl.ANY if k in (2, 3, 4, 9) else VMEM) for k in range(15)],
         held=[False] + [True] * 7,
         out_specs=[pl.BlockSpec(memory_space=pl.ANY)] + [pl.BlockSpec(memory_space=VMEM)] * 7,
         name="radial",
@@ -609,18 +601,21 @@
         payload_body, shape_of(n_elem, 2, LANES), [None] * 3, [pltpu.VMEM((8, LANES), F32)], name="payload"
     )(cp_count.reshape(1, 1), cp_pos, cp_coef)
     mine = spread(copies, "elem")
-    *first, held_count, sent, link, minus, both, coupling, const, base = call(
+    *first, held_count, sent, link, held_node, held_derivs, held_blending, held_select, minus, both, coupling, const, base = call(
         setup_body,
         [
             *STATE, shape_of(1, LANES, dtype=I32), shape_of(2, LANES, dtype=I32), shape_of(6, LANES, dtype=I32),
+            shape_of(*node_ref.shape), shape_of(*derivs.shape, dtype=BF16), shape_of(*blending.shape, dtype=BF16),
+            shape_of(*select.shape, dtype=BF16),
             shape_of(2, 136, 136, dtype=BF16), shape_of(2, 136, 136, dtype=BF16), shape_of(2, 136, 288, dtype=BF16),
             shape_of(136, LANES), shape_of(136, LANES),
         ],
-        [None, None, HBM, None, HBM, HBM, HBM, HBM, HBM, HBM],
+        [None, None, HBM, None] + [HBM] * 9,
         [pltpu.VMEM((136, LANES), F32), pltpu.VMEM((136, 256), F32)],
         name="setup",
     )(
-        u_prev, elem_count.reshape(1, 1), select, send_list, vol_block, block_inv, lift_matrix, place, right_side, face_link
+        u_prev, elem_count.reshape(1, 1), select, send_list, vol_block, block_inv, lift_matrix, place, right_side, face_link,
+        node_ref, derivs, blending,
     )
     state, traces, *packets = first
     near = min(RUN, room)
@@ -635,7 +630,7 @@
     received = exchange(packets, ("elem",))
     far = lax.cond(jnp.max(points[:, 7, 0]) > near, lambda x: spread(x, "sub"), lambda x: x, rest)
     displacement, metric, state, traces, *packets = radial_call(
-        points, far, node_ref, derivs, blending, base, state, minus, held_count, select, sent,
+        points, far, held_node, held_derivs, held_blending, base, state, minus, held_count, held_select, sent,
         coupling, link, received,
     )
     for sweep in range(1, ITERS):
@@ -645,7 +640,7 @@
         )
         if sweep < ITERS - 1:
             state, traces, *packets = call(sweep_body, STATE, [VMEM] * 10, name="sweep")(
-                base, held_count, select, sent, coupling, link, *received
+                base, held_count, held_select, sent, coupling, link, *received
             )
         else:
             solution_out = call(

time: 91.8 us -> 91.3 us (level)
  Pallas kernels: 18.4 us -> 17.4 us
  starting transfers between devices: 49.4 us -> 50.4 us
    pallas_call x8, Pallas kernels: 18.4 us -> 17.4 us  [placed(): run(*[a if s is None else pltpu.with_memory_space_constraint(a, s) for a,...]
    ppermute x10, starting transfers between devices: 25.9 us -> 26.9 us  [exchange(): out.append(lax.ppermute(packets[first + turn], axis, pairs))]
where the time goes in v5:
time: 91.3 us; the launch traced here: 90.5 us
  starting transfers between devices  50.4 us (55%)
  waiting for transfers between devices  19.4 us (21%)
  Pallas kernels  17.4 us (19%)
  between operations  2.76 us (3%)
    ppermute x10, starting transfers between devices, exchange(): out.append(lax.ppermute(packets[first + turn], axis, pairs))  26.9 us
    all_to_all x2, starting transfers between devices, spread(): return lax.all_to_all(copies, axis, split_axis=0, concat_axis=0, tiled=True)  23.5 us
    pallas_call x8, Pallas kernels, placed(): run(*[a if s is None else pltpu.with_memory_space_constraint(a, s) for a,...  17.4 us
    all_to_all x2, waiting for transfers between devices, spread(): return lax.all_to_all(copies, axis, split_axis=0, concat_axis=0, tiled=True)  9.86 us
    ppermute x10, waiting for transfers between devices, exchange(): out.append(lax.ppermute(packets[first + turn], axis, pairs))  9.52 us
  transfers between devices with their start and end apart: 12, of which 4 were waited for; matrix products, arithmetic and copies ran while one was open for 1% of the time, Pallas kernels for 5%

profile of v5, /device:TPU:14, one launch (start us, length us, event | category | flops | bytes accessed | tf_op | source)
XLA Modules:
  0.0 90.5 jit_solution(200988828261739424)
XLA Ops:
  1.3 1.5 %payload.1 = f32[64,2,128]{2,1,0:T(2,128)} custom-call(s32[1,1]{1,0:T(1,128)} %bitcast.2.count_ref, f32[3,32]{1,0:T(4,128)} %pos_ref.1, f32[3,32]{1,0:T(4,128)} %coef_ref.1), custom_call_target="tpu_custom_call" | custom-call | tf_op jit(solution)/shard_map/payload/pallas_call | solution.py:127
  2.8 18.7 %all-to-all-start.1 = ((f32[64,2,128]{2,1,0:T(2,128)}), f32[64,2,128]{2,1,0:T(2,128)S(1)}, u32[]{:S(2)}, u32[]{:S(2)}) async-start(f32[64,2,128]{2,1,0:T(2,128)} %payload.1), calls=%async_computation.1 | async-start | bytes 131072 | tf_op jit(solution)/shard_map/all_to_all | solution.py:558
  22.2 3.3 %setup.1 = (f32[136,128]{1,0:T(8,128)S(1)}, f32[6,48,128]{2,1,0:T(8,128)}, f32[24,128]{1,0:T(8,128)S(1)}, f32[24,128]{1,0:T(8,128)S(1)}, f32[24,128]{1,0:T(8,128...) custom-call(f32[5,27,128]{2,1,0:T(8,128)} %u_ref.1, ...), custom_call_target="tpu_custom_call" | custom-call | tf_op jit(solution)/shard_map/setup/pallas_call | solution.py:127
  25.4 9.9 %all-to-all-done.1.in_ref = f32[64,2,128]{2,1,0:T(2,128)S(1)} async-done(((f32[64,2,128]{2,1,0:T(2,128)}), f32[64,2,128]{2,1,0:T(2,128)S(1)}, u32[]{:S(2)}, u32[]{:S(2)}) %all-to-all-start.1) | async-done | bytes 65568 | tf_op jit(solution)/shard_map/all_to_all | solution.py:558
  35.3 2.3 %compact.1 = (f32[8,8,1152]{2,1,0:T(8,128)}, f32[8,8,1280]{2,1,0:T(8,128)S(1)}) custom-call(f32[64,2,128]{2,1,0:T(2,128)S(1)} %all-to-all-done.1.in_ref, f32[24,128]{1,0:T(8,128)S(1)} %get-tuple-element.40.p0, f32[24,128]{1,0:T(8,128)S(1)} %get-tuple-element.41.p1, f32[136,128]{1,0:T(8,128)S(1)} %get-tuple-element.42.order_ref.base_ref), custom_call_target="tpu_custom_call" | custom-call | tf_op jit(solution)/shard_map/compact/pallas_call | solution.py:127
  37.6 4.8 %all-to-all-start.2 = ((f32[8,8,1152]{2,1,0:T(8,128)}), f32[8,8,1152]{2,1,0:T(8,128)S(1)}, u32[]{:S(2)}, u32[]{:S(2)}) async-start(f32[8,8,1152]{2,1,0:T(8,128)} %get-tuple-element.43), calls=%async_computation.2 | async-start | bytes 589824 | tf_op jit(solution)/shard_map/all_to_all | solution.py:558
  42.3 2.6 %collective-permute-start = (f32[24,128]{1,0:T(8,128)S(1)}, f32[24,128]{1,0:T(8,128)S(1)}, u32[]{:S(2)}, u32[]{:S(2)}) collective-permute-start(f32[24,128]{1,0:T(8,128)S(1)} %get-tuple-element.55), channel_id=1, source_target_pairs={{0,8},{8,0},{16,24},{24,16},{32,40},{40,32},{48,56},{56,48},{64,72... | collective-permute-start | bytes 36872 | tf_op jit(solution)/shard_map/ppermute | solution.py:553
  45.0 3.5 %collective-permute-start.1 = (f32[24,128]{1,0:T(8,128)S(1)}, f32[24,128]{1,0:T(8,128)S(1)}, u32[]{:S(2)}, u32[]{:S(2)}) collective-permute-start(f32[24,128]{1,0:T(8,128)S(1)} %get-tuple-element.56), channel_id=1, source_target_pairs={{8,16},{16,8},{24,32},{32,24},{40,48},{48,40},{56,64},{64,56},{72,... | collective-permute-start | bytes 36872 | tf_op jit(solution)/shard_map/ppermute | solution.py:553
  49.8 2.9 %collective-permute-done.1.elem_1 = f32[24,128]{1,0:T(8,128)S(1)} collective-permute-done((f32[24,128]{1,0:T(8,128)S(1)}, f32[24,128]{1,0:T(8,128)S(1)}, u32[]{:S(2)}, u32[]{:S(2)}) %collective-permute-start.1) | collective-permute-done | bytes 12320 | tf_op jit(solution)/shard_map/ppermute | solution.py:553
  52.7 6.6 %radial.1 = (f32[3,27,128]{2,1,0:T(8,128)}, f32[136,128]{1,0:T(8,128)S(1)}, f32[136,128]{1,0:T(8,128)S(1)}, f32[6,48,128]{2,1,0:T(8,128)S(1)}, f32[24,128]{1,0:T...) custom-call(f32[8,8,1152]{2,1,0:T(8,128)S(1)} %all-to-all-done.2.z_ref, ...), custom_call_target="tpu_custom_call" | custom-call | tf_op jit(solution)/shard_map/radial/pallas_call | solution.py:127
  59.3 2.1 %collective-permute-start.2 = (f32[24,128]{1,0:T(8,128)S(1)}, f32[24,128]{1,0:T(8,128)S(1)}, u32[]{:S(2)}, u32[]{:S(2)}) collective-permute-start(f32[24,128]{1,0:T(8,128)S(1)} %get-tuple-element.63), channel_id=1, source_target_pairs={{0,1},{1,0},{2,3},{3,2},{4,5},{5,4},{6,7},{7,6},{8,9},{9,8},{10,11... | collective-permute-start | bytes 36872 | tf_op jit(solution)/shard_map/ppermute | solution.py:553
  61.4 2.9 %collective-permute-start.3 = (f32[24,128]{1,0:T(8,128)S(1)}, f32[24,128]{1,0:T(8,128)S(1)}, u32[]{:S(2)}, u32[]{:S(2)}) collective-permute-start(f32[24,128]{1,0:T(8,128)S(1)} %get-tuple-element.64), channel_id=1, source_target_pairs={{1,2},{2,1},{3,4},{4,3},{5,6},{6,5},{9,10},{10,9},{11,12},{12,11},... | collective-permute-start | bytes 36872 | tf_op jit(solution)/shard_map/ppermute | solution.py:553
  64.3 1.9 %collective-permute-start.4 = (f32[24,128]{1,0:T(8,128)S(1)}, f32[24,128]{1,0:T(8,128)S(1)}, u32[]{:S(2)}, u32[]{:S(2)}) collective-permute-start(f32[24,128]{1,0:T(8,128)S(1)} %get-tuple-element.65), channel_id=1, source_target_pairs={{0,8},{8,0},{16,24},{24,16},{32,40},{40,32},{48,56},{56,48},{64,72... | collective-permute-start | bytes 36872 | tf_op jit(solution)/shard_map/ppermute | solution.py:553
  66.2 4.0 %collective-permute-start.5 = (f32[24,128]{1,0:T(8,128)S(1)}, f32[24,128]{1,0:T(8,128)S(1)}, u32[]{:S(2)}, u32[]{:S(2)}) collective-permute-start(f32[24,128]{1,0:T(8,128)S(1)} %get-tuple-element.66), channel_id=1, source_target_pairs={{8,16},{16,8},{24,32},{32,24},{40,48},{48,40},{56,64},{64,56},{72,... | collective-permute-start | bytes 36872 | tf_op jit(solution)/shard_map/ppermute | solution.py:553
  70.2 0.6 local.2.base_ref
  70.9 3.0 %collective-permute-done.5.elem_1 = f32[24,128]{1,0:T(8,128)S(1)} collective-permute-done((f32[24,128]{1,0:T(8,128)S(1)}, f32[24,128]{1,0:T(8,128)S(1)}, u32[]{:S(2)}, u32[]{:S(2)}) %collective-permute-start.5) | collective-permute-done | bytes 12320 | tf_op jit(solution)/shard_map/ppermute | solution.py:553
  73.9 1.1 %sweep.1 = (f32[136,128]{1,0:T(8,128)S(1)}, f32[6,48,128]{2,1,0:T(8,128)S(1)}, f32[24,128]{1,0:T(8,128)S(1)}, f32[24,128]{1,0:T(8,128)S(1)}, f32[24,128]{1,0:T(8,128)S(1)}, /*index=5*/f32[24,128]{1,0:T(8,128)S(1)}) custom-call(f32[136,128]{1,0:T(8,128)S(1)} %local.2.base_ref, s32[1,128]{1,0:T(1,128)S(1)} %get-tuple-element.50.count_ref, ...), custom_call_target="tpu_custom_call" | custom-call | tf_op jit(solution)/shard_map/sweep/pallas_call | solution.py:127
  75.0 1.9 %collective-permute-start.6 = (f32[24,128]{1,0:T(8,128)S(1)}, f32[24,128]{1,0:T(8,128)S(1)}, u32[]{:S(2)}, u32[]{:S(2)}) collective-permute-start(f32[24,128]{1,0:T(8,128)S(1)} %get-tuple-element.69), channel_id=1, source_target_pairs={{0,1},{1,0},{2,3},{3,2},{4,5},{5,4},{6,7},{7,6},{8,9},{9,8},{10,11... | collective-permute-start | bytes 36872 | tf_op jit(solution)/shard_map/ppermute | solution.py:553
  77.0 2.6 %collective-permute-start.7 = (f32[24,128]{1,0:T(8,128)S(1)}, f32[24,128]{1,0:T(8,128)S(1)}, u32[]{:S(2)}, u32[]{:S(2)}) collective-permute-start(f32[24,128]{1,0:T(8,128)S(1)} %get-tuple-element.70), channel_id=1, source_target_pairs={{1,2},{2,1},{3,4},{4,3},{5,6},{6,5},{9,10},{10,9},{11,12},{12,11},... | collective-permute-start | bytes 36872 | tf_op jit(solution)/shard_map/ppermute | solution.py:553
  79.6 1.9 %collective-permute-start.8 = (f32[24,128]{1,0:T(8,128)S(1)}, f32[24,128]{1,0:T(8,128)S(1)}, u32[]{:S(2)}, u32[]{:S(2)}) collective-permute-start(f32[24,128]{1,0:T(8,128)S(1)} %get-tuple-element.71), channel_id=1, source_target_pairs={{0,8},{8,0},{16,24},{24,16},{32,40},{40,32},{48,56},{56,48},{64,72... | collective-permute-start | bytes 36872 | tf_op jit(solution)/shard_map/ppermute | solution.py:553
  81.5 3.5 %collective-permute-start.9 = (f32[24,128]{1,0:T(8,128)S(1)}, f32[24,128]{1,0:T(8,128)S(1)}, u32[]{:S(2)}, u32[]{:S(2)}) collective-permute-start(f32[24,128]{1,0:T(8,128)S(1)} %get-tuple-element.72), channel_id=1, source_target_pairs={{8,16},{16,8},{24,32},{32,24},{40,48},{48,40},{56,64},{64,56},{72,... | collective-permute-start | bytes 36872 | tf_op jit(solution)/shard_map/ppermute | solution.py:553
  85.0 0.6 local.3.base_ref
  85.6 3.5 %collective-permute-done.9.elem_1 = f32[24,128]{1,0:T(8,128)S(1)} collective-permute-done((f32[24,128]{1,0:T(8,128)S(1)}, f32[24,128]{1,0:T(8,128)S(1)}, u32[]{:S(2)}, u32[]{:S(2)}) %collective-permute-start.9) | collective-permute-done | bytes 12320 | tf_op jit(solution)/shard_map/ppermute | solution.py:553
  89.2 1.3 %last.1 = f32[5,27,128]{2,1,0:T(8,128)} custom-call(f32[136,128]{1,0:T(8,128)S(1)} %local.3.base_ref, s32[1,128]{1,0:T(1,128)S(1)} %get-tuple-element.50.count_ref, bf16[2,136,288]{2,1,0:T(8,128)(2,1)S(1)} %get-tuple-element.53.m_ref, s32[6,128]{1,0:T(8,128)S(1)} %get-tuple-element.54.where_ref, f32[24,128]{1,0:T(8,128)S(1)} %collective-permute-done.6.sub_0, ...), custom_call_target="tpu_custom_call" | custom-call | tf_op jit(solution)/shard_map/last/pallas_call | solution.py:127
  (10 shorter events, 0.6 us)
Async XLA Ops:
  2.8 32.5 %all-to-all-start.1 = ((f32[64,2,128]{2,1,0:T(2,128)}), f32[64,2,128]{2,1,0:T(2,128)S(1)}, u32[]{:S(2)}, u32[]{:S(2)}) async-start(f32[64,2,128]{2,1,0:T(2,128)} %payload.1), calls=%async_computation.1 | async-start | bytes 131072 | tf_op jit(solution)/shard_map/all_to_all | solution.py:558
  37.6 10.9 %all-to-all-start.2 = ((f32[8,8,1152]{2,1,0:T(8,128)}), f32[8,8,1152]{2,1,0:T(8,128)S(1)}, u32[]{:S(2)}, u32[]{:S(2)}) async-start(f32[8,8,1152]{2,1,0:T(8,128)} %get-tuple-element.43), calls=%async_computation.2 | async-start | bytes 589824 | tf_op jit(solution)/shard_map/all_to_all | solution.py:558
  42.3 7.4 %collective-permute-start = (f32[24,128]{1,0:T(8,128)S(1)}, f32[24,128]{1,0:T(8,128)S(1)}, u32[]{:S(2)}, u32[]{:S(2)}) collective-permute-start(f32[24,128]{1,0:T(8,128)S(1)} %get-tuple-element.55), channel_id=1, source_target_pairs={{0,8},{8,0},{16,24},{24,16},{32,40},{40,32},{48,56},{56,48},{64,72... | collective-permute-start | bytes 36872 | tf_op jit(solution)/shard_map/ppermute | solution.py:553
  45.0 7.7 %collective-permute-start.1 = (f32[24,128]{1,0:T(8,128)S(1)}, f32[24,128]{1,0:T(8,128)S(1)}, u32[]{:S(2)}, u32[]{:S(2)}) collective-permute-start(f32[24,128]{1,0:T(8,128)S(1)} %get-tuple-element.56), channel_id=1, source_target_pairs={{8,16},{16,8},{24,32},{32,24},{40,48},{48,40},{56,64},{64,56},{72,... | collective-permute-start | bytes 36872 | tf_op jit(solution)/shard_map/ppermute | solution.py:553
  59.3 11.5 %collective-permute-start.2 = (f32[24,128]{1,0:T(8,128)S(1)}, f32[24,128]{1,0:T(8,128)S(1)}, u32[]{:S(2)}, u32[]{:S(2)}) collective-permute-start(f32[24,128]{1,0:T(8,128)S(1)} %get-tuple-element.63), channel_id=1, source_target_pairs={{0,1},{1,0},{2,3},{3,2},{4,5},{5,4},{6,7},{7,6},{8,9},{9,8},{10,11... | collective-permute-start | bytes 36872 | tf_op jit(solution)/shard_map/ppermute | solution.py:553
  61.4 9.4 %collective-permute-start.3 = (f32[24,128]{1,0:T(8,128)S(1)}, f32[24,128]{1,0:T(8,128)S(1)}, u32[]{:S(2)}, u32[]{:S(2)}) collective-permute-start(f32[24,128]{1,0:T(8,128)S(1)} %get-tuple-element.64), channel_id=1, source_target_pairs={{1,2},{2,1},{3,4},{4,3},{5,6},{6,5},{9,10},{10,9},{11,12},{12,11},... | collective-permute-start | bytes 36872 | tf_op jit(solution)/shard_map/ppermute | solution.py:553
  64.3 6.6 %collective-permute-start.4 = (f32[24,128]{1,0:T(8,128)S(1)}, f32[24,128]{1,0:T(8,128)S(1)}, u32[]{:S(2)}, u32[]{:S(2)}) collective-permute-start(f32[24,128]{1,0:T(8,128)S(1)} %get-tuple-element.65), channel_id=1, source_target_pairs={{0,8},{8,0},{16,24},{24,16},{32,40},{40,32},{48,56},{56,48},{64,72... | collective-permute-start | bytes 36872 | tf_op jit(solution)/shard_map/ppermute | solution.py:553
  66.2 7.7 %collective-permute-start.5 = (f32[24,128]{1,0:T(8,128)S(1)}, f32[24,128]{1,0:T(8,128)S(1)}, u32[]{:S(2)}, u32[]{:S(2)}) collective-permute-start(f32[24,128]{1,0:T(8,128)S(1)} %get-tuple-element.66), channel_id=1, source_target_pairs={{8,16},{16,8},{24,32},{32,24},{40,48},{48,40},{56,64},{64,56},{72,... | collective-permute-start | bytes 36872 | tf_op jit(solution)/shard_map/ppermute | solution.py:553
  75.0 10.6 %collective-permute-start.6 = (f32[24,128]{1,0:T(8,128)S(1)}, f32[24,128]{1,0:T(8,128)S(1)}, u32[]{:S(2)}, u32[]{:S(2)}) collective-permute-start(f32[24,128]{1,0:T(8,128)S(1)} %get-tuple-element.69), channel_id=1, source_target_pairs={{0,1},{1,0},{2,3},{3,2},{4,5},{5,4},{6,7},{7,6},{8,9},{9,8},{10,11... | collective-permute-start | bytes 36872 | tf_op jit(solution)/shard_map/ppermute | solution.py:553
  77.0 8.6 %collective-permute-start.7 = (f32[24,128]{1,0:T(8,128)S(1)}, f32[24,128]{1,0:T(8,128)S(1)}, u32[]{:S(2)}, u32[]{:S(2)}) collective-permute-start(f32[24,128]{1,0:T(8,128)S(1)} %get-tuple-element.70), channel_id=1, source_target_pairs={{1,2},{2,1},{3,4},{4,3},{5,6},{6,5},{9,10},{10,9},{11,12},{12,11},... | collective-permute-start | bytes 36872 | tf_op jit(solution)/shard_map/ppermute | solution.py:553
  79.6 6.1 %collective-permute-start.8 = (f32[24,128]{1,0:T(8,128)S(1)}, f32[24,128]{1,0:T(8,128)S(1)}, u32[]{:S(2)}, u32[]{:S(2)}) collective-permute-start(f32[24,128]{1,0:T(8,128)S(1)} %get-tuple-element.71), channel_id=1, source_target_pairs={{0,8},{8,0},{16,24},{24,16},{32,40},{40,32},{48,56},{56,48},{64,72... | collective-permute-start | bytes 36872 | tf_op jit(solution)/shard_map/ppermute | solution.py:553
  81.5 7.7 %collective-permute-start.9 = (f32[24,128]{1,0:T(8,128)S(1)}, f32[24,128]{1,0:T(8,128)S(1)}, u32[]{:S(2)}, u32[]{:S(2)}) collective-permute-start(f32[24,128]{1,0:T(8,128)S(1)} %get-tuple-element.72), channel_id=1, source_target_pairs={{8,16},{16,8},{24,32},{32,24},{40,48},{48,40},{56,64},{64,56},{72,... | collective-permute-start | bytes 36872 | tf_op jit(solution)/shard_map/ppermute | solution.py:553

commit v6 on v5

--- a/solution.py
+++ b/solution.py
@@ -326,22 +326,21 @@
             return length
 
         def four(step, carry):
-            for i in range(2):
-                for c in range(0, 64, 8):
-                    total = [sum_ref[axis, c : c + 8, :] for axis in range(3)]
-                    place = [corner_ref[axis, c : c + 8, :] for axis in range(3)]
-                    for e in range(2):
-                        entry = list_ref.at[4 * step + 2 * i + e]
-                        gap = [place[axis] - entry[axis : axis + 1, :] for axis in range(3)]
-                        square = gap[0] * gap[0] + gap[1] * gap[1] + gap[2] * gap[2]
-                        ratio = square * lax.rsqrt(jnp.maximum(square, 1e-20))
-                        inside = jnp.maximum(1.0 - ratio, 0.0)
-                        inside = inside * inside
-                        kernel = inside * inside * (ratio + 0.25)
-                        for axis in range(3):
-                            total[axis] = total[axis] + entry[4 + axis : 5 + axis, :] * kernel
+            for c in range(0, 64, 8):
+                total = [sum_ref[axis, c : c + 8, :] for axis in range(3)]
+                place = [corner_ref[axis, c : c + 8, :] for axis in range(3)]
+                for e in range(4):
+                    entry = list_ref.at[4 * step + e]
+                    gap = [place[axis] - entry[axis : axis + 1, :] for axis in range(3)]
+                    square = gap[0] * gap[0] + gap[1] * gap[1] + gap[2] * gap[2]
+                    ratio = square * lax.rsqrt(jnp.maximum(square, 1e-20))
+                    inside = jnp.maximum(1.0 - ratio, 0.0)
+                    inside = inside * inside
+                    kernel = inside * inside * (ratio + 0.25)
                     for axis in range(3):
-                        sum_ref[axis, c : c + 8, :] = total[axis]
+                        total[axis] = total[axis] + entry[4 + axis : 5 + axis, :] * kernel
+                for axis in range(3):
+                    sum_ref[axis, c : c + 8, :] = total[axis]
             return carry
 
         def evaluate(length):

time: 91.3 us -> 91.1 us (level)
  starting transfers between devices: 50.4 us -> 49.3 us
  waiting for transfers between devices: 19.4 us -> 20.4 us
    ppermute x10, waiting for transfers between devices: 9.52 us -> 10.6 us  [exchange(): out.append(lax.ppermute(packets[first + turn], axis, pairs))]
    ppermute x10, starting transfers between devices: 26.9 us -> 25.8 us  [exchange(): out.append(lax.ppermute(packets[first + turn], axis, pairs))]
where the time goes in v6:
time: 91.1 us; the launch traced here: 90.4 us
  starting transfers between devices  49.3 us (54%)
  waiting for transfers between devices  20.4 us (22%)
  Pallas kernels  17.3 us (19%)
  between operations  2.76 us (3%)
    ppermute x10, starting transfers between devices, exchange(): out.append(lax.ppermute(packets[first + turn], axis, pairs))  25.8 us
    all_to_all x2, starting transfers between devices, spread(): return lax.all_to_all(copies, axis, split_axis=0, concat_axis=0, tiled=True)  23.5 us
    pallas_call x8, Pallas kernels, placed(): run(*[a if s is None else pltpu.with_memory_space_constraint(a, s) for a,...  17.3 us
    ppermute x10, waiting for transfers between devices, exchange(): out.append(lax.ppermute(packets[first + turn], axis, pairs))  10.6 us
    all_to_all x2, waiting for transfers between devices, spread(): return lax.all_to_all(copies, axis, split_axis=0, concat_axis=0, tiled=True)  9.86 us
  transfers between devices with their start and end apart: 12, of which 4 were waited for; matrix products, arithmetic and copies ran while one was open for 1% of the time, Pallas kernels for 5%

profile of v6, /device:TPU:14, one launch (start us, length us, event | category | flops | bytes accessed | tf_op | source)
XLA Modules:
  0.0 90.4 jit_solution(488835887054226173)
XLA Ops:
  1.3 1.5 %payload.1 = f32[64,2,128]{2,1,0:T(2,128)} custom-call(s32[1,1]{1,0:T(1,128)} %bitcast.2.count_ref, f32[3,32]{1,0:T(4,128)} %pos_ref.1, f32[3,32]{1,0:T(4,128)} %coef_ref.1), custom_call_target="tpu_custom_call" | custom-call | tf_op jit(solution)/shard_map/payload/pallas_call | solution.py:127
  2.8 18.7 %all-to-all-start.1 = ((f32[64,2,128]{2,1,0:T(2,128)}), f32[64,2,128]{2,1,0:T(2,128)S(1)}, u32[]{:S(2)}, u32[]{:S(2)}) async-start(f32[64,2,128]{2,1,0:T(2,128)} %payload.1), calls=%async_computation.1 | async-start | bytes 131072 | tf_op jit(solution)/shard_map/all_to_all | solution.py:557
  22.2 3.3 %setup.1 = (f32[136,128]{1,0:T(8,128)S(1)}, f32[6,48,128]{2,1,0:T(8,128)}, f32[24,128]{1,0:T(8,128)S(1)}, f32[24,128]{1,0:T(8,128)S(1)}, f32[24,128]{1,0:T(8,128...) custom-call(f32[5,27,128]{2,1,0:T(8,128)} %u_ref.1, ...), custom_call_target="tpu_custom_call" | custom-call | tf_op jit(solution)/shard_map/setup/pallas_call | solution.py:127
  25.4 9.9 %all-to-all-done.1.in_ref = f32[64,2,128]{2,1,0:T(2,128)S(1)} async-done(((f32[64,2,128]{2,1,0:T(2,128)}), f32[64,2,128]{2,1,0:T(2,128)S(1)}, u32[]{:S(2)}, u32[]{:S(2)}) %all-to-all-start.1) | async-done | bytes 65568 | tf_op jit(solution)/shard_map/all_to_all | solution.py:557
  35.3 2.3 %compact.1 = (f32[8,8,1152]{2,1,0:T(8,128)}, f32[8,8,1280]{2,1,0:T(8,128)S(1)}) custom-call(f32[64,2,128]{2,1,0:T(2,128)S(1)} %all-to-all-done.1.in_ref, f32[24,128]{1,0:T(8,128)S(1)} %get-tuple-element.40.p0, f32[24,128]{1,0:T(8,128)S(1)} %get-tuple-element.41.p1, f32[136,128]{1,0:T(8,128)S(1)} %get-tuple-element.42.order_ref.base_ref), custom_call_target="tpu_custom_call" | custom-call | tf_op jit(solution)/shard_map/compact/pallas_call | solution.py:127
  37.6 4.8 %all-to-all-start.2 = ((f32[8,8,1152]{2,1,0:T(8,128)}), f32[8,8,1152]{2,1,0:T(8,128)S(1)}, u32[]{:S(2)}, u32[]{:S(2)}) async-start(f32[8,8,1152]{2,1,0:T(8,128)} %get-tuple-element.43), calls=%async_computation.2 | async-start | bytes 589824 | tf_op jit(solution)/shard_map/all_to_all | solution.py:557
  42.3 2.6 %collective-permute-start = (f32[24,128]{1,0:T(8,128)S(1)}, f32[24,128]{1,0:T(8,128)S(1)}, u32[]{:S(2)}, u32[]{:S(2)}) collective-permute-start(f32[24,128]{1,0:T(8,128)S(1)} %get-tuple-element.55), channel_id=1, source_target_pairs={{0,8},{8,0},{16,24},{24,16},{32,40},{40,32},{48,56},{56,48},{64,72... | collective-permute-start | bytes 36872 | tf_op jit(solution)/shard_map/ppermute | solution.py:552
  45.0 3.5 %collective-permute-start.1 = (f32[24,128]{1,0:T(8,128)S(1)}, f32[24,128]{1,0:T(8,128)S(1)}, u32[]{:S(2)}, u32[]{:S(2)}) collective-permute-start(f32[24,128]{1,0:T(8,128)S(1)} %get-tuple-element.56), channel_id=1, source_target_pairs={{8,16},{16,8},{24,32},{32,24},{40,48},{48,40},{56,64},{64,56},{72,... | collective-permute-start | bytes 36872 | tf_op jit(solution)/shard_map/ppermute | solution.py:552
  49.8 2.9 %collective-permute-done.1.elem_1 = f32[24,128]{1,0:T(8,128)S(1)} collective-permute-done((f32[24,128]{1,0:T(8,128)S(1)}, f32[24,128]{1,0:T(8,128)S(1)}, u32[]{:S(2)}, u32[]{:S(2)}) %collective-permute-start.1) | collective-permute-done | bytes 12320 | tf_op jit(solution)/shard_map/ppermute | solution.py:552
  52.7 6.6 %radial.1 = (f32[3,27,128]{2,1,0:T(8,128)}, f32[136,128]{1,0:T(8,128)S(1)}, f32[136,128]{1,0:T(8,128)S(1)}, f32[6,48,128]{2,1,0:T(8,128)S(1)}, f32[24,128]{1,0:T...) custom-call(f32[8,8,1152]{2,1,0:T(8,128)S(1)} %all-to-all-done.2.z_ref, ...), custom_call_target="tpu_custom_call" | custom-call | tf_op jit(solution)/shard_map/radial/pallas_call | solution.py:127
  59.3 2.1 %collective-permute-start.2 = (f32[24,128]{1,0:T(8,128)S(1)}, f32[24,128]{1,0:T(8,128)S(1)}, u32[]{:S(2)}, u32[]{:S(2)}) collective-permute-start(f32[24,128]{1,0:T(8,128)S(1)} %get-tuple-element.63), channel_id=1, source_target_pairs={{0,1},{1,0},{2,3},{3,2},{4,5},{5,4},{6,7},{7,6},{8,9},{9,8},{10,11... | collective-permute-start | bytes 36872 | tf_op jit(solution)/shard_map/ppermute | solution.py:552
  61.4 3.4 %collective-permute-start.3 = (f32[24,128]{1,0:T(8,128)S(1)}, f32[24,128]{1,0:T(8,128)S(1)}, u32[]{:S(2)}, u32[]{:S(2)}) collective-permute-start(f32[24,128]{1,0:T(8,128)S(1)} %get-tuple-element.64), channel_id=1, source_target_pairs={{1,2},{2,1},{3,4},{4,3},{5,6},{6,5},{9,10},{10,9},{11,12},{12,11},... | collective-permute-start | bytes 36872 | tf_op jit(solution)/shard_map/ppermute | solution.py:552
  64.8 1.9 %collective-permute-start.4 = (f32[24,128]{1,0:T(8,128)S(1)}, f32[24,128]{1,0:T(8,128)S(1)}, u32[]{:S(2)}, u32[]{:S(2)}) collective-permute-start(f32[24,128]{1,0:T(8,128)S(1)} %get-tuple-element.65), channel_id=1, source_target_pairs={{0,8},{8,0},{16,24},{24,16},{32,40},{40,32},{48,56},{56,48},{64,72... | collective-permute-start | bytes 36872 | tf_op jit(solution)/shard_map/ppermute | solution.py:552
  66.7 2.9 %collective-permute-start.5 = (f32[24,128]{1,0:T(8,128)S(1)}, f32[24,128]{1,0:T(8,128)S(1)}, u32[]{:S(2)}, u32[]{:S(2)}) collective-permute-start(f32[24,128]{1,0:T(8,128)S(1)} %get-tuple-element.66), channel_id=1, source_target_pairs={{8,16},{16,8},{24,32},{32,24},{40,48},{48,40},{56,64},{64,56},{72,... | collective-permute-start | bytes 36872 | tf_op jit(solution)/shard_map/ppermute | solution.py:552
  69.7 0.6 local.2.base_ref
  70.4 4.0 %collective-permute-done.5.elem_1 = f32[24,128]{1,0:T(8,128)S(1)} collective-permute-done((f32[24,128]{1,0:T(8,128)S(1)}, f32[24,128]{1,0:T(8,128)S(1)}, u32[]{:S(2)}, u32[]{:S(2)}) %collective-permute-start.5) | collective-permute-done | bytes 12320 | tf_op jit(solution)/shard_map/ppermute | solution.py:552
  74.4 1.1 %sweep.1 = (f32[136,128]{1,0:T(8,128)S(1)}, f32[6,48,128]{2,1,0:T(8,128)S(1)}, f32[24,128]{1,0:T(8,128)S(1)}, f32[24,128]{1,0:T(8,128)S(1)}, f32[24,128]{1,0:T(8,128)S(1)}, /*index=5*/f32[24,128]{1,0:T(8,128)S(1)}) custom-call(f32[136,128]{1,0:T(8,128)S(1)} %local.2.base_ref, s32[1,128]{1,0:T(1,128)S(1)} %get-tuple-element.50.count_ref, ...), custom_call_target="tpu_custom_call" | custom-call | tf_op jit(solution)/shard_map/sweep/pallas_call | solution.py:127
  75.5 1.9 %collective-permute-start.6 = (f32[24,128]{1,0:T(8,128)S(1)}, f32[24,128]{1,0:T(8,128)S(1)}, u32[]{:S(2)}, u32[]{:S(2)}) collective-permute-start(f32[24,128]{1,0:T(8,128)S(1)} %get-tuple-element.69), channel_id=1, source_target_pairs={{0,1},{1,0},{2,3},{3,2},{4,5},{5,4},{6,7},{7,6},{8,9},{9,8},{10,11... | collective-permute-start | bytes 36872 | tf_op jit(solution)/shard_map/ppermute | solution.py:552
  77.4 2.1 %collective-permute-start.7 = (f32[24,128]{1,0:T(8,128)S(1)}, f32[24,128]{1,0:T(8,128)S(1)}, u32[]{:S(2)}, u32[]{:S(2)}) collective-permute-start(f32[24,128]{1,0:T(8,128)S(1)} %get-tuple-element.70), channel_id=1, source_target_pairs={{1,2},{2,1},{3,4},{4,3},{5,6},{6,5},{9,10},{10,9},{11,12},{12,11},... | collective-permute-start | bytes 36872 | tf_op jit(solution)/shard_map/ppermute | solution.py:552
  79.5 1.9 %collective-permute-start.8 = (f32[24,128]{1,0:T(8,128)S(1)}, f32[24,128]{1,0:T(8,128)S(1)}, u32[]{:S(2)}, u32[]{:S(2)}) collective-permute-start(f32[24,128]{1,0:T(8,128)S(1)} %get-tuple-element.71), channel_id=1, source_target_pairs={{0,8},{8,0},{16,24},{24,16},{32,40},{40,32},{48,56},{56,48},{64,72... | collective-permute-start | bytes 36872 | tf_op jit(solution)/shard_map/ppermute | solution.py:552
  81.4 3.5 %collective-permute-start.9 = (f32[24,128]{1,0:T(8,128)S(1)}, f32[24,128]{1,0:T(8,128)S(1)}, u32[]{:S(2)}, u32[]{:S(2)}) collective-permute-start(f32[24,128]{1,0:T(8,128)S(1)} %get-tuple-element.72), channel_id=1, source_target_pairs={{8,16},{16,8},{24,32},{32,24},{40,48},{48,40},{56,64},{64,56},{72,... | collective-permute-start | bytes 36872 | tf_op jit(solution)/shard_map/ppermute | solution.py:552
  84.9 0.6 local.3.base_ref
  85.6 3.5 %collective-permute-done.9.elem_1 = f32[24,128]{1,0:T(8,128)S(1)} collective-permute-done((f32[24,128]{1,0:T(8,128)S(1)}, f32[24,128]{1,0:T(8,128)S(1)}, u32[]{:S(2)}, u32[]{:S(2)}) %collective-permute-start.9) | collective-permute-done | bytes 12320 | tf_op jit(solution)/shard_map/ppermute | solution.py:552
  89.1 1.3 %last.1 = f32[5,27,128]{2,1,0:T(8,128)} custom-call(f32[136,128]{1,0:T(8,128)S(1)} %local.3.base_ref, s32[1,128]{1,0:T(1,128)S(1)} %get-tuple-element.50.count_ref, bf16[2,136,288]{2,1,0:T(8,128)(2,1)S(1)} %get-tuple-element.53.m_ref, s32[6,128]{1,0:T(8,128)S(1)} %get-tuple-element.54.where_ref, f32[24,128]{1,0:T(8,128)S(1)} %collective-permute-done.6.sub_0, ...), custom_call_target="tpu_custom_call" | custom-call | tf_op jit(solution)/shard_map/last/pallas_call | solution.py:127
  (10 shorter events, 0.7 us)
Async XLA Ops:
  2.8 32.5 %all-to-all-start.1 = ((f32[64,2,128]{2,1,0:T(2,128)}), f32[64,2,128]{2,1,0:T(2,128)S(1)}, u32[]{:S(2)}, u32[]{:S(2)}) async-start(f32[64,2,128]{2,1,0:T(2,128)} %payload.1), calls=%async_computation.1 | async-start | bytes 131072 | tf_op jit(solution)/shard_map/all_to_all | solution.py:557
  37.6 10.9 %all-to-all-start.2 = ((f32[8,8,1152]{2,1,0:T(8,128)}), f32[8,8,1152]{2,1,0:T(8,128)S(1)}, u32[]{:S(2)}, u32[]{:S(2)}) async-start(f32[8,8,1152]{2,1,0:T(8,128)} %get-tuple-element.43), calls=%async_computation.2 | async-start | bytes 589824 | tf_op jit(solution)/shard_map/all_to_all | solution.py:557
  42.3 7.4 %collective-permute-start = (f32[24,128]{1,0:T(8,128)S(1)}, f32[24,128]{1,0:T(8,128)S(1)}, u32[]{:S(2)}, u32[]{:S(2)}) collective-permute-start(f32[24,128]{1,0:T(8,128)S(1)} %get-tuple-element.55), channel_id=1, source_target_pairs={{0,8},{8,0},{16,24},{24,16},{32,40},{40,32},{48,56},{56,48},{64,72... | collective-permute-start | bytes 36872 | tf_op jit(solution)/shard_map/ppermute | solution.py:552
  45.0 7.7 %collective-permute-start.1 = (f32[24,128]{1,0:T(8,128)S(1)}, f32[24,128]{1,0:T(8,128)S(1)}, u32[]{:S(2)}, u32[]{:S(2)}) collective-permute-start(f32[24,128]{1,0:T(8,128)S(1)} %get-tuple-element.56), channel_id=1, source_target_pairs={{8,16},{16,8},{24,32},{32,24},{40,48},{48,40},{56,64},{64,56},{72,... | collective-permute-start | bytes 36872 | tf_op jit(solution)/shard_map/ppermute | solution.py:552
  59.3 11.0 %collective-permute-start.2 = (f32[24,128]{1,0:T(8,128)S(1)}, f32[24,128]{1,0:T(8,128)S(1)}, u32[]{:S(2)}, u32[]{:S(2)}) collective-permute-start(f32[24,128]{1,0:T(8,128)S(1)} %get-tuple-element.63), channel_id=1, source_target_pairs={{0,1},{1,0},{2,3},{3,2},{4,5},{5,4},{6,7},{7,6},{8,9},{9,8},{10,11... | collective-permute-start | bytes 36872 | tf_op jit(solution)/shard_map/ppermute | solution.py:552
  61.4 8.9 %collective-permute-start.3 = (f32[24,128]{1,0:T(8,128)S(1)}, f32[24,128]{1,0:T(8,128)S(1)}, u32[]{:S(2)}, u32[]{:S(2)}) collective-permute-start(f32[24,128]{1,0:T(8,128)S(1)} %get-tuple-element.64), channel_id=1, source_target_pairs={{1,2},{2,1},{3,4},{4,3},{5,6},{6,5},{9,10},{10,9},{11,12},{12,11},... | collective-permute-start | bytes 36872 | tf_op jit(solution)/shard_map/ppermute | solution.py:552
  64.8 5.6 %collective-permute-start.4 = (f32[24,128]{1,0:T(8,128)S(1)}, f32[24,128]{1,0:T(8,128)S(1)}, u32[]{:S(2)}, u32[]{:S(2)}) collective-permute-start(f32[24,128]{1,0:T(8,128)S(1)} %get-tuple-element.65), channel_id=1, source_target_pairs={{0,8},{8,0},{16,24},{24,16},{32,40},{40,32},{48,56},{56,48},{64,72... | collective-permute-start | bytes 36872 | tf_op jit(solution)/shard_map/ppermute | solution.py:552
  66.7 7.7 %collective-permute-start.5 = (f32[24,128]{1,0:T(8,128)S(1)}, f32[24,128]{1,0:T(8,128)S(1)}, u32[]{:S(2)}, u32[]{:S(2)}) collective-permute-start(f32[24,128]{1,0:T(8,128)S(1)} %get-tuple-element.66), channel_id=1, source_target_pairs={{8,16},{16,8},{24,32},{32,24},{40,48},{48,40},{56,64},{64,56},{72,... | collective-permute-start | bytes 36872 | tf_op jit(solution)/shard_map/ppermute | solution.py:552
  75.5 10.0 %collective-permute-start.6 = (f32[24,128]{1,0:T(8,128)S(1)}, f32[24,128]{1,0:T(8,128)S(1)}, u32[]{:S(2)}, u32[]{:S(2)}) collective-permute-start(f32[24,128]{1,0:T(8,128)S(1)} %get-tuple-element.69), channel_id=1, source_target_pairs={{0,1},{1,0},{2,3},{3,2},{4,5},{5,4},{6,7},{7,6},{8,9},{9,8},{10,11... | collective-permute-start | bytes 36872 | tf_op jit(solution)/shard_map/ppermute | solution.py:552
  77.4 8.1 %collective-permute-start.7 = (f32[24,128]{1,0:T(8,128)S(1)}, f32[24,128]{1,0:T(8,128)S(1)}, u32[]{:S(2)}, u32[]{:S(2)}) collective-permute-start(f32[24,128]{1,0:T(8,128)S(1)} %get-tuple-element.70), channel_id=1, source_target_pairs={{1,2},{2,1},{3,4},{4,3},{5,6},{6,5},{9,10},{10,9},{11,12},{12,11},... | collective-permute-start | bytes 36872 | tf_op jit(solution)/shard_map/ppermute | solution.py:552
  79.5 6.1 %collective-permute-start.8 = (f32[24,128]{1,0:T(8,128)S(1)}, f32[24,128]{1,0:T(8,128)S(1)}, u32[]{:S(2)}, u32[]{:S(2)}) collective-permute-start(f32[24,128]{1,0:T(8,128)S(1)} %get-tuple-element.71), channel_id=1, source_target_pairs={{0,8},{8,0},{16,24},{24,16},{32,40},{40,32},{48,56},{56,48},{64,72... | collective-permute-start | bytes 36872 | tf_op jit(solution)/shard_map/ppermute | solution.py:552
  81.4 7.7 %collective-permute-start.9 = (f32[24,128]{1,0:T(8,128)S(1)}, f32[24,128]{1,0:T(8,128)S(1)}, u32[]{:S(2)}, u32[]{:S(2)}) collective-permute-start(f32[24,128]{1,0:T(8,128)S(1)} %get-tuple-element.72), channel_id=1, source_target_pairs={{8,16},{16,8},{24,32},{32,24},{40,48},{48,40},{56,64},{64,56},{72,... | collective-permute-start | bytes 36872 | tf_op jit(solution)/shard_map/ppermute | solution.py:552
